TPU v7x, 128 devices: a whole 4x4x4 slice. The times are simulated.
128 devices in a mesh: blk: 8 (over x_lo, y), head: 8 (over z, core), grp: 2 (over x_hi).
Axes of the slice: x: 4 (x_hi: 2, x_lo: 2; x = x_hi * 2 + x_lo), y: 4, z: 4, core: 2. Of those that a mesh axis runs over, the one named last changes fastest.
Arguments:
- t_query: bfloat16 [8192, 4096], P('blk', ('head', 'grp')), may hold values from -80 to 80
- t_key: bfloat16 [8192, 4096], P('blk', ('head', 'grp')), may hold values from -80 to 80
- t_value: bfloat16 [8192, 4096], P('blk', ('head', 'grp')), may hold values from -6 to 6
- t_out: bfloat16 [4096, 4096], P(('head', 'grp')), may hold values from -0.09375 to 0.09375
- s_query: bfloat16 [8192, 2048], P('blk', ('head', 'grp')), may hold values from -80 to 80
- s_key: bfloat16 [8192, 2048], P('blk', ('head', 'grp')), may hold values from -80 to 80
- s_value: bfloat16 [8192, 2048], P('blk', ('head', 'grp')), may hold values from -6 to 6
- s_out: bfloat16 [2048, 4096], P(('head', 'grp')), may hold values from -0.125 to 0.125
- segments: int32 [8192], P('blk'), may hold values from 0 to 1, never falling along the last dimension, each value on 1 to 8128 neighbouring positions
- selection: int32 [128, 16], P('blk'), may hold values from 0 to 127, as said below
Outputs:
- mismatch: float32 [8192, 4096], P('blk', ('head', 'grp'))
- s_dq: float32 [8192, 2048], P('blk', ('head', 'grp'))
- s_dk: float32 [8192, 2048], P('blk', ('head', 'grp'))
- s_dv: float32 [8192, 2048], P('blk', ('head', 'grp'))
Inputs may be any that keep to these rules, and one draw needn't show every extreme that they name: `selection`: entry 0 of row b is b itself; for b >= 64, entry 1 of row b is b - 64; every entry of row b lies between 0 and b; entries of a row may repeat. `segments`: document numbers never fall along the sequence.
All inputs are finite; a program needn't handle non-finite values.
Results may differ from a plain program's by a relative error of at most 0.015.
Values may be sent and summed in bfloat16 or wider, within the bound.
No kernel may reach another device: no remote copies, remote signals or barrier semaphores. Data moves between devices by JAX's collectives and lax.ppermute only.
A program may use at most 128 MiB of HBM per device.

v0:
```python
import math

import jax
import jax.numpy as jnp
from jax import lax
from jax.sharding import PartitionSpec as P

HD = 128
BS = 64
NSEL = 16


masked_score = -1e30


def student_forward(queries, key_all, value_all, segment_all, selection, first_row):
    row_count = queries.shape[0]
    head_count = queries.shape[1] // HD
    blocks = row_count // BS
    query_blocks = queries.reshape(blocks, BS, head_count, HD)
    key_blocks = key_all.reshape(-1, BS, head_count, HD)[selection].reshape(
        blocks, NSEL * BS, head_count, HD
    )
    value_blocks = value_all.reshape(-1, BS, head_count, HD)[selection].reshape(
        blocks, NSEL * BS, head_count, HD
    )
    key_pos = (selection[:, :, None] * BS + jnp.arange(BS)[None, None, :]).reshape(
        blocks, NSEL * BS
    )
    query_pos = (first_row + jnp.arange(row_count)).reshape(blocks, BS)
    key_seg = segment_all[key_pos]
    query_seg = segment_all[query_pos]
    scores = jnp.einsum(
        "bqhd,bkhd->bhqk", query_blocks, key_blocks, preferred_element_type=jnp.float32
    ) * HD ** (-0.5)
    allowed = (
        (key_pos[:, None, :] <= query_pos[:, :, None])
        & (key_seg[:, None, :] == query_seg[:, :, None])
    )[:, None]
    scores = jnp.where(allowed, scores, masked_score)
    largest = jnp.max(scores, axis=3, keepdims=True)
    weights = jnp.where(allowed, jnp.exp(scores - largest), 0.0)
    weights = weights / jnp.sum(weights, axis=3, keepdims=True)
    value_wide = value_blocks.astype(jnp.float32)
    blended = jnp.einsum("bhqk,bkhd->bqhd", weights, value_wide, precision=lax.Precision.HIGHEST)
    saved = (query_blocks, key_blocks, value_wide, weights, blended)
    return (blended.reshape(row_count, head_count * HD), saved)


def student_backward(grad_attn, saved, selection, token_count):
    query_blocks, key_blocks, value_wide, weights, blended = saved
    blocks, _, head_count, _ = query_blocks.shape
    row_count = blocks * BS
    grad_blocks = grad_attn.reshape(blocks, BS, head_count, HD)
    value_grad = jnp.einsum(
        "bhqk,bqhd->bkhd", weights, grad_blocks, precision=lax.Precision.HIGHEST
    )
    weight_grad = jnp.einsum(
        "bqhd,bkhd->bhqk", grad_blocks, value_wide, precision=lax.Precision.HIGHEST
    )
    row_dots = jnp.sum(grad_blocks * blended, axis=3).transpose(0, 2, 1)[..., None]
    score_grad = weights * (weight_grad - row_dots) * HD ** (-0.5)
    query_grad = jnp.einsum(
        "bhqk,bkhd->bqhd",
        score_grad,
        key_blocks.astype(jnp.float32),
        precision=lax.Precision.HIGHEST,
    )
    key_grad = jnp.einsum(
        "bhqk,bqhd->bkhd",
        score_grad,
        query_blocks.astype(jnp.float32),
        precision=lax.Precision.HIGHEST,
    )
    flat_sel = selection.reshape(-1)
    width = head_count * HD
    key_total = (
        jnp.zeros((token_count // BS, BS, width), jnp.float32)
        .at[flat_sel]
        .add(key_grad.reshape(blocks * NSEL, BS, width))
    )
    value_total = (
        jnp.zeros((token_count // BS, BS, width), jnp.float32)
        .at[flat_sel]
        .add(value_grad.reshape(blocks * NSEL, BS, width))
    )
    return (
        query_grad.reshape(row_count, width),
        key_total.reshape(token_count, width),
        value_total.reshape(token_count, width),
    )


def teacher_update(
    carried, key_rows, value_rows, seg_rows, first_key, queries, query_seg, query_pos
):
    running_max, running_sum, weighted = carried
    head_count = queries.shape[1]
    key_heads = key_rows.reshape(key_rows.shape[0], head_count, HD)
    value_heads = value_rows.reshape(value_rows.shape[0], head_count, HD)
    scores = jnp.einsum(
        "qhd,khd->hqk", queries, key_heads, preferred_element_type=jnp.float32
    ) * HD ** (-0.5)
    key_pos = first_key + jnp.arange(key_rows.shape[0])
    allowed = (
        (key_pos[None, :] <= query_pos[:, None]) & (seg_rows[None, :] == query_seg[:, None])
    )[None]
    scores = jnp.where(allowed, scores, masked_score)
    new_max = jnp.maximum(running_max, jnp.max(scores, axis=2))
    factor = jnp.exp(running_max - new_max)
    weights = jnp.where(allowed, jnp.exp(scores - new_max[..., None]), 0.0)
    running_sum = factor * running_sum + jnp.sum(weights, axis=2)
    product = jnp.einsum(
        "hqk,khd->hqd",
        weights.astype(jnp.bfloat16),
        value_heads,
        preferred_element_type=jnp.float32,
    )
    weighted = factor[..., None] * weighted + product
    return (new_max, running_sum, weighted)


def teacher_fold(carried, key_rows, value_rows, seg_rows, queries, query_seg, query_pos):
    piece_rows = key_rows.shape[0]
    block_rows = math.gcd(piece_rows, 512)
    turn_count = piece_rows // block_rows
    last_query = query_pos[-1]

    def one_turn(turn_index, status):
        offset = turn_index * block_rows
        key_block = lax.dynamic_slice_in_dim(key_rows, offset, block_rows, 0)
        value_block = lax.dynamic_slice_in_dim(value_rows, offset, block_rows, 0)
        seg_block = lax.dynamic_slice_in_dim(seg_rows, offset, block_rows, 0)

        def compute(inner):
            return teacher_update(
                inner, key_block, value_block, seg_block, offset, queries, query_seg, query_pos
            )

        def keep(inner):
            return inner

        return lax.cond(offset > last_query, keep, compute, status)

    return lax.fori_loop(0, turn_count, one_turn, carried)


def on_device(t_query, t_key, t_value, t_out, s_query, s_key, s_value, s_out, segments, selection):
    row_count = t_query.shape[0]
    head_count = t_query.shape[1] // HD
    cycle_size = lax.axis_size("blk")
    my_index = lax.axis_index("blk")
    first_row = my_index * row_count
    token_count = row_count * cycle_size
    query_pos = first_row + jnp.arange(row_count)
    queries = t_query.reshape(row_count, head_count, HD)
    initial = (
        jnp.full((head_count, row_count), masked_score, jnp.float32),
        jnp.zeros((head_count, row_count), jnp.float32),
        jnp.zeros((head_count, row_count, HD), jnp.float32),
    )
    teacher_state = teacher_fold(
        initial,
        lax.all_gather(t_key, "blk", axis=0, tiled=True),
        lax.all_gather(t_value, "blk", axis=0, tiled=True),
        lax.all_gather(segments, "blk", axis=0, tiled=True),
        queries,
        segments,
        query_pos,
    )
    key_full, value_full, seg_full = (
        lax.all_gather(s_key, "blk", axis=0, tiled=True),
        lax.all_gather(s_value, "blk", axis=0, tiled=True),
        lax.all_gather(segments, "blk", axis=0, tiled=True),
    )
    t_attn = (
        (teacher_state[2] / teacher_state[1][..., None])
        .transpose(1, 0, 2)
        .reshape(row_count, head_count * HD)
    )
    t_attn = t_attn.astype(jnp.bfloat16)
    student_full, saved = student_forward(
        s_query, key_full, value_full, seg_full, selection, first_row
    )
    s_attn = student_full.astype(jnp.bfloat16)
    partial_terms = jnp.dot(s_attn, s_out, preferred_element_type=jnp.float32) - jnp.dot(
        t_attn, t_out, preferred_element_type=jnp.float32
    )
    contract = (((1,), (1,)), ((), ()))
    mismatch = lax.psum_scatter(
        partial_terms.astype(jnp.bfloat16), ("head", "grp"), scatter_dimension=1, tiled=True
    ).astype(jnp.float32)
    grad_attn = lax.dot_general(
        lax.all_gather(mismatch.astype(jnp.bfloat16), ("head", "grp"), axis=1, tiled=True),
        s_out,
        contract,
        preferred_element_type=jnp.float32,
    )
    grad_query, grad_keys, grad_values = student_backward(grad_attn, saved, selection, token_count)
    key_grads, value_grads = (
        lax.psum_scatter(
            grad_keys.astype(jnp.bfloat16), "blk", scatter_dimension=0, tiled=True
        ).astype(jnp.float32),
        lax.psum_scatter(
            grad_values.astype(jnp.bfloat16), "blk", scatter_dimension=0, tiled=True
        ).astype(jnp.float32),
    )
    return (mismatch, grad_query, key_grads, value_grads)


def solution(mesh):
    in_specs = (
        P("blk", ("head", "grp")),
        P("blk", ("head", "grp")),
        P("blk", ("head", "grp")),
        P(("head", "grp"), None),
        P("blk", ("head", "grp")),
        P("blk", ("head", "grp")),
        P("blk", ("head", "grp")),
        P(("head", "grp"), None),
        P("blk"),
        P("blk", None),
    )
    out_specs = (
        P("blk", ("head", "grp")),
        P("blk", ("head", "grp")),
        P("blk", ("head", "grp")),
        P("blk", ("head", "grp")),
    )
    return jax.shard_map(
        on_device, mesh=mesh, in_specs=in_specs, out_specs=out_specs, check_vma=False
    )
```

profile of v0, /device:TPU:6, one launch (start us, length us, event | category | flops | bytes accessed | tf_op | source)
XLA Modules:
  0.0 698.8 jit_solution(14955056844412528402)
XLA Ops:
  8.7 2.0 copy.27
  10.8 2.0 copy.29
  14.1 28.1 %all_gather.20 = s32[8192]{0:T(1024)S(1)} all-gather(s32[1024]{0:T(1024)S(1)} %copy-done.12), channel_id=1, replica_groups=mesh['blk'=8,'head'=8,'grp'=2] {'blk'}, dimensions={0}, use_global_device_ids=true | all-gather | bytes 36864 | tf_op jit(solution)/shard_map/all_gather | solution.py:174
  42.2 6.1 gather_fusion.2
  48.6 90.5 %gather_fusion.1 = s32[16384]{0:T(1024)S(1)} fusion(s32[8192]{0:T(1024)S(1)} %all_gather.20, s32[16384]{0:T(1024)S(1)} %broadcast_clamp_fusion), kind=kCustom, calls=%fused_computation.1 | custom fusion | bytes 196608 | tf_op jit(solution)/shard_map/gather | solution.py:31
  140.3 4.8 gather_fusion
  145.1 4.7 gather_fusion.3
  149.8 6.2 fusion.27
  156.0 6.6 fusion.28
  162.7 8.1 %fusion.29 = f32[1024,4096]{1,0:T(8,128)} fusion(bf16[1024,128]{1,0:T(8,128)(2,1)S(1)} %bitcast.102, bf16[128,4096]{1,0:T(8,128)(2,1)S(1)} %copy-done.7), kind=kOutput, calls=%fused_computation.60 | convolution fusion | flops 1073741824 | bytes 18087936 | tf_op jit(solution)/shard_map/dot_general | solution.py:186
  170.7 32.3 %all-gather.12.cloned.1.call-done = bf16[8192,256]{0,1:T(8,128)(2,1)} async-done(((bf16[1024,256]{0,1:T(8,128)(2,1)}), bf16[8192,256]{0,1:T(8,128)(2,1)}) %all-gather.12.cloned.1.call-update) | async-done | bytes 4194320 | tf_op jit(solution)/shard_map/all_gather | solution.py:165
  204.1 80.3 %while.18 = (s32[]{:T(128)}, f32[2,1024]{1,0:T(2,128)S(1)}, f32[2,1024]{1,0:T(2,128)S(1)}, f32[2,1024,128]{2,1,0:T(8,128)}, s32[]{:T(128)}, /*index=5*/s32[8192]...) while((s32[]{:T(128)}, f32[2,1024]{1,0:T(2,128)S(1)}, ...), condition=%wide.region_7.8_spmd.clone, body=%wide.region_2.7_spmd.clone.sunk | while | flops 552605184 | bytes 27425168 | solution.py:145
  204.8 7.0 conditional.3
  207.6 1.1 fusion.4
  208.7 2.0 fusion.8
  212.4 7.0 conditional.3
  215.2 1.1 fusion.4
  216.3 2.0 fusion.8
  220.0 7.0 conditional.3
  222.8 1.1 fusion.4
  223.9 2.0 fusion.8
  227.6 7.0 conditional.3
  230.4 1.1 fusion.4
  231.5 2.0 fusion.8
  235.2 7.0 conditional.3
  238.0 1.1 fusion.4
  239.1 2.0 fusion.8
  242.8 7.0 conditional.3
  245.6 1.1 fusion.4
  246.8 2.0 fusion.8
  250.4 7.0 conditional.3
  253.2 1.1 fusion.4
  254.4 2.0 fusion.8
  258.0 7.0 conditional.3
  259.7 1.1 fusion.2
  260.8 1.1 fusion.4
  262.0 2.0 fusion.8
  265.6 7.0 conditional.3
  267.3 1.1 fusion.2
  268.4 1.1 fusion.4
  269.6 2.0 fusion.8
  273.2 7.0 conditional.3
  274.9 1.1 fusion.2
  276.0 1.1 fusion.4
  277.2 2.0 fusion.8
  284.4 1.6 copy.31
  286.1 11.4 %subtract_convert_fusion = bf16[1024,4096]{1,0:T(8,128)(2,1)} fusion(f32[1024,4096]{1,0:T(8,128)} %fusion.29, bf16[1024,256]{0,1:T(8,128)(2,1)S(1)} %bitcast.96, bf16[256,4096]{1,0:T(8,128)(2,1)S(1)} %copy-done), kind=kOutput, calls=%fused_computation.26 | convolution fusion | flops 2155872256 | bytes 27787264 | tf_op jit(solution)/shard_map/dot_general | solution.py:186
  297.6 141.4 %reduce-scatter.4.cloned.1.call-done = bf16[1024,256]{1,0:T(8,128)(2,1)} async-done(((bf16[1024,4096]{1,0:T(8,128)(2,1)}), bf16[1024,256]{1,0:T(8,128)(2,1)}) %reduce-scatter.4.cloned.1.call-update) | async-done | bytes 524304 | tf_op jit(solution)/shard_map/reduce_scatter | solution.py:190
  439.4 77.8 %all-gather.14.cloned.1.call-done = bf16[1024,4096]{1,0:T(8,128)(2,1)} async-done(((bf16[1024,256]{1,0:T(8,128)(2,1)}), bf16[1024,4096]{1,0:T(8,128)(2,1)}) %all-gather.14.cloned.1.call-update) | async-done | bytes 8388624 | tf_op jit(solution)/shard_map/all_gather | solution.py:194
  517.2 5.9 fusion.30
  523.3 4.6 multiply_multiply_fusion
  527.9 9.0 %fusion.32 = f32[16,1024,128]{2,1,0:T(8,128)} fusion(f32[16,64,1024]{2,1,0:T(8,128)S(1)} %multiply_multiply_fusion, bf16[16,64,128]{2,1,0:T(8,128)(2,1)S(1)} %bitcast.104), kind=kOutput, calls=%fused_computation.63 | convolution fusion | flops 1610612736 | bytes 12845056 | tf_op jit(solution)/shard_map/bhqk,bqhd->bkhd/dot_general | solution.py:69
  536.9 2.5 broadcast.200.clone
  539.4 39.2 %scatter_fusion = f32[128,64,128]{2,1,0:T(8,128)} fusion(f32[128,64,128]{2,1,0:T(8,128)} %broadcast.200.clone, s32[256]{0:T(256)S(1)} %bitcast.106, f32[256,64,128]{2,1,0:T(8,128)} %bitcast.85), kind=kCustom, calls=%fused_computation.4 | custom fusion | flops 2097152 | bytes 25166848 | tf_op jit(solution)/shard_map/scatter-add | solution.py:80
  578.6 4.0 convert_element_type.63
  583.0 10.6 %convolution_bitcast_fusion = f32[16,1024,1,128]{1,3,0,2:T(8,128)} fusion(f32[16,64,128]{2,1,0:T(8,128)S(1)} %bitcast.101, f32[16,64,1024]{2,1,0:T(8,128)} %get-tuple-element.409, f32[16,64]{1,0:T(8,128)S(1)} %get-tuple-element.408), kind=kOutput, calls=%fused_computation.31 | convolution fusion | flops 1611661312 | bytes 13111296 | tf_op jit(solution)/shard_map/bhqk,bqhd->bkhd/dot_general | solution.py:55
  593.5 9.3 %copy.32 = f32[16,1024,1,128]{3,1,0,2:T(8,128)} copy(f32[16,1024,1,128]{1,3,0,2:T(8,128)} %convolution_bitcast_fusion) | data formatting | bytes 16777216 | tf_op jit(solution)/shard_map/bhqk,bqhd->bkhd/transpose | solution.py:55
  602.8 2.5 broadcast.200.clone.1
  605.4 39.3 %scatter_fusion.1 = f32[128,64,128]{2,1,0:T(8,128)} fusion(f32[128,64,128]{2,1,0:T(8,128)} %broadcast.200.clone.1, s32[256]{0:T(256)S(1)} %bitcast.107, f32[256,64,128]{2,1,0:T(8,128)} %bitcast.84), kind=kCustom, calls=%fused_computation.5 | custom fusion | flops 2097152 | bytes 25166848 | tf_op jit(solution)/shard_map/scatter-add | solution.py:85
  644.7 4.1 convert_element_type.66
  649.9 6.4 fusion.31
  656.3 1.8 convert_element_type.65
  658.1 32.0 %reduce-scatter.8.cloned.1.call-done = bf16[1024,128]{1,0:T(8,128)(2,1)} async-done(((bf16[8192,128]{1,0:T(8,128)(2,1)}), bf16[1024,128]{1,0:T(8,128)(2,1)}) %reduce-scatter.8.cloned.1.call-update) | async-done | bytes 262160 | tf_op jit(solution)/shard_map/reduce_scatter | solution.py:204
  690.1 1.8 convert_element_type.68
  (237 shorter events, 41.8 us)
Async XLA Ops:
  7.2 278.9 %copy-start = (bf16[256,4096]{1,0:T(8,128)(2,1)S(1)}, bf16[256,4096]{1,0:T(8,128)(2,1)}, u32[]{:S(2)}) copy-start(bf16[256,4096]{1,0:T(8,128)(2,1)} %param.17) | copy-start | bytes 6291460
  7.2 6.9 copy-start.12
  7.2 133.1 %all-gather.6.cloned.1.call-start = ((), (), s32[]{:S(2)}) async-start(), calls=%async_computation.3 | async-start | bytes 2359296 | tf_op jit(solution)/shard_map/all_gather | solution.py:173
  7.9 137.2 %all-gather.8.cloned.1.call-start = ((), (), s32[]{:S(2)}) async-start(), calls=%async_computation.4 | async-start | bytes 2359296 | tf_op jit(solution)/shard_map/all_gather | solution.py:172
  8.7 162.1 %all-gather.10.cloned.1.call-start = ((), (), s32[]{:S(2)}) async-start(), calls=%async_computation.5 | async-start | bytes 4718592 | tf_op jit(solution)/shard_map/all_gather | solution.py:164
  10.8 192.3 %all-gather.12.cloned.1.call-start = ((), (), s32[]{:S(2)}) async-start(), calls=%async_computation.6 | async-start | bytes 4718592 | tf_op jit(solution)/shard_map/all_gather | solution.py:165
  12.9 426.1 %reduce-scatter.4.cloned.1.call-start = ((), (), s32[]{:S(2)}) async-start(), calls=%async_computation.7 | async-start | bytes 8912896 | tf_op jit(solution)/shard_map/reduce_scatter | solution.py:190
  48.6 91.2 %copy-start.9 = (bf16[1024,256]{1,0:T(8,128)(2,1)S(1)}, bf16[1024,256]{1,0:T(8,128)(2,1)}, u32[]{:S(2)}) copy-start(bf16[1024,256]{1,0:T(8,128)(2,1)} %param.14) | copy-start | bytes 1572868
  145.1 4.7 copy-start.11
  156.0 6.6 copy-start.7
  206.5 2.3 copy-start.4
  210.7 1.0 copy-start.5
  214.1 2.3 copy-start.4
  218.4 1.0 copy-start.5
  221.7 2.3 copy-start.4
  226.0 1.0 copy-start.5
  229.3 2.3 copy-start.4
  233.6 1.0 copy-start.5
  236.9 2.3 copy-start.4
  241.2 1.0 copy-start.5
  244.5 2.3 copy-start.4
  248.8 1.0 copy-start.5
  252.1 2.3 copy-start.4
  256.4 1.0 copy-start.5
  259.7 2.3 copy-start.4
  264.0 1.0 copy-start.5
  267.3 2.3 copy-start.4
  271.6 1.0 copy-start.5
  274.9 2.3 copy-start.4
  279.2 1.0 copy-start.5
  297.5 141.8 %copy-start.13 = (s32[16,16]{1,0:T(8,128)S(1)}, s32[16,16]{1,0:T(8,128)}, u32[]{:S(2)}) copy-start(s32[16,16]{1,0:T(8,128)} %param.23) | copy-start | bytes 3076
  297.5 219.6 %copy-start.8 = (bf16[128,4096]{1,0:T(8,128)(2,1)S(1)}, bf16[128,4096]{1,0:T(8,128)(2,1)}, u32[]{:S(2)}) copy-start(bf16[128,4096]{1,0:T(8,128)(2,1)} %param.21) | copy-start | bytes 3145732
  297.5 219.6 %all-gather.14.cloned.1.call-start = ((), (), s32[]{:S(2)}) async-start(), calls=%async_computation.8 | async-start | bytes 8912896 | tf_op jit(solution)/shard_map/all_gather | solution.py:194
  439.0 217.3 %reduce-scatter.6.cloned.1.call-start = ((), (), s32[]{:S(2)}) async-start(), calls=%async_computation.9 | async-start | bytes 2359296 | tf_op jit(solution)/shard_map/reduce_scatter | solution.py:201
  439.4 83.6 %copy-start.10 = (f32[16,64,1,128]{3,1,0,2:T(8,128)S(1)}, f32[16,64,1,128]{3,1,0,2:T(8,128)}, u32[]{:S(2)}) copy-start(f32[16,64,1,128]{3,1,0,2:T(8,128)} %get-tuple-element.411) | copy-start | bytes 1572868
  517.2 6.1 copy-start.3
  517.2 6.1 copy-start.14
  527.9 9.0 %copy-start.2 = (f32[16,64,1024]{2,1,0:T(8,128)}, f32[16,64,1024]{2,1,0:T(8,128)S(1)}, u32[]{:S(2)}) copy-start(f32[16,64,1024]{2,1,0:T(8,128)S(1)} %multiply_multiply_fusion) | copy-start | bytes 12582916
  582.6 107.5 %reduce-scatter.8.cloned.1.call-start = ((), (), s32[]{:S(2)}) async-start(), calls=%async_computation.10 | async-start | bytes 2359296 | tf_op jit(solution)/shard_map/reduce_scatter | solution.py:204
  644.7 4.1 copy-start.6
  648.8 43.1 %copy-start.1 = (bf16[256,4096]{1,0:T(8,128)(2,1)S(1)}, bf16[256,4096]{1,0:T(8,128)(2,1)}, u32[]{:S(2)}) copy-start(bf16[256,4096]{1,0:T(8,128)(2,1)} %param.17) | copy-start | bytes 6291460
Sparse Core Ops, SparseCore 0:
  9.7 43.5 all-gather.5
  54.9 40.3 all-gather.7
  97.5 52.0 all-gather.9
  151.7 51.3 all-gather.11
  297.7 141.2 reduce-scatter.3
  441.1 75.9 all-gather.13
  582.8 40.9 reduce-scatter.5
  649.0 41.1 reduce-scatter.7
where the time goes:
time: 702 us; the launch traced here: 699 us
  waiting for transfers between devices  285 us (41%)
  local copies, waits for them, and re-layouts  150 us (21%)
  other arithmetic  109 us (16%)
  matrix products  99.8 us (14%)
  blocking collectives  28.1 us (4%)
  between operations  14.4 us (2%)
  loops' own time  11.5 us (2%)
    reduce_scatter x1, waiting for transfers between devices, on_device(): lax.psum_scatter(partial_terms.astype(jnp.bfloat16), ('head', 'grp'), sca...  141 us
    gather x2, local copies, waits for them, and re-layouts, student_forward(): key_seg = segment_all[key_pos]  90.6 us
    all_gather x1, waiting for transfers between devices, on_device(): lax.all_gather(mismatch.astype(jnp.bfloat16), ('head', 'grp'), axis=1, ti...  77.8 us
    scatter-add x1, other arithmetic, student_backward(): value_total = jnp.zeros((token_count // BS, BS, width), jnp.float32).at[f...  39.3 us
    scatter-add x1, other arithmetic, student_backward(): key_total = jnp.zeros((token_count // BS, BS, width), jnp.float32).at[fla...  39.2 us
    all_gather x1, waiting for transfers between devices, on_device(): lax.all_gather(t_value, 'blk', axis=0, tiled=True)  32.3 us
    reduce_scatter x1, waiting for transfers between devices, on_device(): lax.psum_scatter(grad_values.astype(jnp.bfloat16), 'blk', scatter_dimensi...  32 us
    all_gather x1, blocking collectives, on_device(): lax.all_gather(segments, 'blk', axis=0, tiled=True)  28.1 us
  transfers between devices with their start and end apart: 8, of which 4 were waited for; matrix products, arithmetic and copies ran while one was open for 30% of the time, Pallas kernels for 0%

commit v1 on v0

v1 whole, which is shorter than its diff:
```python
import jax
import jax.numpy as jnp
from jax import lax
from jax.experimental import pallas as pl
from jax.experimental.pallas import tpu as pltpu
from jax.sharding import Mesh
from jax.sharding import PartitionSpec as P

HD = 128
BS = 64
NSEL = 16
BLOCK = 1024
TILE_Q = 512
TILE_K = 512
SCALE = HD ** (-0.5)
EXP_SCALE = SCALE * 1.4426950408889634
LOWEST = -1e30

BLK = ("xlo", "y")
GROUP = ("z", "core", "xhi")
ZX = ("z", "xhi")
f32 = jnp.float32
bf16 = jnp.bfloat16

SMEM = pltpu.SMEM
ROWS_NT = (((1,), (1,)), ((), ()))
ROWS_TN = (((0,), (0,)), ((), ()))


def y_pairs(shift, all_x, causal_x):
    pairs = []
    for x in range(2):
        for y in range(4):
            to = (y + shift) % 4
            if x in all_x or (x in causal_x and y < to):
                pairs.append((4 * x + y, 4 * x + to))
    return pairs


def place(meta, kv_refs, key_all, value_all):
    for j, ref in enumerate(kv_refs):
        start = pl.multiple_of(meta[8 + j] * BLOCK, BLOCK)
        key_all[pl.ds(start, BLOCK), :] = ref[:BLOCK, :]
        value_all[pl.ds(start, BLOCK), :] = ref[BLOCK : 2 * BLOCK, :]


def find_border(kv_refs, border_ref):
    counts = None
    for ref in kv_refs:
        part = ref[2 * BLOCK :, :].astype(f32)
        counts = part if counts is None else counts + part
    border_ref[0] = jnp.sum(counts).astype(jnp.int32)


def teacher_kernel(meta, q_ref, *refs):
    kv_refs, o_ref, key_all, value_all, border_ref = refs[:8], *refs[8:]
    step = pl.program_id(0)

    @pl.when(step == 0)
    def _():
        place(meta, kv_refs, key_all, value_all)
        find_border(kv_refs, border_ref)

    first = meta[0] * BLOCK + step * TILE_Q
    border = border_ref[0]
    low_first = jnp.where(first >= border, border, 0)
    low_last = jnp.where(first + TILE_Q - 1 >= border, border, 0)
    queries = q_ref[...]
    q_pos = first + lax.broadcasted_iota(jnp.int32, (TILE_Q, 1), 0)
    q_low = jnp.where(q_pos >= border, border, 0)

    def turn(masked, j, carry):
        largest, total, acc = carry
        start = pl.multiple_of(j * TILE_K, TILE_K)
        scores = lax.dot_general(
            queries, key_all[pl.ds(start, TILE_K), :], ROWS_NT, preferred_element_type=f32
        )
        if masked:
            k_pos = start + lax.broadcasted_iota(jnp.int32, (1, TILE_K), 1)
            scores = jnp.where((k_pos <= q_pos) & (k_pos >= q_low), scores, LOWEST)
        new = jnp.maximum(largest, jnp.max(scores, axis=1, keepdims=True))
        factor = jnp.exp2((largest - new) * EXP_SCALE)
        weights = jnp.exp2((scores - new) * EXP_SCALE)
        total = factor * total + jnp.sum(weights, axis=1, keepdims=True)
        acc = factor * acc + jnp.dot(
            weights.astype(bf16), value_all[pl.ds(start, TILE_K), :], preferred_element_type=f32
        )
        return new, total, acc

    carry = (
        jnp.full((TILE_Q, 1), LOWEST, f32),
        jnp.zeros((TILE_Q, 1), f32),
        jnp.zeros((TILE_Q, HD), f32),
    )
    begin = low_first // TILE_K
    diagonal = first // TILE_K
    clear = jnp.minimum((low_last + TILE_K - 1) // TILE_K, diagonal)
    carry = lax.fori_loop(begin, clear, lambda j, c: turn(True, j, c), carry)
    carry = lax.fori_loop(clear, diagonal, lambda j, c: turn(False, j, c), carry)
    for j in range(max(TILE_Q // TILE_K, 1)):
        carry = turn(True, diagonal + j, carry)
    _, total, acc = carry
    o_ref[...] = (acc / total).astype(bf16)


def teacher_attention(meta, queries, kv_blocks):
    return pl.pallas_call(
        teacher_kernel,
        grid=(BLOCK // TILE_Q,),
        in_specs=[
            pl.BlockSpec(memory_space=SMEM),
            pl.BlockSpec((TILE_Q, HD), lambda i: (i, 0)),
        ]
        + [pl.BlockSpec(memory_space=pltpu.VMEM)] * 8,
        out_specs=pl.BlockSpec((TILE_Q, HD), lambda i: (i, 0)),
        out_shape=jax.ShapeDtypeStruct((BLOCK, HD), bf16),
        scratch_shapes=[pltpu.VMEM((8 * BLOCK, HD), bf16)] * 2 + [SMEM((1,), jnp.int32)],
        compiler_params=pltpu.CompilerParams(vmem_limit_bytes=40 << 20),
        cost_estimate=pl.CostEstimate(
            flops=4 * 4 * BLOCK * BLOCK * HD, bytes_accessed=5 << 20, transcendentals=5 * BLOCK * BLOCK
        ),
        name="teacher_attention",
    )(meta, queries, *kv_blocks)


def chosen_rows(sel, row, table):
    pieces = []
    for n in range(NSEL):
        start = pl.multiple_of(sel[row * NSEL + n] * BS, BS)
        pieces.append(table[pl.ds(start, BS), :])
    return jnp.concatenate(pieces, axis=0)


def student_forward_kernel(meta, sel, q_ref, kpos_ref, *refs):
    kv_refs, o_ref, p_ref, key_all, value_all, border_ref = refs[:8], *refs[8:]
    row = pl.program_id(0)

    @pl.when(row == 0)
    def _():
        place(meta, kv_refs, key_all, value_all)
        find_border(kv_refs, border_ref)

    border = border_ref[0]
    q_pos = meta[0] * BLOCK + row * BS + lax.broadcasted_iota(jnp.int32, (BS, 1), 0)
    q_low = jnp.where(q_pos >= border, border, 0)
    k_pos = kpos_ref[0]
    scores = lax.dot_general(
        q_ref[...], chosen_rows(sel, row, key_all), ROWS_NT, preferred_element_type=f32
    )
    scores = jnp.where((k_pos <= q_pos) & (k_pos >= q_low), scores, LOWEST)
    weights = jnp.exp2((scores - jnp.max(scores, axis=1, keepdims=True)) * EXP_SCALE)
    total = jnp.sum(weights, axis=1, keepdims=True)
    p_ref[...] = weights / total
    blended = jnp.dot(
        weights.astype(bf16), chosen_rows(sel, row, value_all), preferred_element_type=f32
    )
    o_ref[...] = (blended / total).astype(bf16)


def student_forward(meta, sel, queries, k_pos, kv_blocks):
    rows = BLOCK // BS
    return pl.pallas_call(
        student_forward_kernel,
        grid=(rows,),
        in_specs=[
            pl.BlockSpec(memory_space=SMEM),
            pl.BlockSpec(memory_space=SMEM),
            pl.BlockSpec((BS, HD), lambda i: (i, 0)),
            pl.BlockSpec((1, 1, NSEL * BS), lambda i: (i, 0, 0)),
        ]
        + [pl.BlockSpec(memory_space=pltpu.VMEM)] * 8,
        out_specs=[
            pl.BlockSpec((BS, HD), lambda i: (i, 0)),
            pl.BlockSpec((BS, NSEL * BS), lambda i: (i, 0)),
        ],
        out_shape=[
            jax.ShapeDtypeStruct((BLOCK, HD), bf16),
            jax.ShapeDtypeStruct((BLOCK, NSEL * BS), f32),
        ],
        scratch_shapes=[pltpu.VMEM((8 * BLOCK, HD), bf16)] * 2 + [SMEM((1,), jnp.int32)],
        compiler_params=pltpu.CompilerParams(vmem_limit_bytes=40 << 20),
        cost_estimate=pl.CostEstimate(
            flops=4 * BLOCK * NSEL * BS * HD, bytes_accessed=9 << 20, transcendentals=BLOCK * NSEL * BS
        ),
        name="student_forward",
    )(meta, sel, queries, k_pos, *kv_blocks)


def student_backward_kernel(meta, sel, q_ref, p_ref, g_ref, *refs):
    kv_refs, dq_ref, out_refs = refs[:8], refs[8], refs[9:17]
    key_all, value_all, dk_all, dv_all = refs[17:]
    row = pl.program_id(0)

    @pl.when(row == 0)
    def _():
        place(meta, kv_refs, key_all, value_all)
        dk_all[...] = jnp.zeros_like(dk_all)
        dv_all[...] = jnp.zeros_like(dv_all)

    grad = jnp.sum(g_ref[...].astype(f32), axis=0).astype(bf16)
    weights = p_ref[...]
    weight_grad = lax.dot_general(
        grad, chosen_rows(sel, row, value_all), ROWS_NT, preferred_element_type=f32
    )
    row_dots = jnp.sum(weights * weight_grad, axis=1, keepdims=True)
    score_grad = (weights * (weight_grad - row_dots) * SCALE).astype(bf16)
    dq_ref[...] = jnp.dot(score_grad, chosen_rows(sel, row, key_all), preferred_element_type=f32)
    key_grad = lax.dot_general(score_grad, q_ref[...], ROWS_TN, preferred_element_type=f32)
    value_grad = lax.dot_general(weights.astype(bf16), grad, ROWS_TN, preferred_element_type=f32)
    for n in range(NSEL):
        start = pl.multiple_of(sel[row * NSEL + n] * BS, BS)
        dk_all[pl.ds(start, BS), :] += key_grad[n * BS : (n + 1) * BS, :]
        dv_all[pl.ds(start, BS), :] += value_grad[n * BS : (n + 1) * BS, :]

    @pl.when(row == pl.num_programs(0) - 1)
    def _():
        for j, ref in enumerate(out_refs):
            start = pl.multiple_of(meta[16 + j] * BLOCK, BLOCK)
            ref[:BLOCK, :] = dk_all[pl.ds(start, BLOCK), :].astype(bf16)
            ref[BLOCK:, :] = dv_all[pl.ds(start, BLOCK), :].astype(bf16)


def student_backward(meta, sel, queries, weights, grad_pieces, kv_blocks):
    rows = BLOCK // BS
    return pl.pallas_call(
        student_backward_kernel,
        grid=(rows,),
        in_specs=[
            pl.BlockSpec(memory_space=SMEM),
            pl.BlockSpec(memory_space=SMEM),
            pl.BlockSpec((BS, HD), lambda i: (i, 0)),
            pl.BlockSpec((BS, NSEL * BS), lambda i: (i, 0)),
            pl.BlockSpec((8, BS, HD), lambda i: (0, i, 0)),
        ]
        + [pl.BlockSpec(memory_space=pltpu.VMEM)] * 8,
        out_specs=[pl.BlockSpec((BS, HD), lambda i: (i, 0))] + [pl.BlockSpec(memory_space=pltpu.VMEM)] * 8,
        out_shape=[jax.ShapeDtypeStruct((BLOCK, HD), f32)]
        + [jax.ShapeDtypeStruct((2 * BLOCK, HD), bf16)] * 8,
        scratch_shapes=[pltpu.VMEM((8 * BLOCK, HD), bf16)] * 2
        + [pltpu.VMEM((8 * BLOCK, HD), f32)] * 2,
        compiler_params=pltpu.CompilerParams(vmem_limit_bytes=48 << 20),
        cost_estimate=pl.CostEstimate(
            flops=8 * BLOCK * NSEL * BS * HD, bytes_accessed=15 << 20, transcendentals=0
        ),
        name="student_backward",
    )(meta, sel, queries, weights, grad_pieces, *kv_blocks)


def project_kernel(transposed, added, where, s_ref, a_ref, b_ref, w_ref, *refs):
    acc = None
    for ref, j in ((s_ref, 0), (a_ref, 1 + where[1]), (b_ref, 2 - where[1])):
        span = pl.ds(pl.multiple_of(j * HD, HD), HD)
        if transposed:
            part = lax.dot_general(ref[...], w_ref[:, span], ROWS_NT, preferred_element_type=f32)
        else:
            part = jnp.dot(ref[...], w_ref[span, :], preferred_element_type=f32)
        acc = part if acc is None else acc + part
    if added:
        acc = acc + refs[0][0].astype(f32)
    refs[-1][0] = acc.astype(bf16)


def project(where, attn, weight, width, transposed, extra=None):
    def piece(p, at):
        return (p // 2) * 4 + at[0] * 2 + p % 2

    if transposed:
        w_spec = pl.BlockSpec((width, 3 * HD), lambda p, c: (piece(p, c), 0))
    else:
        w_spec = pl.BlockSpec((3 * HD, width), lambda p, c: (0, piece(p, c)))
    out_spec = pl.BlockSpec((1, BLOCK, width), lambda p, c: (p, 0, 0))
    args = list(attn) + [weight] + ([] if extra is None else [extra])

    def kernel(*refs):
        project_kernel(transposed, extra is not None, *refs)

    return pl.pallas_call(
        kernel,
        grid_spec=pltpu.PrefetchScalarGridSpec(
            num_scalar_prefetch=1,
            grid=(8,),
            in_specs=[pl.BlockSpec((BLOCK, HD), lambda p, c: (0, 0))] * 3
            + [w_spec]
            + ([] if extra is None else [out_spec]),
            out_specs=out_spec,
        ),
        out_shape=jax.ShapeDtypeStruct((8, BLOCK, width), bf16),
        compiler_params=pltpu.CompilerParams(vmem_limit_bytes=32 << 20),
        cost_estimate=pl.CostEstimate(
            flops=2 * 8 * BLOCK * width * 3 * HD,
            bytes_accessed=2 * 8 * BLOCK * width * (1 if extra is None else 2) + (2 << 20),
            transcendentals=0,
        ),
        name="project_grad" if transposed else "project_mismatch",
    )(where, *args)


def on_device(t_query, t_key, t_value, t_out, s_query, s_key, s_value, s_out, segments, selection):
    x, y, core = lax.axis_index("xlo"), lax.axis_index("y"), lax.axis_index("core")
    mine = 4 * x + y
    partner = 4 * (1 - x) + y

    def half(array, which, axis=1):
        return lax.dynamic_slice_in_dim(array, which * HD, HD, axis)

    def along_y(block, all_x, causal_x):
        return tuple(
            lax.ppermute(block, BLK, y_pairs(shift, all_x, causal_x)) for shift in (1, -1, 2)
        )

    to_partner = [(i, i ^ 4) for i in range(8)]
    spots = jnp.stack([y, (y + 3) % 4, (y + 1) % 4, (y + 2) % 4]).astype(jnp.int32)

    zeros = jnp.sum((segments == 0).reshape(8, HD).astype(f32), axis=0, keepdims=True)
    zeros = jnp.pad(zeros, ((0, 15), (0, 0))).astype(bf16)

    s_own = jnp.concatenate([s_key, s_value, zeros], axis=0)
    s_near = along_y(s_own, (0,), (1,))
    sent = jnp.concatenate([half(t_key, 1 - x), half(t_value, 1 - x), zeros], axis=0)
    t_got = lax.ppermute(sent, BLK, to_partner)
    q_got = lax.ppermute(half(t_query, 1 - x), BLK, to_partner)
    t_own = jnp.concatenate([half(t_key, x), half(t_value, x), zeros], axis=0)
    t_near = along_y(t_own, (0,), (1,))
    t_far = along_y(t_got, (1,), (0,))
    up = [(i, i + 4) for i in range(4)]
    s_low = tuple(lax.ppermute(block, BLK, up) for block in (s_own,) + s_near)

    weight = jnp.concatenate([s_out, -t_out], axis=0)
    rows = lax.dynamic_slice_in_dim(s_out, mine * (HD // 8), HD // 8, 0)
    rows = lax.all_gather(rows, GROUP, axis=0, tiled=True)
    rows, t_near = lax.optimization_barrier((rows, t_near))
    through = lax.dot_general(rows, weight, ROWS_NT, preferred_element_type=f32).astype(bf16)
    through = lax.all_gather(through, BLK, axis=0, tiled=True)
    through = through.reshape(8, 16, HD // 8, 3 * HD).transpose(1, 0, 2, 3).reshape(16 * HD, 3 * HD)

    def meta_of(first, order):
        head = jnp.stack([first] + [jnp.int32(0)] * 7).astype(jnp.int32)
        return jnp.concatenate([head, order, spots, 4 + spots])

    order = jnp.concatenate([4 * x + spots, 4 * (1 - x) + spots]).astype(jnp.int32)
    sel = selection.reshape(-1)
    k_pos = (selection[:, :, None] * BS + jnp.arange(BS, dtype=jnp.int32)).reshape(-1, 1, NSEL * BS)

    s_blocks = (s_own,) + s_near + s_low
    s_attn, weights = student_forward(meta_of(mine, order), sel, s_query, k_pos, s_blocks)

    t_blocks = (t_own,) + t_near + (t_got,) + t_far
    away = teacher_attention(meta_of(partner, order), q_got, t_blocks)
    back = lax.ppermute(away, BLK, to_partner)
    here = teacher_attention(meta_of(mine, order), half(t_query, x), t_blocks)

    attn = (s_attn, here, back)
    this = jnp.stack([core, x]).astype(jnp.int32)
    other = jnp.stack([1 - core, x]).astype(jnp.int32)
    to_core = [(0, 1), (1, 0)]
    grad = project(other, attn, through, HD, True)
    grad = lax.ppermute(grad, "core", to_core)
    grad = project(this, attn, through, HD, True, grad)
    attn, grad = lax.optimization_barrier((attn, grad))
    grad = lax.all_to_all(grad, ZX, 0, 0, tiled=True)

    part = project(other, attn, weight, 2 * HD, False)
    part = lax.ppermute(part, "core", to_core)
    part = project(this, attn, weight, 2 * HD, False, part)
    part, grad = lax.optimization_barrier((part, grad))
    part = lax.all_to_all(part, ZX, 0, 0, tiled=True)

    out = student_backward(meta_of(mine, order), sel, s_query, weights, grad, s_blocks)
    s_dq, pieces = out[0], out[1:]

    def earlier(shift, all_x, causal_x):
        pairs = []
        for i in range(2):
            for j in range(4):
                to = (j + shift) % 4
                if i in all_x or (i in causal_x and to < j):
                    pairs.append((4 * i + j, 4 * i + to))
        return pairs

    low, high = pieces[:4], pieces[4:]
    low_sum, high_sum = low[0].astype(f32), high[0].astype(f32)
    for j, shift in ((1, -1), (2, 1), (3, 2)):
        low_sum += lax.ppermute(low[j], BLK, earlier(shift, (1,), (0,))).astype(f32)
    for j, shift in ((1, -1), (2, 1), (3, 2)):
        high_sum += lax.ppermute(high[j], BLK, earlier(shift, (), (1,))).astype(f32)
    across = lax.ppermute(low_sum.astype(bf16), BLK, [(i + 4, i) for i in range(4)])
    total = jnp.where(x == 0, low_sum + across.astype(f32), high_sum)

    mismatch = jnp.sum(part.astype(f32), axis=0)
    return mismatch, s_dq, total[:BLOCK], total[BLOCK:]


def solution(mesh):
    fine = Mesh(mesh.devices.reshape(2, 4, 4, 2, 2), ("xlo", "y", "z", "core", "xhi"))
    data = P(BLK, GROUP)
    flat = P(GROUP, None)
    return jax.shard_map(
        on_device,
        mesh=fine,
        in_specs=(data, data, data, flat, data, data, data, flat, P(BLK), P(BLK, None)),
        out_specs=(data, data, data, data),
        check_vma=False,
    )
```

time: 702 us -> 349 us (0.50)
  waiting for transfers between devices: 285 us -> 152 us
  local copies, waits for them, and re-layouts: 150 us -> 21 us
  other arithmetic: 109 us -> 10.8 us
  matrix products: 99.8 us -> 4.44 us
  starting transfers between devices: 0.8 us -> 82 us
  Pallas kernels: 0 us -> 62 us
  blocking collectives: 28.1 us -> 0 us
  loops' own time: 11.5 us -> 0 us
    reduce_scatter x3 -> x0, waiting for transfers between devices: 173 us -> none  [the longest x1 141 us: on_device(): lax.psum_scatter(partial_terms.astype(jnp.bfloat16), ('head', 'grp'), sca...]
    ppermute x0 -> x25, waiting for transfers between devices: none -> 117 us  [the longest x9 44.3 us: along_y(): lax.ppermute(block, BLK, y_pairs(shift, all_x, causal_x))]
    gather x6 -> x0, local copies, waits for them, and re-layouts: 106 us -> none  [the longest x2 90.6 us: student_forward(): key_seg = segment_all[key_pos]]
    all_gather x5 -> x2, waiting for transfers between devices: 110 us -> 20.4 us  [the longest x1 20.4 us: on_device(): rows = lax.all_gather(rows, GROUP, axis=0, tiled=True)]
    dot_general x28 -> x1, matrix products: 93.6 us -> 4.44 us  [on_device(): lax.dot_general(rows, weight, ROWS_NT, preferred_element_type=f32)]
    scatter-add x2 -> x0, other arithmetic: 78.6 us -> none  [the longest x1 39.3 us: student_backward(): value_total = jnp.zeros((token_count // BS, BS, width), jnp.float32).at[f...]
    ppermute x0 -> x25, starting transfers between devices: none -> 67.3 us  [the longest x9 28.3 us: along_y(): lax.ppermute(block, BLK, y_pairs(shift, all_x, causal_x))]
    pallas_call x0 -> x8, Pallas kernels: none -> 62 us  [the longest x4 22.2 us: project(): pl.pallas_call(kernel, grid_spec=pltpu.PrefetchScalarGridSpec(num_scalar_...]
  transfers between devices with their start and end apart: 8 -> 29, of which waited for: 4 -> 15; matrix products, arithmetic and copies ran while one was open for 30% -> 4% of each run, Pallas kernels for 0% -> 14%
where the time goes in v1:
time: 349 us; the launch traced here: 347 us
  waiting for transfers between devices  152 us (44%)
  starting transfers between devices  82 us (23%)
  Pallas kernels  62 us (18%)
  local copies, waits for them, and re-layouts  21 us (6%)
  between operations  14.7 us (4%)
  other arithmetic  10.8 us (3%)
  matrix products  4.44 us (1%)
    ppermute x9, waiting for transfers between devices, along_y(): lax.ppermute(block, BLK, y_pairs(shift, all_x, causal_x))  44.3 us
    ppermute x3, waiting for transfers between devices, on_device(): low_sum += lax.ppermute(low[j], BLK, earlier(shift, (1,), (0,))).astype(f32)  31.2 us
    ppermute x9, starting transfers between devices, along_y(): lax.ppermute(block, BLK, y_pairs(shift, all_x, causal_x))  28.3 us
    pallas_call x4, Pallas kernels, project(): pl.pallas_call(kernel, grid_spec=pltpu.PrefetchScalarGridSpec(num_scalar_...  22.2 us
    ppermute x4, waiting for transfers between devices, on_device(): s_low = tuple((lax.ppermute(block, BLK, up) for block in (s_own,) + s_near))  21.5 us
    all_gather x1, waiting for transfers between devices, on_device(): rows = lax.all_gather(rows, GROUP, axis=0, tiled=True)  20.4 us
    ppermute x3, starting transfers between devices, on_device(): low_sum += lax.ppermute(low[j], BLK, earlier(shift, (1,), (0,))).astype(f32)  18.9 us
    pallas_call x1, Pallas kernels, student_backward(): pl.pallas_call(student_backward_kernel, grid=(rows,), in_specs=[pl.BlockS...  17.5 us
  transfers between devices with their start and end apart: 29, of which 15 were waited for; matrix products, arithmetic and copies ran while one was open for 4% of the time, Pallas kernels for 14%

profile of v1, /device:TPU:6, one launch (start us, length us, event | category | flops | bytes accessed | tf_op | source)
XLA Modules:
  0.0 347.4 jit_solution(6198334422910145450)
XLA Ops:
  7.2 1.6 constant_dynamic-slice_fusion.3
  9.6 1.3 constant_dynamic-slice_fusion.1
  11.1 5.4 %collective-permute-start.9 = (bf16[2064,128]{1,0:T(8,128)(2,1)S(1)}, bf16[2064,128]{1,0:T(8,128)(2,1)S(1)}, u32[]{:S(2)}, u32[]{:S(2)}) collective-permute-start(bf16[2064,128]{1,0:T(8,128)(2,1)S(1)} %get-tuple-element.58.refs_0_), channel_id=1, source_target_pairs={{0,32},{16,48},{32,0},{48,16},{64,96},{80,112},{1,33},{17,49},{33,... | collective-permute-start | bytes 1585160 | tf_op jit(solution)/shard_map/ppermute | solution.py:308
  16.5 1.3 collective-permute-start.8
  17.8 2.0 collective-permute-start.7
  19.8 1.8 neg.3
  21.6 7.3 %collective-permute-done.9.refs_3_ = bf16[2064,128]{1,0:T(8,128)(2,1)S(1)} collective-permute-done((bf16[2064,128]{1,0:T(8,128)(2,1)S(1)}, bf16[2064,128]{1,0:T(8,128)(2,1)S(1)}, u32[]{:S(2)}, u32[]{:S(2)}) %collective-permute-start.9) | collective-permute-done | bytes 528416 | tf_op jit(solution)/shard_map/ppermute | solution.py:308
  28.9 10.2 %collective-permute-done.8.refs_2_ = bf16[2064,128]{1,0:T(8,128)(2,1)S(1)} collective-permute-done((bf16[2064,128]{1,0:T(8,128)(2,1)S(1)}, bf16[2064,128]{1,0:T(8,128)(2,1)S(1)}, u32[]{:S(2)}, u32[]{:S(2)}) %collective-permute-start.8) | collective-permute-done | bytes 528416 | tf_op jit(solution)/shard_map/ppermute | solution.py:308
  39.1 20.4 %all-gather.3.cloned.1.call-done = bf16[256,4096]{1,0:T(8,128)(2,1)} async-done(((bf16[16,4096]{1,0:T(8,128)(2,1)}), bf16[256,4096]{1,0:T(8,128)(2,1)}) %all-gather.3.cloned.1.call-update) | async-done | bytes 2097168 | tf_op jit(solution)/shard_map/all_gather | solution.py:330
  59.5 4.4 %convolution_convert_fusion = bf16[256,384]{1,0:T(8,128)(2,1)} fusion(bf16[256,4096]{1,0:T(8,128)(2,1)} %all-gather.3.cloned.1.call-done, bf16[256,4096]{1,0:T(8,128)(2,1)} %neg.3, bf16[128,4096]{1,0:T(8,128)(2,1)} %param.17), kind=kOutput, calls=%fused_computation.2 | convolution fusion | flops 811696128 | bytes 5439488 | tf_op jit(solution)/shard_map/dot_general | solution.py:332
  64.1 4.9 %collective-permute-start.2 = (bf16[2064,128]{1,0:T(8,128)(2,1)S(1)}, bf16[2064,128]{1,0:T(8,128)(2,1)S(1)}, u32[]{:S(2)}, u32[]{:S(2)}) collective-permute-start(bf16[2064,128]{1,0:T(8,128)(2,1)S(1)} %get-tuple-element.57.refs_0_), channel_id=1, source_target_pairs={{0,32},{16,48},{32,0},{48,16},{64,96},{80,112},{1,33},{17,49},{33,... | collective-permute-start | bytes 1585160 | tf_op jit(solution)/shard_map/ppermute | solution.py:308
  69.1 1.9 constant_dynamic-slice_fusion
  70.9 2.0 collective-permute-start.14
  72.9 3.1 collective-permute-start.1
  76.0 1.3 collective-permute-start
  77.4 4.4 %collective-permute-done.10.refs_4_ = bf16[2064,128]{1,0:T(8,128)(2,1)} collective-permute-done((bf16[2064,128]{1,0:T(8,128)(2,1)S(1)}, bf16[2064,128]{1,0:T(8,128)(2,1)}, u32[]{:S(2)}, u32[]{:S(2)}) %collective-permute-start.10) | collective-permute-done | bytes 528416 | tf_op jit(solution)/shard_map/ppermute | solution.py:320
  81.8 2.2 collective-permute-start.13
  84.0 5.7 %collective-permute-done.14.q_ref = bf16[1024,128]{1,0:T(8,128)(2,1)S(1)} collective-permute-done((bf16[1024,128]{1,0:T(8,128)(2,1)}, bf16[1024,128]{1,0:T(8,128)(2,1)S(1)}, u32[]{:S(2)}, u32[]{:S(2)}) %collective-permute-start.14) | collective-permute-done | bytes 262176 | tf_op jit(solution)/shard_map/ppermute | solution.py:321
  89.7 6.2 %collective-permute-start.12 = (bf16[2064,128]{1,0:T(8,128)(2,1)}, bf16[2064,128]{1,0:T(8,128)(2,1)}, u32[]{:S(2)}, u32[]{:S(2)}) collective-permute-start(bf16[2064,128]{1,0:T(8,128)(2,1)} %collective-permute-done.10.refs_4_), channel_id=1, source_target_pairs={{0,48},{64,112},{80,64},{96,80},{112,96},{1,49},{65,113},{81,65},{... | collective-permute-start | bytes 1585160 | tf_op jit(solution)/shard_map/ppermute | solution.py:308
  96.8 1.9 collective-permute-start.11
  98.9 19.3 %collective-permute-done.1.refs_2_ = bf16[2064,128]{1,0:T(8,128)(2,1)S(1)} collective-permute-done((bf16[2064,128]{1,0:T(8,128)(2,1)S(1)}, bf16[2064,128]{1,0:T(8,128)(2,1)S(1)}, u32[]{:S(2)}, u32[]{:S(2)}) %collective-permute-start.1) | collective-permute-done | bytes 528416 | tf_op jit(solution)/shard_map/ppermute | solution.py:308
  118.2 1.3 collective-permute-start.3
  119.5 1.3 collective-permute-start.6
  120.8 1.3 collective-permute-start.5
  122.1 7.4 %collective-permute-done.12.refs_6_ = bf16[2064,128]{1,0:T(8,128)(2,1)} collective-permute-done((bf16[2064,128]{1,0:T(8,128)(2,1)}, bf16[2064,128]{1,0:T(8,128)(2,1)}, u32[]{:S(2)}, u32[]{:S(2)}) %collective-permute-start.12) | collective-permute-done | bytes 528416 | tf_op jit(solution)/shard_map/ppermute | solution.py:308
  129.6 1.3 collective-permute-start.4
  131.8 1.0 copy-done.23
  132.8 1.0 copy-done.26
  133.8 1.0 copy-done.29
  134.9 0.9 copy-done.32
  135.8 5.1 %teacher_attention.3 = bf16[1024,128]{1,0:T(8,128)(2,1)} custom-call(s32[24]{0:T(128)S(1)} %concatenate.29.meta, bf16[1024,128]{1,0:T(8,128)(2,1)S(1)} %copy-done.32, bf16[2064,128]{1,0:T(8,128)(2,1)S(1)} %get-tuple-element.58.refs_0_, bf16[2064,128]{1,0:T(8,128)(2,1)S(1)} %copy-done.29, bf16[2064,128]{1,0:T(8,128)(2,1)S(1)} %copy-done.26, ...), custom_call_target="tpu_custom_call" | custom-call | flops 2147483648 | bytes 5242880 | tf_op jit(solution)/shard_map/teacher_attention/pallas_call | solution.py:107
  140.9 6.4 %collective-permute-start.15 = (bf16[1024,128]{1,0:T(8,128)(2,1)}, bf16[1024,128]{1,0:T(8,128)(2,1)S(1)}, u32[]{:S(2)}, u32[]{:S(2)}) collective-permute-start(bf16[1024,128]{1,0:T(8,128)(2,1)} %teacher_attention.3), channel_id=1, source_target_pairs={{0,64},{16,80},{32,96},{48,112},{64,0},{80,16},{96,32},{112,48},{1... | collective-permute-start | bytes 786440 | tf_op jit(solution)/shard_map/ppermute | solution.py:349
  147.6 10.1 %collective-permute-done.5.refs_6_ = bf16[2064,128]{1,0:T(8,128)(2,1)} collective-permute-done((bf16[2064,128]{1,0:T(8,128)(2,1)S(1)}, bf16[2064,128]{1,0:T(8,128)(2,1)}, u32[]{:S(2)}, u32[]{:S(2)}) %collective-permute-start.5) | collective-permute-done | bytes 528416 | tf_op jit(solution)/shard_map/ppermute | solution.py:326
  157.7 11.3 %collective-permute-done.4.refs_5_ = bf16[2064,128]{1,0:T(8,128)(2,1)} collective-permute-done((bf16[2064,128]{1,0:T(8,128)(2,1)S(1)}, bf16[2064,128]{1,0:T(8,128)(2,1)}, u32[]{:S(2)}, u32[]{:S(2)}) %collective-permute-start.4) | collective-permute-done | bytes 528416 | tf_op jit(solution)/shard_map/ppermute | solution.py:326
  170.1 9.9 %student_forward.1 = (bf16[1024,128]{1,0:T(8,128)(2,1)S(1)}, f32[1024,1024]{1,0:T(8,128)S(1)}) custom-call(s32[24]{0:T(128)S(1)} %concatenate.25.meta, s32[256]{0:T(256)S(1)} %reshape.57.sel, bf16[1024,128]{1,0:T(8,128)(2,1)S(1)} %copy-done.17, s32[16,1,1024]{2,1,0:T(1,128)S(1)} %broadcast_add_fusion.kpos_ref, ...), custom_call_target="tpu_custom_call" | custom-call | flops 536870912 | bytes 9437184 | tf_op jit(solution)/shard_map/student_forward/pallas_call | solution.py:162
  180.0 2.0 copy-done.4
  182.0 7.5 %teacher_attention.2.refs_2_ = bf16[1024,128]{1,0:T(8,128)(2,1)S(1)} custom-call(s32[24]{0:T(128)S(1)} %concatenate.25.meta, bf16[1024,128]{1,0:T(8,128)(2,1)S(1)} %copy-done.21, bf16[2064,128]{1,0:T(8,128)(2,1)S(1)} %copy-done.20, bf16[2064,128]{1,0:T(8,128)(2,1)S(1)} %copy-done.30, bf16[2064,128]{1,0:T(8,128)(2,1)S(1)} %copy-done.27, ...), custom_call_target="tpu_custom_call" | custom-call | flops 2147483648 | bytes 5242880 | tf_op jit(solution)/shard_map/teacher_attention/pallas_call | solution.py:107
  189.5 1.7 copy.15
  191.3 3.6 %project_grad.2 = bf16[8,1024,128]{2,1,0:T(8,128)(2,1)S(1)} custom-call(s32[2]{0:T(128)S(1)} %pad_add_fusion.2.refs_0_, bf16[1024,128]{1,0:T(8,128)(2,1)S(1)} %get-tuple-element.30.refs_1_, bf16[1024,128]{1,0:T(8,128)(2,1)S(1)} %teacher_attention.2.refs_2_, bf16[1024,128]{1,0:T(8,128)(2,1)S(1)} %collective-permute-done.15.refs_3_, bf16[2048,384]{1,0:T(8,128)(2,1)S(1)} %bitcast.19), custom_call_target="tpu_custom_call" | custom-call | flops 805306368 | bytes 4194304 | tf_op jit(solution)/shard_map/project_grad/pallas_call | solution.py:277
  195.5 3.8 %collective-permute-done.16.refs_5_ = bf16[8,1024,128]{2,1,0:T(8,128)(2,1)S(1)} collective-permute-done((bf16[8,1024,128]{2,1,0:T(8,128)(2,1)S(1)}, bf16[8,1024,128]{2,1,0:T(8,128)(2,1)S(1)}, u32[]{:S(2)}, u32[]{:S(2)}) %collective-permute-start.16) | collective-permute-done | bytes 2097184 | tf_op jit(solution)/shard_map/ppermute | solution.py:357
  199.4 3.7 %project_grad.3 = bf16[8,1024,128]{2,1,0:T(8,128)(2,1)S(1)} custom-call(s32[2]{0:T(128)S(1)} %pad_add_fusion.refs_0_, bf16[1024,128]{1,0:T(8,128)(2,1)S(1)} %copy-done.6, bf16[1024,128]{1,0:T(8,128)(2,1)S(1)} %copy-done.9, bf16[1024,128]{1,0:T(8,128)(2,1)S(1)} %collective-permute-done.15.refs_3_, bf16[2048,384]{1,0:T(8,128)(2,1)S(1)} %bitcast.20, ...), custom_call_target="tpu_custom_call" | custom-call | flops 805306368 | bytes 6291456 | tf_op jit(solution)/shard_map/project_grad/pallas_call | solution.py:277
  203.1 1.3 copy-done.1
  204.3 6.9 %project_mismatch.2 = bf16[8,1024,256]{2,1,0:T(8,128)(2,1)} custom-call(s32[2]{0:T(128)S(1)} %pad_add_fusion.2.refs_0_, bf16[1024,128]{1,0:T(8,128)(2,1)S(1)} %copy-done.6, bf16[1024,128]{1,0:T(8,128)(2,1)S(1)} %copy-done.9, bf16[1024,128]{1,0:T(8,128)(2,1)S(1)} %collective-permute-done.15.refs_3_, bf16[384,4096]{1,0:T(8,128)(2,1)S(1)} %pad_maximum_fusion.refs_4_), custom_call_target="tpu_custom_call" | custom-call | flops 1610612736 | bytes 6291456 | tf_op jit(solution)/shard_map/project_mismatch/pallas_call | solution.py:277
  211.4 7.5 %all-to-all-start = ((bf16[8,1024,128]{2,1,0:T(8,128)(2,1)}), bf16[8,1024,128]{2,1,0:T(8,128)(2,1)}, u32[]{:S(2)}, u32[]{:S(2)}) async-start(bf16[8,1024,128]{2,1,0:T(8,128)(2,1)} %copy-done.1), calls=%async_computation | async-start | bytes 4194304 | tf_op jit(solution)/shard_map/all_to_all | solution.py:360
  219.8 0.9 copy-done.10
  220.7 8.0 %project_mismatch.3 = bf16[8,1024,256]{2,1,0:T(8,128)(2,1)S(1)} custom-call(s32[2]{0:T(128)S(1)} %pad_add_fusion.refs_0_, bf16[1024,128]{1,0:T(8,128)(2,1)S(1)} %copy-done.7, bf16[1024,128]{1,0:T(8,128)(2,1)S(1)} %copy-done.10, bf16[1024,128]{1,0:T(8,128)(2,1)S(1)} %collective-permute-done.15.refs_3_, bf16[384,4096]{1,0:T(8,128)(2,1)S(1)} %pad_maximum_fusion.refs_4_, ...), custom_call_target="tpu_custom_call" | custom-call | flops 1610612736 | bytes 10485760 | tf_op jit(solution)/shard_map/project_mismatch/pallas_call | solution.py:277
  228.7 2.0 copy-done
  230.7 14.8 %all-to-all-done.g_ref = bf16[8,1024,128]{2,1,0:T(8,128)(2,1)} async-done(((bf16[8,1024,128]{2,1,0:T(8,128)(2,1)}), bf16[8,1024,128]{2,1,0:T(8,128)(2,1)}, u32[]{:S(2)}, u32[]{:S(2)}) %all-to-all-start) | async-done | bytes 2097184 | tf_op jit(solution)/shard_map/all_to_all | solution.py:360
  245.5 7.2 %all-to-all-start.1 = ((bf16[8,1024,256]{2,1,0:T(8,128)(2,1)}), bf16[8,1024,256]{2,1,0:T(8,128)(2,1)}, u32[]{:S(2)}, u32[]{:S(2)}) async-start(bf16[8,1024,256]{2,1,0:T(8,128)(2,1)} %copy-done), calls=%async_computation.1 | async-start | bytes 8388608 | tf_op jit(solution)/shard_map/all_to_all | solution.py:366
  252.7 17.5 %student_backward.1 = (f32[1024,128]{1,0:T(8,128)}, bf16[2048,128]{1,0:T(8,128)(2,1)S(1)}, bf16[2048,128]{1,0:T(8,128)(2,1)S(1)}, bf16[2048,128]{1,0:T(8,128)(2,...) custom-call(s32[24]{0:T(128)S(1)} %concatenate.25.meta, ...), custom_call_target="tpu_custom_call" | custom-call | flops 1073741824 | bytes 15728640 | tf_op jit(solution)/shard_map/student_backward/pallas_call | solution.py:225
  270.2 13.6 %collective-permute-start.18 = (bf16[2048,128]{1,0:T(8,128)(2,1)S(1)}, bf16[2048,128]{1,0:T(8,128)(2,1)S(1)}, u32[]{:S(2)}, u32[]{:S(2)}) collective-permute-start(bf16[2048,128]{1,0:T(8,128)(2,1)S(1)} %get-tuple-element.39), channel_id=1, source_target_pairs={{16,0},{32,16},{48,32},{64,112},{80,64},{96,80},{112,96},{17,1},{3... | collective-permute-start | bytes 1572872 | tf_op jit(solution)/shard_map/ppermute | solution.py:383
  283.8 1.9 collective-permute-start.19
  285.8 3.4 collective-permute-start.20
  289.1 1.3 collective-permute-start.22
  290.4 1.3 collective-permute-start.23
  291.7 13.9 %collective-permute-done.18 = bf16[2048,128]{1,0:T(8,128)(2,1)S(1)} collective-permute-done((bf16[2048,128]{1,0:T(8,128)(2,1)S(1)}, bf16[2048,128]{1,0:T(8,128)(2,1)S(1)}, u32[]{:S(2)}, u32[]{:S(2)}) %collective-permute-start.18) | collective-permute-done | bytes 524320 | tf_op jit(solution)/shard_map/ppermute | solution.py:383
  305.6 1.3 collective-permute-start.24
  306.9 17.3 %collective-permute-done.19 = bf16[2048,128]{1,0:T(8,128)(2,1)S(1)} collective-permute-done((bf16[2048,128]{1,0:T(8,128)(2,1)S(1)}, bf16[2048,128]{1,0:T(8,128)(2,1)S(1)}, u32[]{:S(2)}, u32[]{:S(2)}) %collective-permute-start.19) | collective-permute-done | bytes 524320 | tf_op jit(solution)/shard_map/ppermute | solution.py:383
  324.3 1.1 fusion.4
  325.4 2.1 collective-permute-start.21
  327.5 6.0 %collective-permute-done.23 = bf16[2048,128]{1,0:T(8,128)(2,1)} collective-permute-done((bf16[2048,128]{1,0:T(8,128)(2,1)}, bf16[2048,128]{1,0:T(8,128)(2,1)}, u32[]{:S(2)}, u32[]{:S(2)}) %collective-permute-start.23) | collective-permute-done | bytes 524320 | tf_op jit(solution)/shard_map/ppermute | solution.py:385
  333.7 2.0 add_select_fusion
  335.6 1.0 fusion.5
  336.7 3.8 %convert_reduce_fusion = f32[1024,256]{1,0:T(8,128)} fusion(bf16[8,1024,256]{2,1,0:T(8,128)(2,1)} %all-to-all-done.1), kind=kLoop, calls=%fused_computation | loop fusion | flops 3932160 | bytes 5242880 | tf_op jit(solution)/shard_map/reduce_sum | solution.py:389
  (110 shorter events, 6.1 us)
Async XLA Ops:
  7.2 3.8 %copy-start.36 = (bf16[1024,128]{1,0:T(8,128)(2,1)S(1)}, bf16[1024,128]{1,0:T(8,128)(2,1)}, u32[]{:S(2)}) copy-start(bf16[1024,128]{1,0:T(8,128)(2,1)} %param.16) | copy-start | bytes 786436
  7.2 3.8 %copy-start.37 = (bf16[1024,128]{1,0:T(8,128)(2,1)S(1)}, bf16[1024,128]{1,0:T(8,128)(2,1)}, u32[]{:S(2)}) copy-start(bf16[1024,128]{1,0:T(8,128)(2,1)} %param.15) | copy-start | bytes 786436
  7.2 52.4 %all-gather.3.cloned.1.call-start = ((), (), s32[]{:S(2)}) async-start(), calls=%async_computation.2 | async-start | bytes 2228224 | tf_op jit(solution)/shard_map/all_gather | solution.py:330
  8.9 180.6 %all-gather.5.cloned.1.call-start = ((), (), s32[]{:S(2)}) async-start(), calls=%async_computation.3 | async-start | bytes 1769472 | tf_op jit(solution)/shard_map/all_gather | solution.py:333
  10.9 8.9 %copy-start.34 = (bf16[256,4096]{1,0:T(8,128)(2,1)S(1)}, bf16[256,4096]{1,0:T(8,128)(2,1)}, u32[]{:S(2)}) copy-start(bf16[256,4096]{1,0:T(8,128)(2,1)} %param.13) | copy-start | bytes 6291460
  11.1 120.7 %copy-start.19 = (bf16[2064,128]{1,0:T(8,128)(2,1)}, bf16[2064,128]{1,0:T(8,128)(2,1)S(1)}, u32[]{:S(2)}) copy-start(bf16[2064,128]{1,0:T(8,128)(2,1)S(1)} %get-tuple-element.58.refs_0_) | copy-start | bytes 1585156
  11.1 158.0 %copy-start.2 = (bf16[2064,128]{1,0:T(8,128)(2,1)}, bf16[2064,128]{1,0:T(8,128)(2,1)S(1)}, u32[]{:S(2)}) copy-start(bf16[2064,128]{1,0:T(8,128)(2,1)S(1)} %get-tuple-element.57.refs_0_) | copy-start | bytes 1585156
  11.1 17.8 %collective-permute-start.9 = (bf16[2064,128]{1,0:T(8,128)(2,1)S(1)}, bf16[2064,128]{1,0:T(8,128)(2,1)S(1)}, u32[]{:S(2)}, u32[]{:S(2)}) collective-permute-start(bf16[2064,128]{1,0:T(8,128)(2,1)S(1)} %get-tuple-element.58.refs_0_), channel_id=1, source_target_pairs={{0,32},{16,48},{32,0},{48,16},{64,96},{80,112},{1,33},{17,49},{33,... | collective-permute-start | bytes 1585160 | tf_op jit(solution)/shard_map/ppermute | solution.py:308
  16.5 22.7 %collective-permute-start.8 = (bf16[2064,128]{1,0:T(8,128)(2,1)S(1)}, bf16[2064,128]{1,0:T(8,128)(2,1)S(1)}, u32[]{:S(2)}, u32[]{:S(2)}) collective-permute-start(bf16[2064,128]{1,0:T(8,128)(2,1)S(1)} %get-tuple-element.58.refs_0_), channel_id=1, source_target_pairs={{0,48},{16,0},{32,16},{48,32},{64,112},{1,49},{17,1},{33,17},{49,3... | collective-permute-start | bytes 1585160 | tf_op jit(solution)/shard_map/ppermute | solution.py:308
  17.8 21.3 %collective-permute-start.7 = (bf16[2064,128]{1,0:T(8,128)(2,1)S(1)}, bf16[2064,128]{1,0:T(8,128)(2,1)S(1)}, u32[]{:S(2)}, u32[]{:S(2)}) collective-permute-start(bf16[2064,128]{1,0:T(8,128)(2,1)S(1)} %get-tuple-element.58.refs_0_), channel_id=1, source_target_pairs={{0,16},{16,32},{32,48},{48,0},{64,80},{80,96},{96,112},{1,17},{17,... | collective-permute-start | bytes 1585160 | tf_op jit(solution)/shard_map/ppermute | solution.py:308
  21.6 74.3 %copy-start.38 = (s32[16,16]{1,0:T(8,128)S(1)}, s32[16,16]{1,0:T(8,128)}, u32[]{:S(2)}) copy-start(s32[16,16]{1,0:T(8,128)} %param.19) | copy-start | bytes 3076
  28.9 35.1 %copy-start.22 = (bf16[2064,128]{1,0:T(8,128)(2,1)}, bf16[2064,128]{1,0:T(8,128)(2,1)S(1)}, u32[]{:S(2)}) copy-start(bf16[2064,128]{1,0:T(8,128)(2,1)S(1)} %collective-permute-done.9.refs_3_) | copy-start | bytes 1585156
  39.1 24.9 %copy-start.25 = (bf16[2064,128]{1,0:T(8,128)(2,1)}, bf16[2064,128]{1,0:T(8,128)(2,1)S(1)}, u32[]{:S(2)}) copy-start(bf16[2064,128]{1,0:T(8,128)(2,1)S(1)} %collective-permute-done.8.refs_2_) | copy-start | bytes 1585156
  39.1 24.9 %copy-start.28 = (bf16[2064,128]{1,0:T(8,128)(2,1)}, bf16[2064,128]{1,0:T(8,128)(2,1)S(1)}, u32[]{:S(2)}) copy-start(bf16[2064,128]{1,0:T(8,128)(2,1)S(1)} %collective-permute-done.7.refs_1_) | copy-start | bytes 1585156
  64.0 17.8 %collective-permute-start.10 = (bf16[2064,128]{1,0:T(8,128)(2,1)S(1)}, bf16[2064,128]{1,0:T(8,128)(2,1)}, u32[]{:S(2)}, u32[]{:S(2)}) collective-permute-start(bf16[2064,128]{1,0:T(8,128)(2,1)S(1)} %get-tuple-element.56), channel_id=1, source_target_pairs={{0,64},{16,80},{32,96},{48,112},{64,0},{80,16},{96,32},{112,48},{1... | collective-permute-start | bytes 1585160 | tf_op jit(solution)/shard_map/ppermute | solution.py:320
  64.1 32.7 %collective-permute-start.2 = (bf16[2064,128]{1,0:T(8,128)(2,1)S(1)}, bf16[2064,128]{1,0:T(8,128)(2,1)S(1)}, u32[]{:S(2)}, u32[]{:S(2)}) collective-permute-start(bf16[2064,128]{1,0:T(8,128)(2,1)S(1)} %get-tuple-element.57.refs_0_), channel_id=1, source_target_pairs={{0,32},{16,48},{32,0},{48,16},{64,96},{80,112},{1,33},{17,49},{33,... | collective-permute-start | bytes 1585160 | tf_op jit(solution)/shard_map/ppermute | solution.py:308
  70.9 18.7 %collective-permute-start.14 = (bf16[1024,128]{1,0:T(8,128)(2,1)}, bf16[1024,128]{1,0:T(8,128)(2,1)S(1)}, u32[]{:S(2)}, u32[]{:S(2)}) collective-permute-start(bf16[1024,128]{1,0:T(8,128)(2,1)} %get-tuple-element.50), channel_id=1, source_target_pairs={{0,64},{16,80},{32,96},{48,112},{64,0},{80,16},{96,32},{112,48},{1... | collective-permute-start | bytes 786440 | tf_op jit(solution)/shard_map/ppermute | solution.py:321
  72.9 45.3 %collective-permute-start.1 = (bf16[2064,128]{1,0:T(8,128)(2,1)S(1)}, bf16[2064,128]{1,0:T(8,128)(2,1)S(1)}, u32[]{:S(2)}, u32[]{:S(2)}) collective-permute-start(bf16[2064,128]{1,0:T(8,128)(2,1)S(1)} %get-tuple-element.57.refs_0_), channel_id=1, source_target_pairs={{0,48},{16,0},{32,16},{48,32},{64,112},{1,49},{17,1},{33,17},{49,3... | collective-permute-start | bytes 1585160 | tf_op jit(solution)/shard_map/ppermute | solution.py:308
  76.0 43.5 %collective-permute-start = (bf16[2064,128]{1,0:T(8,128)(2,1)S(1)}, bf16[2064,128]{1,0:T(8,128)(2,1)S(1)}, u32[]{:S(2)}, u32[]{:S(2)}) collective-permute-start(bf16[2064,128]{1,0:T(8,128)(2,1)S(1)} %get-tuple-element.57.refs_0_), channel_id=1, source_target_pairs={{0,16},{16,32},{32,48},{48,0},{64,80},{80,96},{96,112},{1,17},{17,... | collective-permute-start | bytes 1585160 | tf_op jit(solution)/shard_map/ppermute | solution.py:308
  81.8 39.0 %collective-permute-start.13 = (bf16[2064,128]{1,0:T(8,128)(2,1)}, bf16[2064,128]{1,0:T(8,128)(2,1)}, u32[]{:S(2)}, u32[]{:S(2)}) collective-permute-start(bf16[2064,128]{1,0:T(8,128)(2,1)} %collective-permute-done.10.refs_4_), channel_id=1, source_target_pairs={{0,32},{16,48},{64,96},{80,112},{96,64},{112,80},{1,33},{17,49},{6... | collective-permute-start | bytes 1585160 | tf_op jit(solution)/shard_map/ppermute | solution.py:308
  89.7 9.1 %copy-start.31 = (bf16[1024,128]{1,0:T(8,128)(2,1)}, bf16[1024,128]{1,0:T(8,128)(2,1)S(1)}, u32[]{:S(2)}) copy-start(bf16[1024,128]{1,0:T(8,128)(2,1)S(1)} %collective-permute-done.14.q_ref) | copy-start | bytes 786436
  89.7 39.9 %collective-permute-start.12 = (bf16[2064,128]{1,0:T(8,128)(2,1)}, bf16[2064,128]{1,0:T(8,128)(2,1)}, u32[]{:S(2)}, u32[]{:S(2)}) collective-permute-start(bf16[2064,128]{1,0:T(8,128)(2,1)} %collective-permute-done.10.refs_4_), channel_id=1, source_target_pairs={{0,48},{64,112},{80,64},{96,80},{112,96},{1,49},{65,113},{81,65},{... | collective-permute-start | bytes 1585160 | tf_op jit(solution)/shard_map/ppermute | solution.py:308
  96.8 72.3 %copy-start.11 = (bf16[2064,128]{1,0:T(8,128)(2,1)}, bf16[2064,128]{1,0:T(8,128)(2,1)S(1)}, u32[]{:S(2)}) copy-start(bf16[2064,128]{1,0:T(8,128)(2,1)S(1)} %collective-permute-done.2.refs_3_) | copy-start | bytes 1585156
  96.8 35.0 %collective-permute-start.11 = (bf16[2064,128]{1,0:T(8,128)(2,1)}, bf16[2064,128]{1,0:T(8,128)(2,1)}, u32[]{:S(2)}, u32[]{:S(2)}) collective-permute-start(bf16[2064,128]{1,0:T(8,128)(2,1)} %collective-permute-done.10.refs_4_), channel_id=1, source_target_pairs={{0,16},{16,32},{32,48},{64,80},{80,96},{96,112},{112,64},{1,17},{1... | collective-permute-start | bytes 1585160 | tf_op jit(solution)/shard_map/ppermute | solution.py:308
  118.2 50.9 %copy-start.12 = (bf16[2064,128]{1,0:T(8,128)(2,1)}, bf16[2064,128]{1,0:T(8,128)(2,1)S(1)}, u32[]{:S(2)}) copy-start(bf16[2064,128]{1,0:T(8,128)(2,1)S(1)} %collective-permute-done.1.refs_2_) | copy-start | bytes 1585156
  118.2 29.4 %collective-permute-start.3 = (bf16[2064,128]{1,0:T(8,128)(2,1)S(1)}, bf16[2064,128]{1,0:T(8,128)(2,1)S(1)}, u32[]{:S(2)}, u32[]{:S(2)}) collective-permute-start(bf16[2064,128]{1,0:T(8,128)(2,1)S(1)} %get-tuple-element.57.refs_0_), channel_id=1, source_target_pairs={{0,64},{16,80},{32,96},{48,112},{1,65},{17,81},{33,97},{49,113},{2... | collective-permute-start | bytes 1585160 | tf_op jit(solution)/shard_map/ppermute | solution.py:326
  119.5 49.6 %copy-start.14 = (bf16[2064,128]{1,0:T(8,128)(2,1)}, bf16[2064,128]{1,0:T(8,128)(2,1)S(1)}, u32[]{:S(2)}) copy-start(bf16[2064,128]{1,0:T(8,128)(2,1)S(1)} %collective-permute-done.refs_1_) | copy-start | bytes 1585156
  119.5 28.1 %collective-permute-start.6 = (bf16[2064,128]{1,0:T(8,128)(2,1)S(1)}, bf16[2064,128]{1,0:T(8,128)(2,1)}, u32[]{:S(2)}, u32[]{:S(2)}) collective-permute-start(bf16[2064,128]{1,0:T(8,128)(2,1)S(1)} %collective-permute-done.2.refs_3_), channel_id=1, source_target_pairs={{0,64},{16,80},{32,96},{48,112},{1,65},{17,81},{33,97},{49,113},{2... | collective-permute-start | bytes 1585160 | tf_op jit(solution)/shard_map/ppermute | solution.py:326
  120.8 36.9 %collective-permute-start.5 = (bf16[2064,128]{1,0:T(8,128)(2,1)S(1)}, bf16[2064,128]{1,0:T(8,128)(2,1)}, u32[]{:S(2)}, u32[]{:S(2)}) collective-permute-start(bf16[2064,128]{1,0:T(8,128)(2,1)S(1)} %collective-permute-done.1.refs_2_), channel_id=1, source_target_pairs={{0,64},{16,80},{32,96},{48,112},{1,65},{17,81},{33,97},{49,113},{2... | collective-permute-start | bytes 1585160 | tf_op jit(solution)/shard_map/ppermute | solution.py:326
  129.6 39.5 %collective-permute-start.4 = (bf16[2064,128]{1,0:T(8,128)(2,1)S(1)}, bf16[2064,128]{1,0:T(8,128)(2,1)}, u32[]{:S(2)}, u32[]{:S(2)}) collective-permute-start(bf16[2064,128]{1,0:T(8,128)(2,1)S(1)} %collective-permute-done.refs_1_), channel_id=1, source_target_pairs={{0,64},{16,80},{32,96},{48,112},{1,65},{17,81},{33,97},{49,113},{2... | collective-permute-start | bytes 1585160 | tf_op jit(solution)/shard_map/ppermute | solution.py:326
  131.8 1.0 copy-start.23
  132.8 1.0 copy-start.26
  133.8 1.0 copy-start.29
  140.9 50.4 %collective-permute-start.15 = (bf16[1024,128]{1,0:T(8,128)(2,1)}, bf16[1024,128]{1,0:T(8,128)(2,1)S(1)}, u32[]{:S(2)}, u32[]{:S(2)}) collective-permute-start(bf16[1024,128]{1,0:T(8,128)(2,1)} %teacher_attention.3), channel_id=1, source_target_pairs={{0,64},{16,80},{32,96},{48,112},{64,0},{80,16},{96,32},{112,48},{1... | collective-permute-start | bytes 786440 | tf_op jit(solution)/shard_map/ppermute | solution.py:349
  147.6 32.4 %copy-start.16 = (bf16[2064,128]{1,0:T(8,128)(2,1)}, bf16[2064,128]{1,0:T(8,128)(2,1)S(1)}, u32[]{:S(2)}) copy-start(bf16[2064,128]{1,0:T(8,128)(2,1)S(1)} %collective-permute-done.3.refs_4_) | copy-start | bytes 1585156
  170.0 11.9 %copy-start.20 = (bf16[2064,128]{1,0:T(8,128)(2,1)S(1)}, bf16[2064,128]{1,0:T(8,128)(2,1)}, u32[]{:S(2)}) copy-start(bf16[2064,128]{1,0:T(8,128)(2,1)} %copy-done.19) | copy-start | bytes 1585156
  170.0 11.9 %copy-start.21 = (bf16[1024,128]{1,0:T(8,128)(2,1)S(1)}, bf16[1024,128]{1,0:T(8,128)(2,1)}, u32[]{:S(2)}) copy-start(bf16[1024,128]{1,0:T(8,128)(2,1)} %get-tuple-element.51.q_ref) | copy-start | bytes 786436
  170.0 11.9 %copy-start.24 = (bf16[2064,128]{1,0:T(8,128)(2,1)S(1)}, bf16[2064,128]{1,0:T(8,128)(2,1)}, u32[]{:S(2)}) copy-start(bf16[2064,128]{1,0:T(8,128)(2,1)} %copy-done.22) | copy-start | bytes 1585156
  170.0 11.9 %copy-start.27 = (bf16[2064,128]{1,0:T(8,128)(2,1)S(1)}, bf16[2064,128]{1,0:T(8,128)(2,1)}, u32[]{:S(2)}) copy-start(bf16[2064,128]{1,0:T(8,128)(2,1)} %copy-done.25) | copy-start | bytes 1585156
  170.1 11.9 %copy-start.30 = (bf16[2064,128]{1,0:T(8,128)(2,1)S(1)}, bf16[2064,128]{1,0:T(8,128)(2,1)}, u32[]{:S(2)}) copy-start(bf16[2064,128]{1,0:T(8,128)(2,1)} %copy-done.28) | copy-start | bytes 1585156
  180.0 2.0 copy-start.4
  181.9 9.3 %copy-start.5 = (bf16[1024,128]{1,0:T(8,128)(2,1)}, bf16[1024,128]{1,0:T(8,128)(2,1)S(1)}, u32[]{:S(2)}) copy-start(bf16[1024,128]{1,0:T(8,128)(2,1)S(1)} %get-tuple-element.30.refs_1_) | copy-start | bytes 786436
  189.5 5.5 %copy-start.8 = (bf16[1024,128]{1,0:T(8,128)(2,1)}, bf16[1024,128]{1,0:T(8,128)(2,1)S(1)}, u32[]{:S(2)}) copy-start(bf16[1024,128]{1,0:T(8,128)(2,1)S(1)} %teacher_attention.2.refs_2_) | copy-start | bytes 786436
  191.3 4.0 %copy-start.33 = (bf16[256,4096]{1,0:T(8,128)(2,1)S(1)}, bf16[256,4096]{1,0:T(8,128)(2,1)}, u32[]{:S(2)}) copy-start(bf16[256,4096]{1,0:T(8,128)(2,1)} %neg.3) | copy-start | bytes 6291460
  191.3 4.0 %copy-start.35 = (bf16[128,4096]{1,0:T(8,128)(2,1)S(1)}, bf16[128,4096]{1,0:T(8,128)(2,1)}, u32[]{:S(2)}) copy-start(bf16[128,4096]{1,0:T(8,128)(2,1)} %param.17) | copy-start | bytes 3145732
  195.0 4.4 %collective-permute-start.16 = (bf16[8,1024,128]{2,1,0:T(8,128)(2,1)S(1)}, bf16[8,1024,128]{2,1,0:T(8,128)(2,1)S(1)}, u32[]{:S(2)}, u32[]{:S(2)}) collective-permute-start(bf16[8,1024,128]{2,1,0:T(8,128)(2,1)S(1)} %project_grad.2), channel_id=1, source_target_pairs={{0,2},{2,0},{1,3},{3,1},{4,6},{6,4},{5,7},{7,5},{8,10},{10,8},{9,1... | collective-permute-start | bytes 6291464 | tf_op jit(solution)/shard_map/ppermute | solution.py:357
  195.3 4.1 %copy-start.6 = (bf16[1024,128]{1,0:T(8,128)(2,1)S(1)}, bf16[1024,128]{1,0:T(8,128)(2,1)}, u32[]{:S(2)}) copy-start(bf16[1024,128]{1,0:T(8,128)(2,1)} %copy-done.5) | copy-start | bytes 786436
  195.3 4.1 %copy-start.9 = (bf16[1024,128]{1,0:T(8,128)(2,1)S(1)}, bf16[1024,128]{1,0:T(8,128)(2,1)}, u32[]{:S(2)}) copy-start(bf16[1024,128]{1,0:T(8,128)(2,1)} %copy-done.8) | copy-start | bytes 786436
  203.0 1.3 copy-start.1
  211.2 7.6 %collective-permute-start.17 = (bf16[8,1024,256]{2,1,0:T(8,128)(2,1)}, bf16[8,1024,256]{2,1,0:T(8,128)(2,1)}, u32[]{:S(2)}, u32[]{:S(2)}) collective-permute-start(bf16[8,1024,256]{2,1,0:T(8,128)(2,1)} %project_mismatch.2), channel_id=1, source_target_pairs={{0,2},{2,0},{1,3},{3,1},{4,6},{6,4},{5,7},{7,5},{8,10},{10,8},{9,1... | collective-permute-start | bytes 12582920 | tf_op jit(solution)/shard_map/ppermute | solution.py:363
  211.4 34.2 %all-to-all-start = ((bf16[8,1024,128]{2,1,0:T(8,128)(2,1)}), bf16[8,1024,128]{2,1,0:T(8,128)(2,1)}, u32[]{:S(2)}, u32[]{:S(2)}) async-start(bf16[8,1024,128]{2,1,0:T(8,128)(2,1)} %copy-done.1), calls=%async_computation | async-start | bytes 4194304 | tf_op jit(solution)/shard_map/all_to_all | solution.py:360
  228.7 2.0 copy-start
  230.7 22.0 %copy-start.3 = (bf16[2064,128]{1,0:T(8,128)(2,1)S(1)}, bf16[2064,128]{1,0:T(8,128)(2,1)}, u32[]{:S(2)}) copy-start(bf16[2064,128]{1,0:T(8,128)(2,1)} %copy-done.2) | copy-start | bytes 1585156
  230.7 22.0 %copy-start.13 = (bf16[2064,128]{1,0:T(8,128)(2,1)S(1)}, bf16[2064,128]{1,0:T(8,128)(2,1)}, u32[]{:S(2)}) copy-start(bf16[2064,128]{1,0:T(8,128)(2,1)} %copy-done.12) | copy-start | bytes 1585156
  230.7 22.0 %copy-start.15 = (bf16[2064,128]{1,0:T(8,128)(2,1)S(1)}, bf16[2064,128]{1,0:T(8,128)(2,1)}, u32[]{:S(2)}) copy-start(bf16[2064,128]{1,0:T(8,128)(2,1)} %copy-done.14) | copy-start | bytes 1585156
  230.7 22.0 %copy-start.18 = (bf16[1024,128]{1,0:T(8,128)(2,1)S(1)}, bf16[1024,128]{1,0:T(8,128)(2,1)}, u32[]{:S(2)}) copy-start(bf16[1024,128]{1,0:T(8,128)(2,1)} %q_ref.3) | copy-start | bytes 786436
  245.5 91.2 %all-to-all-start.1 = ((bf16[8,1024,256]{2,1,0:T(8,128)(2,1)}), bf16[8,1024,256]{2,1,0:T(8,128)(2,1)}, u32[]{:S(2)}, u32[]{:S(2)}) async-start(bf16[8,1024,256]{2,1,0:T(8,128)(2,1)} %copy-done), calls=%async_computation.1 | async-start | bytes 8388608 | tf_op jit(solution)/shard_map/all_to_all | solution.py:366
  270.2 35.4 %collective-permute-start.18 = (bf16[2048,128]{1,0:T(8,128)(2,1)S(1)}, bf16[2048,128]{1,0:T(8,128)(2,1)S(1)}, u32[]{:S(2)}, u32[]{:S(2)}) collective-permute-start(bf16[2048,128]{1,0:T(8,128)(2,1)S(1)} %get-tuple-element.39), channel_id=1, source_target_pairs={{16,0},{32,16},{48,32},{64,112},{80,64},{96,80},{112,96},{17,1},{3... | collective-permute-start | bytes 1572872 | tf_op jit(solution)/shard_map/ppermute | solution.py:383
  283.8 40.4 %collective-permute-start.19 = (bf16[2048,128]{1,0:T(8,128)(2,1)S(1)}, bf16[2048,128]{1,0:T(8,128)(2,1)S(1)}, u32[]{:S(2)}, u32[]{:S(2)}) collective-permute-start(bf16[2048,128]{1,0:T(8,128)(2,1)S(1)} %get-tuple-element.40), channel_id=1, source_target_pairs={{48,0},{64,80},{80,96},{96,112},{112,64},{49,1},{65,81},{81,97},{9... | collective-permute-start | bytes 1572872 | tf_op jit(solution)/shard_map/ppermute | solution.py:383
  285.8 38.5 %collective-permute-start.20 = (bf16[2048,128]{1,0:T(8,128)(2,1)S(1)}, bf16[2048,128]{1,0:T(8,128)(2,1)S(1)}, u32[]{:S(2)}, u32[]{:S(2)}) collective-permute-start(bf16[2048,128]{1,0:T(8,128)(2,1)S(1)} %get-tuple-element.41), channel_id=1, source_target_pairs={{32,0},{48,16},{64,96},{80,112},{96,64},{112,80},{33,1},{49,17},{6... | collective-permute-start | bytes 1572872 | tf_op jit(solution)/shard_map/ppermute | solution.py:383
  289.1 38.4 %collective-permute-start.22 = (bf16[2048,128]{1,0:T(8,128)(2,1)}, bf16[2048,128]{1,0:T(8,128)(2,1)S(1)}, u32[]{:S(2)}, u32[]{:S(2)}) collective-permute-start(bf16[2048,128]{1,0:T(8,128)(2,1)} %get-tuple-element.43), channel_id=1, source_target_pairs={{80,64},{96,80},{112,96},{81,65},{97,81},{113,97},{82,66},{98,82},... | collective-permute-start | bytes 1572872 | tf_op jit(solution)/shard_map/ppermute | solution.py:385
  290.4 43.1 %collective-permute-start.23 = (bf16[2048,128]{1,0:T(8,128)(2,1)}, bf16[2048,128]{1,0:T(8,128)(2,1)}, u32[]{:S(2)}, u32[]{:S(2)}) collective-permute-start(bf16[2048,128]{1,0:T(8,128)(2,1)} %get-tuple-element.44), channel_id=1, source_target_pairs={{112,64},{113,65},{114,66},{115,67},{116,68},{117,69},{118,70},{11... | collective-permute-start | bytes 1572872 | tf_op jit(solution)/shard_map/ppermute | solution.py:385
  305.6 27.9 %collective-permute-start.24 = (bf16[2048,128]{1,0:T(8,128)(2,1)}, bf16[2048,128]{1,0:T(8,128)(2,1)}, u32[]{:S(2)}, u32[]{:S(2)}) collective-permute-start(bf16[2048,128]{1,0:T(8,128)(2,1)} %get-tuple-element.45), channel_id=1, source_target_pairs={{96,64},{112,80},{97,65},{113,81},{98,66},{114,82},{99,67},{115,83... | collective-permute-start | bytes 1572872 | tf_op jit(solution)/shard_map/ppermute | solution.py:385
  325.4 8.3 %collective-permute-start.21 = (bf16[2048,128]{1,0:T(8,128)(2,1)}, bf16[2048,128]{1,0:T(8,128)(2,1)}, u32[]{:S(2)}, u32[]{:S(2)}) collective-permute-start(bf16[2048,128]{1,0:T(8,128)(2,1)} %fusion.4), channel_id=1, source_target_pairs={{64,0},{80,16},{96,32},{112,48},{65,1},{81,17},{97,33},{113,49},{6... | collective-permute-start | bytes 1572872 | tf_op jit(solution)/shard_map/ppermute | solution.py:386
  (4 other events, 3.8 us)
Sparse Core Ops, SparseCore 0:
  11.1 48.4 all-gather.2
  64.1 54.5 all-gather.4

commit v2 on v1

v2 whole, which is shorter than its diff:
```python
import jax
import jax.numpy as jnp
from jax import lax
from jax.experimental import pallas as pl
from jax.experimental.pallas import tpu as pltpu
from jax.sharding import Mesh
from jax.sharding import PartitionSpec as P

HD = 128
BS = 64
NSEL = 16
BLOCK = 1024
COUNTS = 16
FORWARD_ROWS = 4
BACKWARD_ROWS = 4
TILE_Q = 512
TILE_K = 512
SCALE = HD ** (-0.5)
EXP_SCALE = SCALE * 1.4426950408889634
LOWEST = -1e30

BLK = ("xlo", "y")
GROUP = ("z", "core", "xhi")
ZX = ("z", "xhi")
f32 = jnp.float32
bf16 = jnp.bfloat16

SMEM = pltpu.SMEM
ANY = pl.BlockSpec(memory_space=pl.ANY)
FAR = pl.BlockSpec(memory_space=pltpu.HBM)

VMEM = pl.BlockSpec(memory_space=pltpu.VMEM)
ROWS_NT = (((1,), (1,)), ((), ()))
ROWS_TN = (((0,), (0,)), ((), ()))


def y_pairs(shift, all_x, causal_x):
    pairs = []
    for x in range(2):
        for y in range(4):
            to = (y + shift) % 4
            if x in all_x or (x in causal_x and y < to):
                pairs.append((4 * x + y, 4 * x + to))
    return pairs


def far(array):
    return pltpu.with_memory_space_constraint(array, pltpu.HBM)


SPAN = 2 * BLOCK + COUNTS


def blocks_of(refs):
    return [(ref, k * SPAN) for ref in refs for k in range(ref.shape[0] // SPAN)]


def load(blocks, key_all, value_all, counts, sems):
    copies = []

    def bring(source, target):
        copy = pltpu.make_async_copy(source, target, sems.at[len(copies)])
        copy.start()
        copies.append(copy)

    for j, (ref, at) in enumerate(blocks):
        slot = pl.ds(j * BLOCK, BLOCK)
        bring(ref.at[pl.ds(at, BLOCK)], key_all.at[slot])
        bring(ref.at[pl.ds(at + BLOCK, BLOCK)], value_all.at[slot])
        if counts is not None:
            bring(ref.at[pl.ds(at + 2 * BLOCK, COUNTS)], counts.at[pl.ds(j * COUNTS, COUNTS)])
    for copy in copies:
        copy.wait()


def border_of(counts):
    return jnp.sum(counts[...].astype(f32)).astype(jnp.int32)


KEYS = [pltpu.VMEM((8 * BLOCK, HD), bf16)] * 2
WITH_COUNTS = KEYS + [pltpu.VMEM((8 * COUNTS, HD), bf16), pltpu.SemaphoreType.DMA((24,))]


def teacher_kernel(meta, away_ref, here_ref, *refs):
    blocks = blocks_of(refs[:-6])
    away_out, here_out, key_all, value_all, counts, sems = refs[-6:]
    load(blocks, key_all, value_all, counts, sems)
    border = border_of(counts)
    per_block = BLOCK // TILE_K

    def one_tile(q_ref, o_ref, block, step):
        first = block * BLOCK + step * TILE_Q
        low_first = jnp.where(first >= border, border, 0)
        low_last = jnp.where(first + TILE_Q - 1 >= border, border, 0)
        span = pl.ds(step * TILE_Q, TILE_Q)
        queries = q_ref[span, :]
        q_pos = first + lax.broadcasted_iota(jnp.int32, (TILE_Q, 1), 0)
        q_low = jnp.where(q_pos >= border, border, 0)

        def turn(masked, j, carry):
            largest, total, acc = carry
            slot = meta[8 + j // per_block]
            start = pl.multiple_of(slot * BLOCK + (j % per_block) * TILE_K, TILE_K)
            scores = lax.dot_general(
                queries, key_all[pl.ds(start, TILE_K), :], ROWS_NT, preferred_element_type=f32
            )
            if masked:
                k_pos = j * TILE_K + lax.broadcasted_iota(jnp.int32, (1, TILE_K), 1)
                scores = jnp.where((k_pos <= q_pos) & (k_pos >= q_low), scores, LOWEST)
            new = jnp.maximum(largest, jnp.max(scores, axis=1, keepdims=True))
            factor = jnp.exp2((largest - new) * EXP_SCALE)
            weights = jnp.exp2((scores - new) * EXP_SCALE)
            total = factor * total + jnp.sum(weights, axis=1, keepdims=True)
            acc = factor * acc + jnp.dot(
                weights.astype(bf16), value_all[pl.ds(start, TILE_K), :], preferred_element_type=f32
            )
            return new, total, acc

        carry = (
            jnp.full((TILE_Q, 1), LOWEST, f32),
            jnp.zeros((TILE_Q, 1), f32),
            jnp.zeros((TILE_Q, HD), f32),
        )
        begin = low_first // TILE_K
        diagonal = first // TILE_K
        clear = jnp.minimum((low_last + TILE_K - 1) // TILE_K, diagonal)
        carry = lax.fori_loop(begin, clear, lambda j, c: turn(True, j, c), carry)
        carry = lax.fori_loop(clear, diagonal, lambda j, c: turn(False, j, c), carry)
        for j in range(max(TILE_Q // TILE_K, 1)):
            carry = turn(True, diagonal + j, carry)
        _, total, acc = carry
        o_ref[span, :] = (acc / total).astype(bf16)

    for step in range(BLOCK // TILE_Q):
        one_tile(away_ref, away_out, meta[1], step)
    for step in range(BLOCK // TILE_Q):
        one_tile(here_ref, here_out, meta[0], step)


def teacher_attention(meta, away, here, kv_blocks):
    return pl.pallas_call(
        teacher_kernel,
        in_specs=[pl.BlockSpec(memory_space=SMEM), VMEM, VMEM] + [FAR] * len(kv_blocks),
        out_specs=[pl.BlockSpec((BLOCK, HD), lambda: (0, 0))] * 2,
        out_shape=[pltpu.HBM((BLOCK, HD), bf16)] * 2,
        scratch_shapes=WITH_COUNTS,
        compiler_params=pltpu.CompilerParams(vmem_limit_bytes=24 << 20),
        cost_estimate=pl.CostEstimate(
            flops=8 * 4 * BLOCK * BLOCK * HD, bytes_accessed=5 << 20, transcendentals=8 * BLOCK * BLOCK
        ),
        name="teacher_attention",
    )(meta, away, here, *map(far, kv_blocks))


def chosen_rows(sel, row, table):
    pieces = []
    for n in range(NSEL):
        start = pl.multiple_of(sel[row * NSEL + n], BS)
        pieces.append(table[pl.ds(start, BS), :])
    return jnp.concatenate(pieces, axis=0)


def student_forward_kernel(meta, sel, q_ref, kpos_ref, *refs):
    blocks = blocks_of(refs[:-6])
    o_ref, p_ref, key_all, value_all, counts, sems = refs[-6:]
    step = pl.program_id(0)

    @pl.when(step == 0)
    def _():
        load(blocks, key_all, value_all, counts, sems)

    border = border_of(counts)
    for u in range(FORWARD_ROWS):
        row = step * FORWARD_ROWS + u
        span = pl.ds(u * BS, BS)
        q_pos = meta[0] * BLOCK + row * BS + lax.broadcasted_iota(jnp.int32, (BS, 1), 0)
        q_low = jnp.where(q_pos >= border, border, 0)
        k_pos = kpos_ref[u]
        scores = lax.dot_general(
            q_ref[span, :], chosen_rows(sel, row, key_all), ROWS_NT, preferred_element_type=f32
        )
        scores = jnp.where((k_pos <= q_pos) & (k_pos >= q_low), scores, LOWEST)
        weights = jnp.exp2((scores - jnp.max(scores, axis=1, keepdims=True)) * EXP_SCALE)
        inverse = 1.0 / jnp.sum(weights, axis=1, keepdims=True)
        p_ref[span, :] = weights * inverse
        blended = jnp.dot(
            weights.astype(bf16), chosen_rows(sel, row, value_all), preferred_element_type=f32
        )
        o_ref[span, :] = (blended * inverse).astype(bf16)


def student_forward(meta, sel, queries, k_pos, kv_blocks):
    size = FORWARD_ROWS * BS
    return pl.pallas_call(
        student_forward_kernel,
        grid=(BLOCK // size,),
        in_specs=[
            pl.BlockSpec(memory_space=SMEM),
            pl.BlockSpec(memory_space=SMEM),
            pl.BlockSpec((size, HD), lambda i: (i, 0)),
            pl.BlockSpec((FORWARD_ROWS, 1, NSEL * BS), lambda i: (i, 0, 0)),
        ]
        + [FAR] * len(kv_blocks),
        out_specs=[
            pl.BlockSpec((size, HD), lambda i: (i, 0)),
            pl.BlockSpec((size, NSEL * BS), lambda i: (i, 0)),
        ],
        out_shape=[
            pltpu.HBM((BLOCK, HD), bf16),
            pltpu.HBM((BLOCK, NSEL * BS), f32),
        ],
        scratch_shapes=WITH_COUNTS,
        compiler_params=pltpu.CompilerParams(vmem_limit_bytes=24 << 20),
        cost_estimate=pl.CostEstimate(
            flops=4 * BLOCK * NSEL * BS * HD, bytes_accessed=9 << 20, transcendentals=BLOCK * NSEL * BS
        ),
        name="student_forward",
    )(meta, sel, queries, k_pos, *map(far, kv_blocks))


def student_backward_kernel(meta, sel, q_ref, p_ref, g_ref, *refs):
    blocks = blocks_of(refs[:-14])
    dq_ref, out_refs = refs[-14], refs[-13:-5]
    key_all, value_all, sems, dk_all, dv_all = refs[-5:]
    step = pl.program_id(0)

    @pl.when(step == 0)
    def _():
        load(blocks, key_all, value_all, None, sems)
        dk_all[...] = jnp.zeros_like(dk_all)
        dv_all[...] = jnp.zeros_like(dv_all)

    for u in range(BACKWARD_ROWS):
        row = step * BACKWARD_ROWS + u
        span = pl.ds(u * BS, BS)
        grad = jnp.sum(g_ref[:, span, :].astype(f32), axis=0).astype(bf16)
        weights = p_ref[span, :]
        weight_grad = lax.dot_general(
            grad, chosen_rows(sel, row, value_all), ROWS_NT, preferred_element_type=f32
        )
        row_dots = jnp.sum(weights * weight_grad, axis=1, keepdims=True)
        score_grad = (weights * (weight_grad - row_dots) * SCALE).astype(bf16)
        dq_ref[span, :] = jnp.dot(
            score_grad, chosen_rows(sel, row, key_all), preferred_element_type=f32
        )
        key_grad = lax.dot_general(score_grad, q_ref[span, :], ROWS_TN, preferred_element_type=f32)
        value_grad = lax.dot_general(
            weights.astype(bf16), grad, ROWS_TN, preferred_element_type=f32
        )
        for n in range(NSEL):
            start = pl.multiple_of(sel[row * NSEL + n], BS)
            dk_all[pl.ds(start, BS), :] += key_grad[n * BS : (n + 1) * BS, :]
            dv_all[pl.ds(start, BS), :] += value_grad[n * BS : (n + 1) * BS, :]

    @pl.when(step == pl.num_programs(0) - 1)
    def _():
        copies = []
        for j in (4, 5, 6, 7, 0, 1, 2, 3):
            ref = out_refs[j]
            start = pl.multiple_of((meta[1] * 4 + j) % 8 * BLOCK, BLOCK)
            for k, (total, table) in enumerate(((dk_all, key_all), (dv_all, value_all))):
                spot = pl.ds(k * BLOCK, BLOCK)
                if j < 4:
                    ref[spot, :] = total[pl.ds(start, BLOCK), :].astype(bf16)
                    continue
                slot = pl.ds((j - 4) * BLOCK, BLOCK)
                table[slot, :] = total[pl.ds(start, BLOCK), :].astype(bf16)
                copy = pltpu.make_async_copy(table.at[slot], ref.at[spot], sems.at[len(copies)])
                copy.start()
                copies.append(copy)
        for copy in copies:
            copy.wait()


def student_backward(meta, sel, queries, weights, grad_pieces, kv_blocks):
    size = BACKWARD_ROWS * BS
    return pl.pallas_call(
        student_backward_kernel,
        grid=(BLOCK // size,),
        in_specs=[
            pl.BlockSpec(memory_space=SMEM),
            pl.BlockSpec(memory_space=SMEM),
            pl.BlockSpec((size, HD), lambda i: (i, 0)),
            pl.BlockSpec((size, NSEL * BS), lambda i: (i, 0)),
            pl.BlockSpec((8, size, HD), lambda i: (0, i, 0)),
        ]
        + [FAR] * len(kv_blocks),
        out_specs=[pl.BlockSpec((size, HD), lambda i: (i, 0))] + [VMEM] * 4 + [FAR] * 4,
        out_shape=[jax.ShapeDtypeStruct((BLOCK, HD), f32)]
        + [jax.ShapeDtypeStruct((2 * BLOCK, HD), bf16)] * 4
        + [pltpu.HBM((2 * BLOCK, HD), bf16)] * 4,
        scratch_shapes=KEYS + [pltpu.SemaphoreType.DMA((16,))] + [pltpu.VMEM((8 * BLOCK, HD), f32)] * 2,
        compiler_params=pltpu.CompilerParams(vmem_limit_bytes=32 << 20),
        cost_estimate=pl.CostEstimate(
            flops=8 * BLOCK * NSEL * BS * HD, bytes_accessed=15 << 20, transcendentals=0
        ),
        name="student_backward",
    )(meta, sel, queries, far(weights), grad_pieces, *map(far, kv_blocks))


def project(where, attn, weights, width, extra=None, after=()):
    composed = len(weights) == 1

    def piece(p, at):
        return (p // 2) * 4 + at[0] * 2 + p % 2

    if composed:
        w_specs = [pl.BlockSpec((8, 1, COUNTS, 3 * HD), lambda p, c: (0, piece(p, c), 0, 0))]
    else:
        w_specs = [
            pl.BlockSpec((HD, width), lambda p, c: (0, piece(p, c))),
            pl.BlockSpec((2 * HD, width), lambda p, c: (0, piece(p, c))),
        ]
    out_spec = pl.BlockSpec((1, BLOCK, width), lambda p, c: (p, 0, 0))
    more = [] if extra is None else [extra]
    args = list(attn) + list(weights) + more + list(after)

    def kernel(at, s_ref, a_ref, b_ref, *refs):
        near = pl.multiple_of(at[1] * HD, HD)
        far = pl.multiple_of((1 - at[1]) * HD, HD)
        if composed:
            wide = refs[0][...].reshape(HD, 3 * HD)
            here, back = a_ref[...], b_ref[...]
            first = jnp.where(at[1] == 0, here, back)
            second = jnp.where(at[1] == 0, back, here)

            def times(value, j):
                return lax.dot_general(
                    value, wide[:, j * HD : (j + 1) * HD], ROWS_NT, preferred_element_type=f32
                )

            acc = times(s_ref[...], 0) - times(first, 1) - times(second, 2)
        else:
            acc = jnp.dot(s_ref[...], refs[0][...], preferred_element_type=f32)
            acc -= jnp.dot(a_ref[...], refs[1][pl.ds(near, HD), :], preferred_element_type=f32)
            acc -= jnp.dot(b_ref[...], refs[1][pl.ds(far, HD), :], preferred_element_type=f32)
        if extra is not None:
            acc = acc + refs[len(weights)][0].astype(f32)
        refs[-1][0] = acc.astype(bf16)

    return pl.pallas_call(
        kernel,
        grid_spec=pltpu.PrefetchScalarGridSpec(
            num_scalar_prefetch=1,
            grid=(8,),
            in_specs=[pl.BlockSpec((BLOCK, HD), lambda p, c: (0, 0))] * 3
            + w_specs
            + [out_spec] * len(more)
            + [ANY] * len(after),
            out_specs=out_spec,
        ),
        out_shape=(pltpu.HBM if more else jax.ShapeDtypeStruct)((8, BLOCK, width), bf16),
        compiler_params=pltpu.CompilerParams(vmem_limit_bytes=16 << 20),
        cost_estimate=pl.CostEstimate(
            flops=2 * 8 * BLOCK * width * 3 * HD,
            bytes_accessed=2 * 8 * BLOCK * width * (1 + len(more)) + (2 << 20),
            transcendentals=0,
        ),
        name="project_grad" if composed else "project_mismatch",
    )(where, *args)


def token(*arrays):
    total = None
    for array in arrays:
        corner = array[:COUNTS, :] if array.ndim == 2 else array[0, :COUNTS, :]
        total = corner if total is None else total + corner
    return total


def gate(values, after):
    def kernel(*refs):
        pass

    n = len(values)
    return tuple(
        pl.pallas_call(
            kernel,
            in_specs=[FAR] * n + [ANY] * len(after),
            out_specs=[FAR] * n,
            out_shape=[pltpu.HBM(v.shape, v.dtype) for v in values],
            input_output_aliases={k: k for k in range(n)},
            name="gate",
        )(*map(far, values), *after)
    )


def pack_kernel(at, seg_ref, tq_ref, tk_ref, tv_ref, sk_ref, sv_ref, so_ref, *refs):
    outs, stages, sems = refs[:6], refs[6:12], refs[12]
    s_own, t_own, t_sent, q_own, q_sent, rows = stages
    near = pl.ds(pl.multiple_of(at[0] * HD, HD), HD)
    other = pl.ds(pl.multiple_of((1 - at[0]) * HD, HD), HD)
    started = 0

    def move(source, target):
        nonlocal started
        copy = pltpu.make_async_copy(source, target, sems.at[started])
        copy.start()
        started += 1
        return copy

    keys, values, last = pl.ds(0, BLOCK), pl.ds(BLOCK, BLOCK), pl.ds(2 * BLOCK, COUNTS)
    part = pl.ds(pl.multiple_of(at[1] * COUNTS, COUNTS), COUNTS)
    coming = (
        (0, [move(sk_ref, s_own.at[keys]), move(sv_ref, s_own.at[values])]),
        (2, [move(tk_ref.at[:, other], t_sent.at[keys]), move(tv_ref.at[:, other], t_sent.at[values])]),
        (4, [move(tq_ref.at[:, other], q_sent)]),
        (5, [move(so_ref.at[part], rows)]),
        (1, [move(tk_ref.at[:, near], t_own.at[keys]), move(tv_ref.at[:, near], t_own.at[values])]),
        (3, [move(tq_ref.at[:, near], q_own)]),
    )
    found = jnp.sum((seg_ref[...] == 0).astype(f32), axis=0, keepdims=True)
    first = lax.broadcasted_iota(jnp.int32, (COUNTS, HD), 0) == 0
    counts = jnp.where(first, found, 0.0).astype(bf16)
    for stage in (s_own, t_own, t_sent):
        stage[last, :] = counts
    going = []
    for k, copies in coming:
        for copy in copies:
            copy.wait()
        going.append(move(stages[k], outs[k]))
    for copy in going:
        copy.wait()


def pack(at, seg, *arrays):
    shapes = [(SPAN, HD)] * 3 + [(BLOCK, HD)] * 2 + [(COUNTS, arrays[-1].shape[1])]
    return pl.pallas_call(
        pack_kernel,
        in_specs=[pl.BlockSpec(memory_space=SMEM), VMEM] + [FAR] * 6,
        out_specs=[FAR] * 6,
        out_shape=[pltpu.HBM(shape, bf16) for shape in shapes],
        scratch_shapes=[pltpu.VMEM(shape, bf16) for shape in shapes] + [pltpu.SemaphoreType.DMA((15,))],
        compiler_params=pltpu.CompilerParams(vmem_limit_bytes=8 << 20),
        cost_estimate=pl.CostEstimate(flops=0, bytes_accessed=5 << 20, transcendentals=0),
        name="pack",
    )(at, seg, *map(far, arrays))


def repack_kernel(*refs):
    for n, ref in enumerate(refs[:5]):
        target, k = (refs[-2], n) if n < 2 else (refs[-1], n - 2)
        target[k * SPAN : (k + 1) * SPAN, :] = ref[...]


def repack(teacher, student, after):
    return pl.pallas_call(
        repack_kernel,
        in_specs=[VMEM] * 5 + [ANY] * len(after),
        out_specs=[VMEM] * 2,
        out_shape=[jax.ShapeDtypeStruct((k * SPAN, HD), bf16) for k in (2, 3)],
        compiler_params=pltpu.CompilerParams(vmem_limit_bytes=8 << 20),
        cost_estimate=pl.CostEstimate(flops=0, bytes_accessed=5 << 20, transcendentals=0),
        name="repack",
    )(*teacher, *student, *after)


def compose_kernel(rows_ref, s_ref, t_ref, *refs):
    rows = rows_ref[...]
    for ref, low, high in ((s_ref, 0, HD), (t_ref, HD, 3 * HD)):
        refs[-1][:, low:high] = lax.dot_general(
            rows, ref[...], ROWS_NT, preferred_element_type=f32
        ).astype(bf16)


def compose(rows, s_out, t_out, after):
    return pl.pallas_call(
        compose_kernel,
        in_specs=[VMEM] * 3 + [ANY] * len(after),
        out_specs=VMEM,
        out_shape=jax.ShapeDtypeStruct((rows.shape[0], 3 * HD), bf16),
        compiler_params=pltpu.CompilerParams(vmem_limit_bytes=24 << 20),
        cost_estimate=pl.CostEstimate(
            flops=2 * rows.shape[0] * 3 * HD * rows.shape[1], bytes_accessed=5 << 20, transcendentals=0
        ),
        name="compose",
    )(rows, s_out, t_out, *after)


def add_pieces_kernel(in_ref, out_ref):
    out_ref[...] = jnp.sum(in_ref[...].astype(f32), axis=0)


def add_pieces(pieces):
    count, rows, width = pieces.shape
    size = rows // 4
    return pl.pallas_call(
        add_pieces_kernel,
        grid=(4,),
        in_specs=[pl.BlockSpec((count, size, width), lambda i: (0, i, 0))],
        out_specs=pl.BlockSpec((size, width), lambda i: (i, 0)),
        out_shape=jax.ShapeDtypeStruct((rows, width), f32),
        compiler_params=pltpu.CompilerParams(vmem_limit_bytes=16 << 20),
        cost_estimate=pl.CostEstimate(flops=8 << 20, bytes_accessed=5 << 20, transcendentals=0),
        name="add_pieces",
    )(pieces)


def finish_kernel(at, *refs):
    low, across, high, (dk_ref, dv_ref) = refs[:4], refs[4], refs[5:9], refs[-2:]

    def write(parts):
        for ref, span in ((dk_ref, pl.ds(0, BLOCK)), (dv_ref, pl.ds(BLOCK, BLOCK))):
            total = parts[0][span, :].astype(f32)
            for part in parts[1:]:
                total = total + part[span, :].astype(f32)
            ref[...] = total

    @pl.when(at[0] == 0)
    def _():
        write(low + (across,))

    @pl.when(at[0] == 1)
    def _():
        write(high)


def finish(at, low, across, high, after):
    near = [pltpu.with_memory_space_constraint(part, pltpu.VMEM) for part in (*low, across, *high)]
    return pl.pallas_call(
        finish_kernel,
        in_specs=[pl.BlockSpec(memory_space=SMEM)] + [VMEM] * 9 + [ANY] * len(after),
        out_specs=[pl.BlockSpec((BLOCK, HD), lambda: (0, 0))] * 2,
        out_shape=[pltpu.HBM((BLOCK, HD), f32)] * 2,
        compiler_params=pltpu.CompilerParams(vmem_limit_bytes=16 << 20),
        cost_estimate=pl.CostEstimate(flops=4 << 20, bytes_accessed=5 << 20, transcendentals=0),
        name="finish",
    )(at, *near, *after)


def on_device(t_query, t_key, t_value, t_out, s_query, s_key, s_value, s_out, segments, selection):
    x, y, core = lax.axis_index("xlo"), lax.axis_index("y"), lax.axis_index("core")
    mine = 4 * x + y
    partner = 4 * (1 - x) + y

    def along_y(block, all_x, causal_x):
        return tuple(
            lax.ppermute(block, BLK, y_pairs(shift, all_x, causal_x)) for shift in (1, -1, 2)
        )

    to_partner = [(i, i ^ 4) for i in range(8)]
    at_x = jnp.stack([x, mine]).astype(jnp.int32)
    s_own, t_own, t_sent, q_own, q_sent, rows = pack(
        at_x, segments.reshape(8, HD), t_query, t_key, t_value, s_key, s_value, s_out
    )
    up = [(i, i + 4) for i in range(4)]
    s_near = along_y(s_own, (0,), (1,))
    t_got = lax.ppermute(t_sent, BLK, to_partner)
    s_low = lax.ppermute(s_own, BLK, up)
    t_two, s_three = repack((t_own, t_got), s_near, (token(s_low),))
    t_near = along_y(t_two, (0, 1), ())
    s_lows = lax.ppermute(s_three, BLK, up)
    q_got = lax.ppermute(q_sent, BLK, to_partner)

    rows = lax.all_gather(rows, GROUP, axis=0, tiled=True)
    through = compose(rows, s_out, t_out, (token(*t_near, s_lows, q_got),))
    through = lax.all_gather(through, BLK, axis=0, tiled=True).reshape(8, 16, HD // 8, 3 * HD)

    def place_of(block):
        step = (block + 4 - y) % 4
        return jnp.where(step == 0, 0, jnp.where(step == 3, 1, step + 1)), (block // 4 != x).astype(jnp.int32)

    near, half = place_of(jnp.arange(8, dtype=jnp.int32))
    t_meta = jnp.concatenate([jnp.stack([mine, partner] + [0] * 6).astype(jnp.int32), 2 * near + half])
    near, half = place_of(selection // 16)
    sel = ((near + 4 * half) * BLOCK + selection % 16 * BS).reshape(-1).astype(jnp.int32)
    k_pos = (selection[:, :, None] * BS + jnp.arange(BS, dtype=jnp.int32)).reshape(-1, 1, NSEL * BS)
    s_meta = jnp.stack([mine, x]).astype(jnp.int32)

    t_blocks = (t_own, t_got, *t_near)
    away, here = teacher_attention(t_meta, q_got, q_own, t_blocks)
    back = lax.ppermute(away, BLK, to_partner)
    s_blocks = (s_own, *s_near, s_low, s_lows)
    s_attn, weights = student_forward(s_meta, sel, s_query, k_pos, s_blocks)
    attn = (s_attn, here, back)

    this = jnp.stack([core, x]).astype(jnp.int32)
    other = jnp.stack([1 - core, x]).astype(jnp.int32)
    to_core = [(0, 1), (1, 0)]
    grad = project(other, attn, (through,), HD)
    grad = lax.ppermute(grad, "core", to_core)
    grad = project(this, attn, (through,), HD, grad)
    part = project(other, attn, (s_out, t_out), 2 * HD, None, (token(grad),))
    grad = lax.all_to_all(grad, ZX, 0, 0, tiled=True)
    part = lax.ppermute(part, "core", to_core)
    part = project(this, attn, (s_out, t_out), 2 * HD, part)
    part = lax.all_to_all(part, ZX, 0, 0, tiled=True)

    out = student_backward(s_meta, sel, s_query, weights, grad, s_blocks)
    s_dq, pieces = out[0], out[1:]

    def earlier(shift, all_x, causal_x):
        pairs = []
        for i in range(2):
            for j in range(4):
                to = (j + shift) % 4
                if i in all_x or (i in causal_x and to < j):
                    pairs.append((4 * i + j, 4 * i + to))
        return pairs

    low, high = list(pieces[:4]), list(pieces[4:])
    for j, shift in ((1, -1), (2, 1), (3, 2)):
        low[j] = lax.ppermute(low[j], BLK, earlier(shift, (1,), (0,)))
    low_sum = low[0].astype(f32) + low[1].astype(f32) + low[2].astype(f32) + low[3].astype(f32)
    across = low_sum.astype(bf16)
    high = list(gate(high, (token(across),)))
    across = lax.ppermute(across, BLK, [(i + 4, i) for i in range(4)])
    for j, shift in ((1, -1), (2, 1), (3, 2)):
        high[j] = lax.ppermute(high[j], BLK, earlier(shift, (), (1,)))
    mismatch = add_pieces(part)
    s_dk, s_dv = finish(at_x, tuple(low), across, tuple(high), (token(mismatch[:, :HD]),))
    return mismatch, s_dq, s_dk, s_dv


def solution(mesh):
    fine = Mesh(mesh.devices.reshape(2, 4, 4, 2, 2), ("xlo", "y", "z", "core", "xhi"))
    data = P(BLK, GROUP)
    flat = P(GROUP, None)
    return jax.shard_map(
        on_device,
        mesh=fine,
        in_specs=(data, data, data, flat, data, data, data, flat, P(BLK), P(BLK, None)),
        out_specs=(data, data, data, data),
        check_vma=False,
    )
```

time: 349 us -> 298 us (0.85)
  waiting for transfers between devices: 152 us -> 125 us
  starting transfers between devices: 82 us -> 59 us
  Pallas kernels: 62 us -> 81.6 us
  other arithmetic: 10.8 us -> 0.67 us
  matrix products: 4.44 us -> 0 us
  local copies, waits for them, and re-layouts: 21 us -> 17.4 us
    ppermute x9 -> x6, waiting for transfers between devices: 44.3 us -> 8.24 us  [along_y(): lax.ppermute(block, BLK, y_pairs(shift, all_x, causal_x))]
    all_gather x1, waiting for transfers between devices: 20.4 us -> 0.01 us  [on_device(): rows = lax.all_gather(rows, GROUP, axis=0, tiled=True)]
    ppermute x13 -> x11, waiting for transfers between devices: 69 us -> 89.1 us  [the longest x1 36.8 us: on_device(): q_got = lax.ppermute(q_sent, BLK, to_partner)]
    pallas_call x4 -> x9, Pallas kernels: 39.9 us -> 56.2 us  [the longest x1 19.4 us: teacher_attention(): pl.pallas_call(teacher_kernel, in_specs=[pl.BlockSpec(memory_space=SMEM),...]
    ppermute x9 -> x6, starting transfers between devices: 28.3 us -> 14.1 us  [along_y(): lax.ppermute(block, BLK, y_pairs(shift, all_x, causal_x))]
    all_gather x1, waiting for transfers between devices: 0.02 us -> 7.59 us  [on_device(): lax.all_gather(through, BLK, axis=0, tiled=True)]
    ppermute x13 -> x11, starting transfers between devices: 32.1 us -> 27.1 us  [the longest x3 12.8 us: on_device(): low[j] = lax.ppermute(low[j], BLK, earlier(shift, (1,), (0,)))]
    dynamic_slice x3 -> x0, local copies, waits for them, and re-layouts: 4.73 us -> none  [the longest x2 3.12 us: half(): return lax.dynamic_slice_in_dim(array, which * HD, HD, axis)]
  transfers between devices with their start and end apart: 29 -> 24, of which waited for: 15 -> 13; matrix products, arithmetic and copies ran while one was open for 4% -> 1% of each run, Pallas kernels for 14% -> 19%
where the time goes in v2:
time: 298 us
  waiting for transfers between devices  125 us (42%)
  Pallas kernels  81.6 us (27%)
  starting transfers between devices  59 us (20%)
  local copies, waits for them, and re-layouts  17.4 us (6%)
  between operations  14.4 us (5%)
    ppermute x1, waiting for transfers between devices, on_device(): q_got = lax.ppermute(q_sent, BLK, to_partner)  36.8 us
    pallas_call x4, Pallas kernels, project(): pl.pallas_call(kernel, grid_spec=pltpu.PrefetchScalarGridSpec(num_scalar_...  25.4 us
    ppermute x3, waiting for transfers between devices, on_device(): low[j] = lax.ppermute(low[j], BLK, earlier(shift, (1,), (0,)))  19.7 us
    pallas_call x1, Pallas kernels, teacher_attention(): pl.pallas_call(teacher_kernel, in_specs=[pl.BlockSpec(memory_space=SMEM),...  19.4 us
    ppermute x3, waiting for transfers between devices, on_device(): high[j] = lax.ppermute(high[j], BLK, earlier(shift, (), (1,)))  16.5 us
    all_to_all x1, waiting for transfers between devices, on_device(): grad = lax.all_to_all(grad, ZX, 0, 0, tiled=True)  15.3 us
    unnamed x62, local copies, waits for them, and re-layouts  15 us
    pallas_call x1, Pallas kernels, student_backward(): pl.pallas_call(student_backward_kernel, grid=(BLOCK // size,), in_specs=[...  14.7 us
  transfers between devices with their start and end apart: 24, of which 13 were waited for; matrix products, arithmetic and copies ran while one was open for 1% of the time, Pallas kernels for 19%

profile of v2, /device:TPU:6, one launch (start us, length us, event | category | flops | bytes accessed | tf_op | source)
XLA Modules:
  0.0 298.3 jit_solution(12248128823500299867)
XLA Ops:
  7.3 0.7 copy-done.19
  8.0 3.1 %pack.1 = (bf16[2064,128]{1,0:T(8,128)(2,1)}, bf16[2064,128]{1,0:T(8,128)(2,1)}, bf16[2064,128]{1,0:T(8,128)(2,1)}, bf16[1024,128]{1,0:T(8,128)(2,1)}, bf16[1024...) custom-call(s32[2]{0:T(128)S(1)} %pad_add_fusion.2.at, s32[8,128]{1,0:T(8,128)S(1)} %bitcast.11, bf16[1024,256]{1,0:T(8,128)(2,1)} %tq_ref.1, ...), custom_call_target="tpu_custom_call" | custom-call | bytes 5242880 | tf_op jit(solution)/shard_map/pack/pallas_call | solution.py:428
  11.1 1.4 collective-permute-start.3
  12.6 2.8 collective-permute-start.4
  15.3 5.1 %collective-permute-start.2 = (bf16[2064,128]{1,0:T(8,128)(2,1)}, bf16[2064,128]{1,0:T(8,128)(2,1)S(1)}, u32[]{:S(2)}, u32[]{:S(2)}) collective-permute-start(bf16[2064,128]{1,0:T(8,128)(2,1)} %get-tuple-element.31.refs_0_), channel_id=1, source_target_pairs={{0,32},{16,48},{32,0},{48,16},{64,96},{80,112},{1,33},{17,49},{33,... | collective-permute-start | bytes 1585160 | tf_op jit(solution)/shard_map/ppermute | solution.py:538
  20.4 1.3 collective-permute-start.1
  21.8 2.0 collective-permute-start
  23.8 5.9 %collective-permute-done.3.refs_4_ = bf16[2064,128]{1,0:T(8,128)(2,1)S(1)} collective-permute-done((bf16[2064,128]{1,0:T(8,128)(2,1)}, bf16[2064,128]{1,0:T(8,128)(2,1)S(1)}, u32[]{:S(2)}, u32[]{:S(2)}) %collective-permute-start.3) | collective-permute-done | bytes 528416 | tf_op jit(solution)/shard_map/ppermute | solution.py:549
  29.7 10.2 %collective-permute-done.4.refs_1_ = bf16[2064,128]{1,0:T(8,128)(2,1)S(1)} collective-permute-done((bf16[2064,128]{1,0:T(8,128)(2,1)}, bf16[2064,128]{1,0:T(8,128)(2,1)S(1)}, u32[]{:S(2)}, u32[]{:S(2)}) %collective-permute-start.4) | collective-permute-done | bytes 528416 | tf_op jit(solution)/shard_map/ppermute | solution.py:548
  39.9 3.0 %collective-permute-done.1.refs_3_.refs_2_ = bf16[2064,128]{1,0:T(8,128)(2,1)S(1)} collective-permute-done((bf16[2064,128]{1,0:T(8,128)(2,1)}, bf16[2064,128]{1,0:T(8,128)(2,1)S(1)}, u32[]{:S(2)}, u32[]{:S(2)}) %collective-permute-start.1) | collective-permute-done | bytes 528416 | tf_op jit(solution)/shard_map/ppermute | solution.py:538
  42.9 1.4 copy-done.17
  44.3 0.2 repack.1
  44.5 0.8 copy-done.4
  45.3 1.3 collective-permute-start.5
  46.6 3.7 %collective-permute-start.9 = (bf16[4128,128]{1,0:T(8,128)(2,1)S(1)}, bf16[4128,128]{1,0:T(8,128)(2,1)S(1)}, u32[]{:S(2)}, u32[]{:S(2)}) collective-permute-start(bf16[4128,128]{1,0:T(8,128)(2,1)S(1)} %get-tuple-element.38), channel_id=1, source_target_pairs={{0,32},{16,48},{32,0},{48,16},{64,96},{80,112},{96,64},{112,80},{1... | collective-permute-start | bytes 3170312 | tf_op jit(solution)/shard_map/ppermute | solution.py:538
  50.2 1.2 collective-permute-start.8
  51.5 0.8 collective-permute-start.7
  52.3 2.7 collective-permute-start.6
  55.0 36.8 %collective-permute-done.6.away_ref = bf16[1024,128]{1,0:T(8,128)(2,1)S(1)} collective-permute-done((bf16[1024,128]{1,0:T(8,128)(2,1)S(1)}, bf16[1024,128]{1,0:T(8,128)(2,1)S(1)}, u32[]{:S(2)}, u32[]{:S(2)}) %collective-permute-start.6) | collective-permute-done | bytes 262176 | tf_op jit(solution)/shard_map/ppermute | solution.py:553
  91.8 5.2 %collective-permute-done.8.refs_3_ = bf16[4128,128]{1,0:T(8,128)(2,1)S(1)} collective-permute-done((bf16[4128,128]{1,0:T(8,128)(2,1)S(1)}, bf16[4128,128]{1,0:T(8,128)(2,1)S(1)}, u32[]{:S(2)}, u32[]{:S(2)}) %collective-permute-start.8) | collective-permute-done | bytes 1056800 | tf_op jit(solution)/shard_map/ppermute | solution.py:538
  97.1 0.9 copy-done.28
  98.0 0.3 copy-done.29
  98.4 1.2 copy-done.23
  99.6 1.6 copy-done.13
  101.1 1.9 compose.1
  103.8 1.0 copy-done.21
  104.8 0.9 copy-done.22
  105.7 19.4 %teacher_attention.1 = (bf16[1024,128]{1,0:T(8,128)(2,1)}, bf16[1024,128]{1,0:T(8,128)(2,1)}) custom-call(s32[16]{0:T(128)S(1)} %concatenate.3.meta, bf16[1024,128]{1,0:T(8,128)(2,1)S(1)} %copy-done.21, bf16[1024,128]{1,0:T(8,128)(2,1)S(1)} %copy-done.22, bf16[2064,128]{1,0:T(8,128)(2,1)} %get-tuple-element.32.refs_0_, bf16[2064,128]{1,0:T(8,128)(2,1)} %copy-done.18, ...), custom_call_target="tpu_custom_call" | custom-call | flops 4294967296 | bytes 5242880 | tf_op jit(solution)/shard_map/teacher_attention/pallas_call | solution.py:141
  125.1 2.5 collective-permute-start.10
  127.7 10.2 %student_forward.1 = (bf16[1024,128]{1,0:T(8,128)(2,1)}, f32[1024,1024]{1,0:T(8,128)}) custom-call(s32[2]{0:T(128)S(1)} %pad_add_fusion.1.meta, s32[256]{0:T(256)S(1)} %reshape.54.sel, bf16[1024,128]{1,0:T(8,128)(2,1)S(1)} %copy-done.15, s32[16,1,1024]{2,1,0:T(1,128)S(1)} %broadcast_add_fusion.kpos_ref, bf16[2064,128]{1,0:T(8,128)(2,1)} %get-tuple-element.31.refs_0_, ...), custom_call_target="tpu_custom_call" | custom-call | flops 536870912 | bytes 9437184 | tf_op jit(solution)/shard_map/student_forward/pallas_call | solution.py:194
  137.9 0.8 collective-permute-done.10.b_ref
  138.7 0.7 copy-done.8
  139.4 7.6 %all-gather.5.cloned.1.call-done = bf16[2048,384]{1,0:T(8,128)(2,1)} async-done(((bf16[256,384]{1,0:T(8,128)(2,1)}), bf16[2048,384]{1,0:T(8,128)(2,1)}) %all-gather.5.cloned.1.call-update) | async-done | bytes 1572880 | tf_op jit(solution)/shard_map/all_gather | solution.py:557
  147.0 1.4 copy-done.2
  148.4 0.9 copy-done.9
  149.4 0.9 copy-done.11
  150.3 3.9 %project_grad.2 = bf16[8,1024,128]{2,1,0:T(8,128)(2,1)S(1)} custom-call(s32[2]{0:T(128)S(1)} %pad_add_fusion.3.at, bf16[1024,128]{1,0:T(8,128)(2,1)S(1)} %copy-done.11, bf16[1024,128]{1,0:T(8,128)(2,1)S(1)} %copy-done.7, bf16[1024,128]{1,0:T(8,128)(2,1)S(1)} %copy-done.9, bf16[8,16,16,384]{3,2,1,0:T(8,128)(2,1)S(1)} %bitcast.9), custom_call_target="tpu_custom_call" | custom-call | flops 805306368 | bytes 4194304 | tf_op jit(solution)/shard_map/project_grad/pallas_call | solution.py:341
  154.4 4.1 %collective-permute-done.11.refs_1_ = bf16[8,1024,128]{2,1,0:T(8,128)(2,1)S(1)} collective-permute-done((bf16[8,1024,128]{2,1,0:T(8,128)(2,1)S(1)}, bf16[8,1024,128]{2,1,0:T(8,128)(2,1)S(1)}, u32[]{:S(2)}, u32[]{:S(2)}) %collective-permute-start.11) | collective-permute-done | bytes 2097184 | tf_op jit(solution)/shard_map/ppermute | solution.py:581
  158.5 5.4 %project_grad.3 = bf16[8,1024,128]{2,1,0:T(8,128)(2,1)} custom-call(s32[2]{0:T(128)S(1)} %pad_add_fusion.at, bf16[1024,128]{1,0:T(8,128)(2,1)S(1)} %copy-done.11, bf16[1024,128]{1,0:T(8,128)(2,1)S(1)} %copy-done.7, bf16[1024,128]{1,0:T(8,128)(2,1)S(1)} %copy-done.9, bf16[8,16,16,384]{3,2,1,0:T(8,128)(2,1)S(1)} %bitcast.10, ...), custom_call_target="tpu_custom_call" | custom-call | flops 805306368 | bytes 6291456 | tf_op jit(solution)/shard_map/project_grad/pallas_call | solution.py:341
  163.9 0.7 slice_bitcast_fusion.refs_2_
  164.5 6.9 %project_mismatch.2 = bf16[8,1024,256]{2,1,0:T(8,128)(2,1)} custom-call(s32[2]{0:T(128)S(1)} %pad_add_fusion.3.at, bf16[1024,128]{1,0:T(8,128)(2,1)S(1)} %copy-done.11, bf16[1024,128]{1,0:T(8,128)(2,1)S(1)} %copy-done.7, bf16[1024,128]{1,0:T(8,128)(2,1)S(1)} %copy-done.9, bf16[128,4096]{1,0:T(8,128)(2,1)S(1)} %copy-done.1, bf16[256,4096]{1,0:T(8,128)(2,1)S(1)} %copy-done, ...), custom_call_target="tpu_custom_call" | custom-call | flops 1610612736 | bytes 6291456 | tf_op jit(solution)/shard_map/project_mismatch/pallas_call | solution.py:341
  171.5 7.9 %all-to-all-start.1 = ((bf16[8,1024,128]{2,1,0:T(8,128)(2,1)}), bf16[8,1024,128]{2,1,0:T(8,128)(2,1)}, u32[]{:S(2)}, u32[]{:S(2)}) async-start(bf16[8,1024,128]{2,1,0:T(8,128)(2,1)} %project_grad.3), calls=%async_computation.1 | async-start | bytes 4194304 | tf_op jit(solution)/shard_map/all_to_all | solution.py:584
  179.4 0.9 copy-done.10
  180.4 0.9 copy-done.12
  181.3 9.2 %project_mismatch.3 = bf16[8,1024,256]{2,1,0:T(8,128)(2,1)} custom-call(s32[2]{0:T(128)S(1)} %pad_add_fusion.at, bf16[1024,128]{1,0:T(8,128)(2,1)S(1)} %copy-done.12, bf16[1024,128]{1,0:T(8,128)(2,1)S(1)} %copy-done.7, bf16[1024,128]{1,0:T(8,128)(2,1)S(1)} %copy-done.10, bf16[128,4096]{1,0:T(8,128)(2,1)S(1)} %copy-done.1, bf16[256,4096]{1,0:T(8,128)(2,1)S(1)} %copy-done, ...), custom_call_target="tpu_custom_call" | custom-call | flops 1610612736 | bytes 10485760 | tf_op jit(solution)/shard_map/project_mismatch/pallas_call | solution.py:341
  190.5 15.3 %all-to-all-done.1.g_ref = bf16[8,1024,128]{2,1,0:T(8,128)(2,1)} async-done(((bf16[8,1024,128]{2,1,0:T(8,128)(2,1)}), bf16[8,1024,128]{2,1,0:T(8,128)(2,1)}, u32[]{:S(2)}, u32[]{:S(2)}) %all-to-all-start.1) | async-done | bytes 2097184 | tf_op jit(solution)/shard_map/all_to_all | solution.py:584
  205.8 7.1 %all-to-all-start = ((bf16[8,1024,256]{2,1,0:T(8,128)(2,1)}), bf16[8,1024,256]{2,1,0:T(8,128)(2,1)}, u32[]{:S(2)}, u32[]{:S(2)}) async-start(bf16[8,1024,256]{2,1,0:T(8,128)(2,1)} %project_mismatch.3), calls=%async_computation | async-start | bytes 8388608 | tf_op jit(solution)/shard_map/all_to_all | solution.py:587
  212.9 14.7 %student_backward.1 = (f32[1024,128]{1,0:T(8,128)}, bf16[2048,128]{1,0:T(8,128)(2,1)S(1)}, bf16[2048,128]{1,0:T(8,128)(2,1)S(1)}, bf16[2048,128]{1,0:T(8,128)(2,...) custom-call(s32[2]{0:T(128)S(1)} %pad_add_fusion.1.meta, ...), custom_call_target="tpu_custom_call" | custom-call | flops 1073741824 | bytes 15728640 | tf_op jit(solution)/shard_map/student_backward/pallas_call | solution.py:277
  227.6 3.9 %collective-permute-start.13 = (bf16[2048,128]{1,0:T(8,128)(2,1)S(1)}, bf16[2048,128]{1,0:T(8,128)(2,1)S(1)}, u32[]{:S(2)}, u32[]{:S(2)}) collective-permute-start(bf16[2048,128]{1,0:T(8,128)(2,1)S(1)} %get-tuple-element.45), channel_id=1, source_target_pairs={{16,0},{32,16},{48,32},{64,112},{80,64},{96,80},{112,96},{17,1},{3... | collective-permute-start | bytes 1572872 | tf_op jit(solution)/shard_map/ppermute | solution.py:603
  231.5 2.0 collective-permute-start.14
  233.5 6.9 %collective-permute-start.15 = (bf16[2048,128]{1,0:T(8,128)(2,1)S(1)}, bf16[2048,128]{1,0:T(8,128)(2,1)S(1)}, u32[]{:S(2)}, u32[]{:S(2)}) collective-permute-start(bf16[2048,128]{1,0:T(8,128)(2,1)S(1)} %get-tuple-element.47), channel_id=1, source_target_pairs={{32,0},{48,16},{64,96},{80,112},{96,64},{112,80},{33,1},{49,17},{6... | collective-permute-start | bytes 1572872 | tf_op jit(solution)/shard_map/ppermute | solution.py:603
  240.5 12.6 %collective-permute-done.13.refs_1_ = bf16[2048,128]{1,0:T(8,128)(2,1)S(1)} collective-permute-done((bf16[2048,128]{1,0:T(8,128)(2,1)S(1)}, bf16[2048,128]{1,0:T(8,128)(2,1)S(1)}, u32[]{:S(2)}, u32[]{:S(2)}) %collective-permute-start.13) | collective-permute-done | bytes 524320 | tf_op jit(solution)/shard_map/ppermute | solution.py:603
  253.0 7.1 %collective-permute-done.15.refs_3_ = bf16[2048,128]{1,0:T(8,128)(2,1)S(1)} collective-permute-done((bf16[2048,128]{1,0:T(8,128)(2,1)S(1)}, bf16[2048,128]{1,0:T(8,128)(2,1)S(1)}, u32[]{:S(2)}, u32[]{:S(2)}) %collective-permute-start.15) | collective-permute-done | bytes 524320 | tf_op jit(solution)/shard_map/ppermute | solution.py:603
  260.2 0.3 add_convert_fusion
  260.4 0.6 slice.45.refs_4_
  261.2 1.3 collective-permute-start.17
  262.5 1.3 collective-permute-start.18
  263.8 1.4 collective-permute-start.19
  265.3 2.1 collective-permute-start.16
  267.3 4.2 %add_pieces.1 = f32[1024,256]{1,0:T(8,128)} custom-call(bf16[8,1024,256]{2,1,0:T(8,128)(2,1)} %all-to-all-done.in_ref), custom_call_target="tpu_custom_call" | custom-call | flops 8388608 | bytes 5242880 | tf_op jit(solution)/shard_map/add_pieces/pallas_call | solution.py:487
  271.5 0.7 slice.46.refs_9_
  272.2 2.7 collective-permute-done.17.refs_6_
  274.9 13.9 %collective-permute-done.18.refs_7_ = bf16[2048,128]{1,0:T(8,128)(2,1)} collective-permute-done((bf16[2048,128]{1,0:T(8,128)(2,1)}, bf16[2048,128]{1,0:T(8,128)(2,1)}, u32[]{:S(2)}, u32[]{:S(2)}) %collective-permute-start.18) | collective-permute-done | bytes 524320 | tf_op jit(solution)/shard_map/ppermute | solution.py:609
  288.8 2.7 finish.1
  (82 shorter events, 1.4 us)
Async XLA Ops:
  7.2 92.4 %all-gather.3.cloned.1.call-start = ((), (), s32[]{:S(2)}) async-start(), calls=%async_computation.2 | async-start | bytes 2228224 | tf_op jit(solution)/shard_map/all_gather | solution.py:555
  7.3 0.7 copy-start.19
  8.0 91.6 %copy-start.1 = (bf16[128,4096]{1,0:T(8,128)(2,1)S(1)}, bf16[128,4096]{1,0:T(8,128)(2,1)}, u32[]{:S(2)}) copy-start(bf16[128,4096]{1,0:T(8,128)(2,1)} %refs_0_.3) | copy-start | bytes 3145732
  11.0 88.5 %copy-start = (bf16[256,4096]{1,0:T(8,128)(2,1)S(1)}, bf16[256,4096]{1,0:T(8,128)(2,1)}, u32[]{:S(2)}) copy-start(bf16[256,4096]{1,0:T(8,128)(2,1)} %refs_1_.3) | copy-start | bytes 6291460
  11.1 135.9 %all-gather.5.cloned.1.call-start = ((), (), s32[]{:S(2)}) async-start(), calls=%async_computation.3 | async-start | bytes 1769472 | tf_op jit(solution)/shard_map/all_gather | solution.py:557
  11.1 18.5 %collective-permute-start.3 = (bf16[2064,128]{1,0:T(8,128)(2,1)}, bf16[2064,128]{1,0:T(8,128)(2,1)S(1)}, u32[]{:S(2)}, u32[]{:S(2)}) collective-permute-start(bf16[2064,128]{1,0:T(8,128)(2,1)} %get-tuple-element.31.refs_0_), channel_id=1, source_target_pairs={{0,64},{16,80},{32,96},{48,112},{1,65},{17,81},{33,97},{49,113},{2... | collective-permute-start | bytes 1585160 | tf_op jit(solution)/shard_map/ppermute | solution.py:549
  12.6 27.3 %collective-permute-start.4 = (bf16[2064,128]{1,0:T(8,128)(2,1)}, bf16[2064,128]{1,0:T(8,128)(2,1)S(1)}, u32[]{:S(2)}, u32[]{:S(2)}) collective-permute-start(bf16[2064,128]{1,0:T(8,128)(2,1)} %get-tuple-element.33), channel_id=1, source_target_pairs={{0,64},{16,80},{32,96},{48,112},{64,0},{80,16},{96,32},{112,48},{1... | collective-permute-start | bytes 1585160 | tf_op jit(solution)/shard_map/ppermute | solution.py:548
  15.3 24.5 %collective-permute-start.2 = (bf16[2064,128]{1,0:T(8,128)(2,1)}, bf16[2064,128]{1,0:T(8,128)(2,1)S(1)}, u32[]{:S(2)}, u32[]{:S(2)}) collective-permute-start(bf16[2064,128]{1,0:T(8,128)(2,1)} %get-tuple-element.31.refs_0_), channel_id=1, source_target_pairs={{0,32},{16,48},{32,0},{48,16},{64,96},{80,112},{1,33},{17,49},{33,... | collective-permute-start | bytes 1585160 | tf_op jit(solution)/shard_map/ppermute | solution.py:538
  20.4 22.4 %collective-permute-start.1 = (bf16[2064,128]{1,0:T(8,128)(2,1)}, bf16[2064,128]{1,0:T(8,128)(2,1)S(1)}, u32[]{:S(2)}, u32[]{:S(2)}) collective-permute-start(bf16[2064,128]{1,0:T(8,128)(2,1)} %get-tuple-element.31.refs_0_), channel_id=1, source_target_pairs={{0,48},{16,0},{32,16},{48,32},{64,112},{1,49},{17,1},{33,17},{49,3... | collective-permute-start | bytes 1585160 | tf_op jit(solution)/shard_map/ppermute | solution.py:538
  21.8 21.1 %collective-permute-start = (bf16[2064,128]{1,0:T(8,128)(2,1)}, bf16[2064,128]{1,0:T(8,128)(2,1)S(1)}, u32[]{:S(2)}, u32[]{:S(2)}) collective-permute-start(bf16[2064,128]{1,0:T(8,128)(2,1)} %get-tuple-element.31.refs_0_), channel_id=1, source_target_pairs={{0,16},{16,32},{32,48},{48,0},{64,80},{80,96},{96,112},{1,17},{17,... | collective-permute-start | bytes 1585160 | tf_op jit(solution)/shard_map/ppermute | solution.py:538
  29.7 13.2 %copy-start.24 = (bf16[2064,128]{1,0:T(8,128)(2,1)}, bf16[2064,128]{1,0:T(8,128)(2,1)S(1)}, u32[]{:S(2)}) copy-start(bf16[2064,128]{1,0:T(8,128)(2,1)S(1)} %collective-permute-done.3.refs_4_) | copy-start | bytes 1585156
  39.8 6.7 %copy-start.18 = (bf16[2064,128]{1,0:T(8,128)(2,1)}, bf16[2064,128]{1,0:T(8,128)(2,1)S(1)}, u32[]{:S(2)}) copy-start(bf16[2064,128]{1,0:T(8,128)(2,1)S(1)} %collective-permute-done.4.refs_1_) | copy-start | bytes 1585156
  42.9 1.6 copy-start.5
  42.9 2.4 copy-start.6
  42.9 1.4 copy-start.17
  44.3 8.0 %copy-start.30 = (bf16[1024,128]{1,0:T(8,128)(2,1)S(1)}, bf16[1024,128]{1,0:T(8,128)(2,1)}, u32[]{:S(2)}) copy-start(bf16[1024,128]{1,0:T(8,128)(2,1)} %get-tuple-element.36) | copy-start | bytes 786436
  44.5 0.8 copy-start.4
  45.3 51.8 %collective-permute-start.5 = (bf16[6192,128]{1,0:T(8,128)(2,1)S(1)}, bf16[6192,128]{1,0:T(8,128)(2,1)S(1)}, u32[]{:S(2)}, u32[]{:S(2)}) collective-permute-start(bf16[6192,128]{1,0:T(8,128)(2,1)S(1)} %get-tuple-element.34), channel_id=1, source_target_pairs={{0,64},{16,80},{32,96},{48,112},{1,65},{17,81},{33,97},{49,113},{2... | collective-permute-start | bytes 4755464 | tf_op jit(solution)/shard_map/ppermute | solution.py:552
  46.6 45.2 %collective-permute-start.9 = (bf16[4128,128]{1,0:T(8,128)(2,1)S(1)}, bf16[4128,128]{1,0:T(8,128)(2,1)S(1)}, u32[]{:S(2)}, u32[]{:S(2)}) collective-permute-start(bf16[4128,128]{1,0:T(8,128)(2,1)S(1)} %get-tuple-element.38), channel_id=1, source_target_pairs={{0,32},{16,48},{32,0},{48,16},{64,96},{80,112},{96,64},{112,80},{1... | collective-permute-start | bytes 3170312 | tf_op jit(solution)/shard_map/ppermute | solution.py:538
  50.2 46.8 %collective-permute-start.8 = (bf16[4128,128]{1,0:T(8,128)(2,1)S(1)}, bf16[4128,128]{1,0:T(8,128)(2,1)S(1)}, u32[]{:S(2)}, u32[]{:S(2)}) collective-permute-start(bf16[4128,128]{1,0:T(8,128)(2,1)S(1)} %get-tuple-element.38), channel_id=1, source_target_pairs={{0,48},{16,0},{32,16},{48,32},{64,112},{80,64},{96,80},{112,96},{1... | collective-permute-start | bytes 3170312 | tf_op jit(solution)/shard_map/ppermute | solution.py:538
  51.5 45.6 %collective-permute-start.7 = (bf16[4128,128]{1,0:T(8,128)(2,1)S(1)}, bf16[4128,128]{1,0:T(8,128)(2,1)S(1)}, u32[]{:S(2)}, u32[]{:S(2)}) collective-permute-start(bf16[4128,128]{1,0:T(8,128)(2,1)S(1)} %get-tuple-element.38), channel_id=1, source_target_pairs={{0,16},{16,32},{32,48},{48,0},{64,80},{80,96},{96,112},{112,64},{1... | collective-permute-start | bytes 3170312 | tf_op jit(solution)/shard_map/ppermute | solution.py:538
  52.3 39.5 %collective-permute-start.6 = (bf16[1024,128]{1,0:T(8,128)(2,1)S(1)}, bf16[1024,128]{1,0:T(8,128)(2,1)S(1)}, u32[]{:S(2)}, u32[]{:S(2)}) collective-permute-start(bf16[1024,128]{1,0:T(8,128)(2,1)S(1)} %copy-done.30), channel_id=1, source_target_pairs={{0,64},{16,80},{32,96},{48,112},{64,0},{80,16},{96,32},{112,48},{1... | collective-permute-start | bytes 786440 | tf_op jit(solution)/shard_map/ppermute | solution.py:553
  91.8 11.2 %copy-start.20 = (bf16[1024,128]{1,0:T(8,128)(2,1)}, bf16[1024,128]{1,0:T(8,128)(2,1)S(1)}, u32[]{:S(2)}) copy-start(bf16[1024,128]{1,0:T(8,128)(2,1)S(1)} %collective-permute-done.6.away_ref) | copy-start | bytes 786436
  91.8 5.2 %copy-start.27 = (bf16[4128,128]{1,0:T(8,128)(2,1)}, bf16[4128,128]{1,0:T(8,128)(2,1)S(1)}, u32[]{:S(2)}) copy-start(bf16[4128,128]{1,0:T(8,128)(2,1)S(1)} %collective-permute-done.9.refs_4_) | copy-start | bytes 3170308
  97.1 1.0 copy-start.28
  97.1 1.3 copy-start.29
  98.3 1.2 copy-start.23
  99.5 1.6 copy-start.13
  101.1 2.0 copy-start.26
  103.8 1.0 copy-start.21
  104.8 0.9 copy-start.22
  105.7 22.0 %copy-start.15 = (bf16[1024,128]{1,0:T(8,128)(2,1)S(1)}, bf16[1024,128]{1,0:T(8,128)(2,1)}, u32[]{:S(2)}) copy-start(bf16[1024,128]{1,0:T(8,128)(2,1)} %q_ref.3) | copy-start | bytes 786436
  125.1 13.6 %collective-permute-start.10 = (bf16[1024,128]{1,0:T(8,128)(2,1)}, bf16[1024,128]{1,0:T(8,128)(2,1)S(1)}, u32[]{:S(2)}, u32[]{:S(2)}) collective-permute-start(bf16[1024,128]{1,0:T(8,128)(2,1)} %get-tuple-element.40), channel_id=1, source_target_pairs={{0,64},{16,80},{32,96},{48,112},{64,0},{80,16},{96,32},{112,48},{1... | collective-permute-start | bytes 786440 | tf_op jit(solution)/shard_map/ppermute | solution.py:572
  127.7 19.3 %copy-start.7 = (bf16[1024,128]{1,0:T(8,128)(2,1)S(1)}, bf16[1024,128]{1,0:T(8,128)(2,1)}, u32[]{:S(2)}) copy-start(bf16[1024,128]{1,0:T(8,128)(2,1)} %get-tuple-element.39.a_ref) | copy-start | bytes 786436
  138.7 0.7 copy-start.8
  147.0 1.4 copy-start.2
  148.4 0.9 copy-start.9
  149.4 0.9 copy-start.11
  150.3 8.1 %copy-start.3 = (bf16[2048,384]{1,0:T(8,128)(2,1)S(1)}, bf16[2048,384]{1,0:T(8,128)(2,1)}, u32[]{:S(2)}) copy-start(bf16[2048,384]{1,0:T(8,128)(2,1)} %all-gather.5.cloned.1.call-done) | copy-start | bytes 4718596
  154.2 4.2 %collective-permute-start.11 = (bf16[8,1024,128]{2,1,0:T(8,128)(2,1)S(1)}, bf16[8,1024,128]{2,1,0:T(8,128)(2,1)S(1)}, u32[]{:S(2)}, u32[]{:S(2)}) collective-permute-start(bf16[8,1024,128]{2,1,0:T(8,128)(2,1)S(1)} %project_grad.2), channel_id=1, source_target_pairs={{0,2},{2,0},{1,3},{3,1},{4,6},{6,4},{5,7},{7,5},{8,10},{10,8},{9,1... | collective-permute-start | bytes 6291464 | tf_op jit(solution)/shard_map/ppermute | solution.py:581
  171.4 8.0 %collective-permute-start.12 = (bf16[8,1024,256]{2,1,0:T(8,128)(2,1)}, bf16[8,1024,256]{2,1,0:T(8,128)(2,1)}, u32[]{:S(2)}, u32[]{:S(2)}) collective-permute-start(bf16[8,1024,256]{2,1,0:T(8,128)(2,1)} %project_mismatch.2), channel_id=1, source_target_pairs={{0,2},{2,0},{1,3},{3,1},{4,6},{6,4},{5,7},{7,5},{8,10},{10,8},{9,1... | collective-permute-start | bytes 12582920 | tf_op jit(solution)/shard_map/ppermute | solution.py:585
  171.5 34.3 %all-to-all-start.1 = ((bf16[8,1024,128]{2,1,0:T(8,128)(2,1)}), bf16[8,1024,128]{2,1,0:T(8,128)(2,1)}, u32[]{:S(2)}, u32[]{:S(2)}) async-start(bf16[8,1024,128]{2,1,0:T(8,128)(2,1)} %project_grad.3), calls=%async_computation.1 | async-start | bytes 4194304 | tf_op jit(solution)/shard_map/all_to_all | solution.py:584
  179.4 1.0 copy-start.10
  180.4 0.9 copy-start.12
  190.5 22.4 %copy-start.16 = (bf16[1024,128]{1,0:T(8,128)(2,1)S(1)}, bf16[1024,128]{1,0:T(8,128)(2,1)}, u32[]{:S(2)}) copy-start(bf16[1024,128]{1,0:T(8,128)(2,1)} %q_ref.3) | copy-start | bytes 786436
  205.8 61.5 %all-to-all-start = ((bf16[8,1024,256]{2,1,0:T(8,128)(2,1)}), bf16[8,1024,256]{2,1,0:T(8,128)(2,1)}, u32[]{:S(2)}, u32[]{:S(2)}) async-start(bf16[8,1024,256]{2,1,0:T(8,128)(2,1)} %project_mismatch.3), calls=%async_computation | async-start | bytes 8388608 | tf_op jit(solution)/shard_map/all_to_all | solution.py:587
  227.6 25.4 %collective-permute-start.13 = (bf16[2048,128]{1,0:T(8,128)(2,1)S(1)}, bf16[2048,128]{1,0:T(8,128)(2,1)S(1)}, u32[]{:S(2)}, u32[]{:S(2)}) collective-permute-start(bf16[2048,128]{1,0:T(8,128)(2,1)S(1)} %get-tuple-element.45), channel_id=1, source_target_pairs={{16,0},{32,16},{48,32},{64,112},{80,64},{96,80},{112,96},{17,1},{3... | collective-permute-start | bytes 1572872 | tf_op jit(solution)/shard_map/ppermute | solution.py:603
  231.5 21.5 %collective-permute-start.14 = (bf16[2048,128]{1,0:T(8,128)(2,1)S(1)}, bf16[2048,128]{1,0:T(8,128)(2,1)S(1)}, u32[]{:S(2)}, u32[]{:S(2)}) collective-permute-start(bf16[2048,128]{1,0:T(8,128)(2,1)S(1)} %get-tuple-element.46), channel_id=1, source_target_pairs={{48,0},{64,80},{80,96},{96,112},{112,64},{49,1},{65,81},{81,97},{9... | collective-permute-start | bytes 1572872 | tf_op jit(solution)/shard_map/ppermute | solution.py:603
  233.5 26.7 %collective-permute-start.15 = (bf16[2048,128]{1,0:T(8,128)(2,1)S(1)}, bf16[2048,128]{1,0:T(8,128)(2,1)S(1)}, u32[]{:S(2)}, u32[]{:S(2)}) collective-permute-start(bf16[2048,128]{1,0:T(8,128)(2,1)S(1)} %get-tuple-element.47), channel_id=1, source_target_pairs={{32,0},{48,16},{64,96},{80,112},{96,64},{112,80},{33,1},{49,17},{6... | collective-permute-start | bytes 1572872 | tf_op jit(solution)/shard_map/ppermute | solution.py:603
  260.4 0.8 copy-start.25
  261.2 13.7 %collective-permute-start.17 = (bf16[2048,128]{1,0:T(8,128)(2,1)}, bf16[2048,128]{1,0:T(8,128)(2,1)S(1)}, u32[]{:S(2)}, u32[]{:S(2)}) collective-permute-start(bf16[2048,128]{1,0:T(8,128)(2,1)} %get-tuple-element.53), channel_id=1, source_target_pairs={{80,64},{96,80},{112,96},{81,65},{97,81},{113,97},{82,66},{98,82},... | collective-permute-start | bytes 1572872 | tf_op jit(solution)/shard_map/ppermute | solution.py:609
  262.5 26.3 %collective-permute-start.18 = (bf16[2048,128]{1,0:T(8,128)(2,1)}, bf16[2048,128]{1,0:T(8,128)(2,1)}, u32[]{:S(2)}, u32[]{:S(2)}) collective-permute-start(bf16[2048,128]{1,0:T(8,128)(2,1)} %get-tuple-element.54), channel_id=1, source_target_pairs={{112,64},{113,65},{114,66},{115,67},{116,68},{117,69},{118,70},{11... | collective-permute-start | bytes 1572872 | tf_op jit(solution)/shard_map/ppermute | solution.py:609
  263.8 25.0 %copy-start.14 = (bf16[2048,128]{1,0:T(8,128)(2,1)S(1)}, bf16[2048,128]{1,0:T(8,128)(2,1)}, u32[]{:S(2)}) copy-start(bf16[2048,128]{1,0:T(8,128)(2,1)} %get-tuple-element.52.refs_5_) | copy-start | bytes 1572868
  263.8 25.0 %collective-permute-start.19 = (bf16[2048,128]{1,0:T(8,128)(2,1)}, bf16[2048,128]{1,0:T(8,128)(2,1)}, u32[]{:S(2)}, u32[]{:S(2)}) collective-permute-start(bf16[2048,128]{1,0:T(8,128)(2,1)} %get-tuple-element.55), channel_id=1, source_target_pairs={{96,64},{112,80},{97,65},{113,81},{98,66},{114,82},{99,67},{115,83... | collective-permute-start | bytes 1572872 | tf_op jit(solution)/shard_map/ppermute | solution.py:609
  265.3 23.5 %collective-permute-start.16 = (bf16[2048,128]{1,0:T(8,128)(2,1)}, bf16[2048,128]{1,0:T(8,128)(2,1)}, u32[]{:S(2)}, u32[]{:S(2)}) collective-permute-start(bf16[2048,128]{1,0:T(8,128)(2,1)} %copy-done.25), channel_id=1, source_target_pairs={{64,0},{80,16},{96,32},{112,48},{65,1},{81,17},{97,33},{113,49},{6... | collective-permute-start | bytes 1572872 | tf_op jit(solution)/shard_map/ppermute | solution.py:607
Sparse Core Ops, SparseCore 0:
  11.2 49.9 all-gather.2
  103.2 43.7 all-gather.4

commit v3 on v2

--- a/solution.py
+++ b/solution.py
@@ -55,7 +55,7 @@
     return [(ref, k * SPAN) for ref in refs for k in range(ref.shape[0] // SPAN)]
 
 
-def load(blocks, key_all, value_all, counts, sems):
+def load(blocks, key_all, value_all, counts, sems, meanwhile=None):
     copies = []
 
     def bring(source, target):
@@ -69,6 +69,8 @@
         bring(ref.at[pl.ds(at + BLOCK, BLOCK)], value_all.at[slot])
         if counts is not None:
             bring(ref.at[pl.ds(at + 2 * BLOCK, COUNTS)], counts.at[pl.ds(j * COUNTS, COUNTS)])
+    if meanwhile is not None:
+        meanwhile()
     for copy in copies:
         copy.wait()
 
@@ -88,16 +90,16 @@
     border = border_of(counts)
     per_block = BLOCK // TILE_K
 
-    def one_tile(q_ref, o_ref, block, step):
-        first = block * BLOCK + step * TILE_Q
-        low_first = jnp.where(first >= border, border, 0)
-        low_last = jnp.where(first + TILE_Q - 1 >= border, border, 0)
-        span = pl.ds(step * TILE_Q, TILE_Q)
-        queries = q_ref[span, :]
-        q_pos = first + lax.broadcasted_iota(jnp.int32, (TILE_Q, 1), 0)
-        q_low = jnp.where(q_pos >= border, border, 0)
-
-        def turn(masked, j, carry):
+    def one_block(q_ref, o_ref, block):
+        first = block * BLOCK
+        tiles = []
+        for step in range(BLOCK // TILE_Q):
+            q_pos = first + step * TILE_Q + lax.broadcasted_iota(jnp.int32, (TILE_Q, 1), 0)
+            q_low = jnp.where(q_pos >= border, border, 0)
+            tiles.append((q_ref[pl.ds(step * TILE_Q, TILE_Q), :], q_pos, q_low))
+
+        def turn(masked, j, tile, carry):
+            queries, q_pos, q_low = tile
             largest, total, acc = carry
             slot = meta[8 + j // per_block]
             start = pl.multiple_of(slot * BLOCK + (j % per_block) * TILE_K, TILE_K)
@@ -116,31 +118,39 @@
             )
             return new, total, acc
 
-        carry = (
-            jnp.full((TILE_Q, 1), LOWEST, f32),
-            jnp.zeros((TILE_Q, 1), f32),
-            jnp.zeros((TILE_Q, HD), f32),
+        def turns(masked, j, carries):
+            return tuple(turn(masked, j, tile, carry) for tile, carry in zip(tiles, carries))
+
+        carries = tuple(
+            (
+                jnp.full((TILE_Q, 1), LOWEST, f32),
+                jnp.zeros((TILE_Q, 1), f32),
+                jnp.zeros((TILE_Q, HD), f32),
+            )
+            for _ in tiles
         )
-        begin = low_first // TILE_K
+        begin = jnp.where(first >= border, border, 0) // TILE_K
         diagonal = first // TILE_K
+        low_last = jnp.where(first + BLOCK - 1 >= border, border, 0)
         clear = jnp.minimum((low_last + TILE_K - 1) // TILE_K, diagonal)
-        carry = lax.fori_loop(begin, clear, lambda j, c: turn(True, j, c), carry)
-        carry = lax.fori_loop(clear, diagonal, lambda j, c: turn(False, j, c), carry)
-        for j in range(max(TILE_Q // TILE_K, 1)):
-            carry = turn(True, diagonal + j, carry)
-        _, total, acc = carry
-        o_ref[span, :] = (acc / total).astype(bf16)
-
-    for step in range(BLOCK // TILE_Q):
-        one_tile(away_ref, away_out, meta[1], step)
-    for step in range(BLOCK // TILE_Q):
-        one_tile(here_ref, here_out, meta[0], step)
+        carries = lax.fori_loop(begin, clear, lambda j, c: turns(True, j, c), carries)
+        carries = lax.fori_loop(clear, diagonal, lambda j, c: turns(False, j, c), carries)
+        carries = list(carries)
+        for k in range(per_block):
+            for n, tile in enumerate(tiles):
+                if k * TILE_K < (n + 1) * TILE_Q:
+                    carries[n] = turn(True, diagonal + k, tile, carries[n])
+        for step, (_, total, acc) in enumerate(carries):
+            o_ref[pl.ds(step * TILE_Q, TILE_Q), :] = (acc / total).astype(bf16)
+
+    one_block(away_ref, away_out, meta[1])
+    one_block(here_ref, here_out, meta[0])
 
 
 def teacher_attention(meta, away, here, kv_blocks):
     return pl.pallas_call(
         teacher_kernel,
-        in_specs=[pl.BlockSpec(memory_space=SMEM), VMEM, VMEM] + [FAR] * len(kv_blocks),
+        in_specs=[pl.BlockSpec(memory_space=SMEM), VMEM, VMEM] + [ANY] * len(kv_blocks),
         out_specs=[pl.BlockSpec((BLOCK, HD), lambda: (0, 0))] * 2,
         out_shape=[pltpu.HBM((BLOCK, HD), bf16)] * 2,
         scratch_shapes=WITH_COUNTS,
@@ -149,7 +159,7 @@
             flops=8 * 4 * BLOCK * BLOCK * HD, bytes_accessed=5 << 20, transcendentals=8 * BLOCK * BLOCK
         ),
         name="teacher_attention",
-    )(meta, away, here, *map(far, kv_blocks))
+    )(meta, away, here, *kv_blocks)
 
 
 def chosen_rows(sel, row, table):
@@ -200,7 +210,7 @@
             pl.BlockSpec((size, HD), lambda i: (i, 0)),
             pl.BlockSpec((FORWARD_ROWS, 1, NSEL * BS), lambda i: (i, 0, 0)),
         ]
-        + [FAR] * len(kv_blocks),
+        + [ANY] * len(kv_blocks),
         out_specs=[
             pl.BlockSpec((size, HD), lambda i: (i, 0)),
             pl.BlockSpec((size, NSEL * BS), lambda i: (i, 0)),
@@ -215,7 +225,7 @@
             flops=4 * BLOCK * NSEL * BS * HD, bytes_accessed=9 << 20, transcendentals=BLOCK * NSEL * BS
         ),
         name="student_forward",
-    )(meta, sel, queries, k_pos, *map(far, kv_blocks))
+    )(meta, sel, queries, k_pos, *kv_blocks)
 
 
 def student_backward_kernel(meta, sel, q_ref, p_ref, g_ref, *refs):
@@ -226,9 +236,11 @@
 
     @pl.when(step == 0)
     def _():
-        load(blocks, key_all, value_all, None, sems)
-        dk_all[...] = jnp.zeros_like(dk_all)
-        dv_all[...] = jnp.zeros_like(dv_all)
+        def clear():
+            dk_all[...] = jnp.zeros_like(dk_all)
+            dv_all[...] = jnp.zeros_like(dv_all)
+
+        load(blocks, key_all, value_all, None, sems, clear)
 
     for u in range(BACKWARD_ROWS):
         row = step * BACKWARD_ROWS + u
@@ -284,7 +296,7 @@
             pl.BlockSpec((size, NSEL * BS), lambda i: (i, 0)),
             pl.BlockSpec((8, size, HD), lambda i: (0, i, 0)),
         ]
-        + [FAR] * len(kv_blocks),
+        + [ANY] * len(kv_blocks),
         out_specs=[pl.BlockSpec((size, HD), lambda i: (i, 0))] + [VMEM] * 4 + [FAR] * 4,
         out_shape=[jax.ShapeDtypeStruct((BLOCK, HD), f32)]
         + [jax.ShapeDtypeStruct((2 * BLOCK, HD), bf16)] * 4
@@ -295,7 +307,7 @@
             flops=8 * BLOCK * NSEL * BS * HD, bytes_accessed=15 << 20, transcendentals=0
         ),
         name="student_backward",
-    )(meta, sel, queries, far(weights), grad_pieces, *map(far, kv_blocks))
+    )(meta, sel, queries, far(weights), grad_pieces, *kv_blocks)
 
 
 def project(where, attn, weights, width, extra=None, after=()):
@@ -313,7 +325,7 @@
         ]
     out_spec = pl.BlockSpec((1, BLOCK, width), lambda p, c: (p, 0, 0))
     more = [] if extra is None else [extra]
-    args = list(attn) + list(weights) + more + list(after)
+    args = [far(a) for a in attn] + list(weights) + more + list(after)
 
     def kernel(at, s_ref, a_ref, b_ref, *refs):
         near = pl.multiple_of(at[1] * HD, HD)
@@ -387,7 +399,7 @@
 
 def pack_kernel(at, seg_ref, tq_ref, tk_ref, tv_ref, sk_ref, sv_ref, so_ref, *refs):
     outs, stages, sems = refs[:6], refs[6:12], refs[12]
-    s_own, t_own, t_sent, q_own, q_sent, rows = stages
+    s_own, t_sent, q_sent, rows, q_own, t_own = stages
     near = pl.ds(pl.multiple_of(at[0] * HD, HD), HD)
     other = pl.ds(pl.multiple_of((1 - at[0]) * HD, HD), HD)
     started = 0
@@ -403,11 +415,11 @@
     part = pl.ds(pl.multiple_of(at[1] * COUNTS, COUNTS), COUNTS)
     coming = (
         (0, [move(sk_ref, s_own.at[keys]), move(sv_ref, s_own.at[values])]),
-        (2, [move(tk_ref.at[:, other], t_sent.at[keys]), move(tv_ref.at[:, other], t_sent.at[values])]),
-        (4, [move(tq_ref.at[:, other], q_sent)]),
-        (5, [move(so_ref.at[part], rows)]),
-        (1, [move(tk_ref.at[:, near], t_own.at[keys]), move(tv_ref.at[:, near], t_own.at[values])]),
-        (3, [move(tq_ref.at[:, near], q_own)]),
+        (1, [move(tk_ref.at[:, other], t_sent.at[keys]), move(tv_ref.at[:, other], t_sent.at[values])]),
+        (2, [move(tq_ref.at[:, other], q_sent)]),
+        (3, [move(so_ref.at[part], rows)]),
+        (5, [move(tk_ref.at[:, near], t_own.at[keys]), move(tv_ref.at[:, near], t_own.at[values])]),
+        (4, [move(tq_ref.at[:, near], q_own)]),
     )
     found = jnp.sum((seg_ref[...] == 0).astype(f32), axis=0, keepdims=True)
     first = lax.broadcasted_iota(jnp.int32, (COUNTS, HD), 0) == 0
@@ -424,35 +436,41 @@
 
 
 def pack(at, seg, *arrays):
-    shapes = [(SPAN, HD)] * 3 + [(BLOCK, HD)] * 2 + [(COUNTS, arrays[-1].shape[1])]
+    short = (BLOCK, HD)
+    shapes = [(SPAN, HD)] * 2 + [short, (COUNTS, arrays[-1].shape[1]), short, (SPAN, HD)]
     return pl.pallas_call(
         pack_kernel,
         in_specs=[pl.BlockSpec(memory_space=SMEM), VMEM] + [FAR] * 6,
         out_specs=[FAR] * 6,
         out_shape=[pltpu.HBM(shape, bf16) for shape in shapes],
         scratch_shapes=[pltpu.VMEM(shape, bf16) for shape in shapes] + [pltpu.SemaphoreType.DMA((15,))],
-        compiler_params=pltpu.CompilerParams(vmem_limit_bytes=8 << 20),
+        compiler_params=pltpu.CompilerParams(vmem_limit_bytes=12 << 20),
         cost_estimate=pl.CostEstimate(flops=0, bytes_accessed=5 << 20, transcendentals=0),
         name="pack",
     )(at, seg, *map(far, arrays))
 
 
-def repack_kernel(*refs):
-    for n, ref in enumerate(refs[:5]):
-        target, k = (refs[-2], n) if n < 2 else (refs[-1], n - 2)
-        target[k * SPAN : (k + 1) * SPAN, :] = ref[...]
-
-
-def repack(teacher, student, after):
+def repack_kernel(kept_ref, *refs):
+    target, sem = refs[-3], refs[-1]
+    copy = pltpu.make_async_copy(kept_ref, target.at[pl.ds(0, SPAN)], sem)
+    copy.start()
+    target[SPAN:, :] = refs[0][...]
+    for k, ref in enumerate(refs[1:4]):
+        refs[-2][k * SPAN : (k + 1) * SPAN, :] = ref[...]
+    copy.wait()
+
+
+def repack(kept, got, student, after):
     return pl.pallas_call(
         repack_kernel,
-        in_specs=[VMEM] * 5 + [ANY] * len(after),
+        in_specs=[FAR] + [VMEM] * 4 + [ANY] * len(after),
         out_specs=[VMEM] * 2,
         out_shape=[jax.ShapeDtypeStruct((k * SPAN, HD), bf16) for k in (2, 3)],
+        scratch_shapes=[pltpu.SemaphoreType.DMA],
         compiler_params=pltpu.CompilerParams(vmem_limit_bytes=8 << 20),
         cost_estimate=pl.CostEstimate(flops=0, bytes_accessed=5 << 20, transcendentals=0),
         name="repack",
-    )(*teacher, *student, *after)
+    )(far(kept), got, *student, *after)
 
 
 def compose_kernel(rows_ref, s_ref, t_ref, *refs):
@@ -540,14 +558,14 @@
 
     to_partner = [(i, i ^ 4) for i in range(8)]
     at_x = jnp.stack([x, mine]).astype(jnp.int32)
-    s_own, t_own, t_sent, q_own, q_sent, rows = pack(
+    s_own, t_sent, q_sent, rows, q_own, t_own = pack(
         at_x, segments.reshape(8, HD), t_query, t_key, t_value, s_key, s_value, s_out
     )
     up = [(i, i + 4) for i in range(4)]
     s_near = along_y(s_own, (0,), (1,))
     t_got = lax.ppermute(t_sent, BLK, to_partner)
     s_low = lax.ppermute(s_own, BLK, up)
-    t_two, s_three = repack((t_own, t_got), s_near, (token(s_low),))
+    t_two, s_three = repack(t_own, t_got, s_near, (token(s_low),))
     t_near = along_y(t_two, (0, 1), ())
     s_lows = lax.ppermute(s_three, BLK, up)
     q_got = lax.ppermute(q_sent, BLK, to_partner)
@@ -560,27 +578,27 @@
         step = (block + 4 - y) % 4
         return jnp.where(step == 0, 0, jnp.where(step == 3, 1, step + 1)), (block // 4 != x).astype(jnp.int32)
 
-    near, half = place_of(jnp.arange(8, dtype=jnp.int32))
-    t_meta = jnp.concatenate([jnp.stack([mine, partner] + [0] * 6).astype(jnp.int32), 2 * near + half])
-    near, half = place_of(selection // 16)
-    sel = ((near + 4 * half) * BLOCK + selection % 16 * BS).reshape(-1).astype(jnp.int32)
+    spot, half = place_of(jnp.arange(8, dtype=jnp.int32))
+    t_meta = jnp.concatenate([jnp.stack([mine, partner] + [0] * 6).astype(jnp.int32), 2 * spot + half])
+    spot, half = place_of(selection // 16)
+    sel = ((spot + 4 * half) * BLOCK + selection % 16 * BS).reshape(-1).astype(jnp.int32)
     k_pos = (selection[:, :, None] * BS + jnp.arange(BS, dtype=jnp.int32)).reshape(-1, 1, NSEL * BS)
     s_meta = jnp.stack([mine, x]).astype(jnp.int32)
 
-    t_blocks = (t_own, t_got, *t_near)
+    t_blocks = tuple(map(far, (t_own, t_got, *t_near)))
     away, here = teacher_attention(t_meta, q_got, q_own, t_blocks)
     back = lax.ppermute(away, BLK, to_partner)
-    s_blocks = (s_own, *s_near, s_low, s_lows)
+    s_blocks = tuple(map(far, (s_own, *s_near, s_low, s_lows)))
     s_attn, weights = student_forward(s_meta, sel, s_query, k_pos, s_blocks)
     attn = (s_attn, here, back)
 
     this = jnp.stack([core, x]).astype(jnp.int32)
     other = jnp.stack([1 - core, x]).astype(jnp.int32)
     to_core = [(0, 1), (1, 0)]
-    grad = project(other, attn, (through,), HD)
+    part = project(other, attn, (s_out, t_out), 2 * HD)
+    grad = project(other, attn, (through,), HD, None, (token(part),))
     grad = lax.ppermute(grad, "core", to_core)
     grad = project(this, attn, (through,), HD, grad)
-    part = project(other, attn, (s_out, t_out), 2 * HD, None, (token(grad),))
     grad = lax.all_to_all(grad, ZX, 0, 0, tiled=True)
     part = lax.ppermute(part, "core", to_core)
     part = project(this, attn, (s_out, t_out), 2 * HD, part)

time: 298 us -> 294 us (0.987)
  waiting for transfers between devices: 125 us -> 119 us
  local copies, waits for them, and re-layouts: 17.4 us -> 12.3 us
  Pallas kernels: 81.6 us -> 85.4 us
    all_gather x1, waiting for transfers between devices: 7.59 us -> 0.01 us  [on_device(): lax.all_gather(through, BLK, axis=0, tiled=True)]
    unnamed x62 -> x46, local copies, waits for them, and re-layouts: 15 us -> 9.77 us
    pallas_call x4, Pallas kernels: 25.4 us -> 29 us  [project(): pl.pallas_call(kernel, grid_spec=pltpu.PrefetchScalarGridSpec(num_scalar_...]
  transfers between devices with their start and end apart: 24 -> 24, of which waited for: 13 -> 12; matrix products, arithmetic and copies ran while one was open for 1% -> 1% of each run, Pallas kernels for 19% -> 27%
where the time goes in v3:
time: 294 us; the launch traced here: 292 us
  waiting for transfers between devices  119 us (40%)
  Pallas kernels  85.4 us (29%)
  starting transfers between devices  59.9 us (20%)
  between operations  14.4 us (5%)
  local copies, waits for them, and re-layouts  12.3 us (4%)
    ppermute x1, waiting for transfers between devices, on_device(): q_got = lax.ppermute(q_sent, BLK, to_partner)  37 us
    pallas_call x4, Pallas kernels, project(): pl.pallas_call(kernel, grid_spec=pltpu.PrefetchScalarGridSpec(num_scalar_...  29 us
    ppermute x3, waiting for transfers between devices, on_device(): low[j] = lax.ppermute(low[j], BLK, earlier(shift, (1,), (0,)))  21.5 us
    pallas_call x1, Pallas kernels, teacher_attention(): pl.pallas_call(teacher_kernel, in_specs=[pl.BlockSpec(memory_space=SMEM),...  18.8 us
    all_to_all x1, waiting for transfers between devices, on_device(): grad = lax.all_to_all(grad, ZX, 0, 0, tiled=True)  16.9 us
    ppermute x3, waiting for transfers between devices, on_device(): high[j] = lax.ppermute(high[j], BLK, earlier(shift, (), (1,)))  15.4 us
    pallas_call x1, Pallas kernels, student_backward(): pl.pallas_call(student_backward_kernel, grid=(BLOCK // size,), in_specs=[...  14.1 us
    ppermute x6, starting transfers between devices, along_y(): lax.ppermute(block, BLK, y_pairs(shift, all_x, causal_x))  14.1 us
  transfers between devices with their start and end apart: 24, of which 12 were waited for; matrix products, arithmetic and copies ran while one was open for 1% of the time, Pallas kernels for 27%

profile of v3, /device:TPU:6, one launch (start us, length us, event | category | flops | bytes accessed | tf_op | source)
XLA Modules:
  0.0 291.9 jit_solution(12018081021292814525)
XLA Ops:
  7.3 0.7 copy-done.10
  8.0 3.1 %pack.1 = (bf16[2064,128]{1,0:T(8,128)(2,1)}, bf16[2064,128]{1,0:T(8,128)(2,1)}, bf16[1024,128]{1,0:T(8,128)(2,1)}, bf16[16,4096]{1,0:T(8,128)(2,1)}, bf16[1024,...) custom-call(s32[2]{0:T(128)S(1)} %pad_add_fusion.2.at, s32[8,128]{1,0:T(8,128)S(1)} %bitcast.11, bf16[1024,256]{1,0:T(8,128)(2,1)} %tq_ref.1, ...), custom_call_target="tpu_custom_call" | custom-call | bytes 5242880 | tf_op jit(solution)/shard_map/pack/pallas_call | solution.py:441
  11.1 1.4 collective-permute-start.3
  12.6 2.8 collective-permute-start.4
  15.3 5.1 %collective-permute-start.2 = (bf16[2064,128]{1,0:T(8,128)(2,1)}, bf16[2064,128]{1,0:T(8,128)(2,1)S(1)}, u32[]{:S(2)}, u32[]{:S(2)}) collective-permute-start(bf16[2064,128]{1,0:T(8,128)(2,1)} %get-tuple-element.31.refs_0_), channel_id=1, source_target_pairs={{0,32},{16,48},{32,0},{48,16},{64,96},{80,112},{1,33},{17,49},{33,... | collective-permute-start | bytes 1585160 | tf_op jit(solution)/shard_map/ppermute | solution.py:556
  20.5 1.3 collective-permute-start.1
  21.8 2.0 collective-permute-start
  23.8 5.9 %collective-permute-done.3.refs_4_ = bf16[2064,128]{1,0:T(8,128)(2,1)S(1)} collective-permute-done((bf16[2064,128]{1,0:T(8,128)(2,1)}, bf16[2064,128]{1,0:T(8,128)(2,1)S(1)}, u32[]{:S(2)}, u32[]{:S(2)}) %collective-permute-start.3) | collective-permute-done | bytes 528416 | tf_op jit(solution)/shard_map/ppermute | solution.py:567
  29.7 10.2 %collective-permute-done.4.refs_0_.refs_1_ = bf16[2064,128]{1,0:T(8,128)(2,1)S(1)} collective-permute-done((bf16[2064,128]{1,0:T(8,128)(2,1)}, bf16[2064,128]{1,0:T(8,128)(2,1)S(1)}, u32[]{:S(2)}, u32[]{:S(2)}) %collective-permute-start.4) | collective-permute-done | bytes 528416 | tf_op jit(solution)/shard_map/ppermute | solution.py:566
  39.9 3.0 %collective-permute-done.1.refs_2_ = bf16[2064,128]{1,0:T(8,128)(2,1)S(1)} collective-permute-done((bf16[2064,128]{1,0:T(8,128)(2,1)}, bf16[2064,128]{1,0:T(8,128)(2,1)S(1)}, u32[]{:S(2)}, u32[]{:S(2)}) %collective-permute-start.1) | collective-permute-done | bytes 528416 | tf_op jit(solution)/shard_map/ppermute | solution.py:556
  42.9 1.4 repack.1
  44.3 0.8 copy-done.3
  45.1 1.3 collective-permute-start.5
  46.4 3.7 %collective-permute-start.9 = (bf16[4128,128]{1,0:T(8,128)(2,1)S(1)}, bf16[4128,128]{1,0:T(8,128)(2,1)S(1)}, u32[]{:S(2)}, u32[]{:S(2)}) collective-permute-start(bf16[4128,128]{1,0:T(8,128)(2,1)S(1)} %get-tuple-element.38), channel_id=1, source_target_pairs={{0,32},{16,48},{32,0},{48,16},{64,96},{80,112},{96,64},{112,80},{1... | collective-permute-start | bytes 3170312 | tf_op jit(solution)/shard_map/ppermute | solution.py:556
  50.1 1.2 collective-permute-start.8
  51.3 0.8 collective-permute-start.7
  52.1 2.7 collective-permute-start.6
  54.9 37.0 %collective-permute-done.6.away_ref = bf16[1024,128]{1,0:T(8,128)(2,1)S(1)} collective-permute-done((bf16[1024,128]{1,0:T(8,128)(2,1)S(1)}, bf16[1024,128]{1,0:T(8,128)(2,1)S(1)}, u32[]{:S(2)}, u32[]{:S(2)}) %collective-permute-start.6) | collective-permute-done | bytes 262176 | tf_op jit(solution)/shard_map/ppermute | solution.py:571
  91.8 5.1 %collective-permute-done.8.refs_3_ = bf16[4128,128]{1,0:T(8,128)(2,1)S(1)} collective-permute-done((bf16[4128,128]{1,0:T(8,128)(2,1)S(1)}, bf16[4128,128]{1,0:T(8,128)(2,1)S(1)}, u32[]{:S(2)}, u32[]{:S(2)}) %collective-permute-start.8) | collective-permute-done | bytes 1056800 | tf_op jit(solution)/shard_map/ppermute | solution.py:556
  96.9 1.0 copy-done.20
  97.9 0.3 copy-done.21
  98.2 1.2 copy-done.14
  99.4 1.6 copy-done.6
  101.0 1.9 compose.1
  103.1 0.1 reshape.54.sel
  103.2 0.1 add.101
  103.3 0.1 add.102
  103.4 0.1 concatenate.3.meta
  103.7 1.0 copy-done.12
  104.6 0.9 copy-done.13
  105.6 18.8 %teacher_attention.1 = (bf16[1024,128]{1,0:T(8,128)(2,1)}, bf16[1024,128]{1,0:T(8,128)(2,1)}) custom-call(s32[16]{0:T(128)S(1)} %concatenate.3.meta, bf16[1024,128]{1,0:T(8,128)(2,1)S(1)} %copy-done.12, bf16[1024,128]{1,0:T(8,128)(2,1)S(1)} %copy-done.13, bf16[2064,128]{1,0:T(8,128)(2,1)} %get-tuple-element.32.kept_ref.refs_0_, bf16[2064,128]{1,0:T(8,128)(2,1)} %copy-done.9, ...), custom_call_target="tpu_custom_call" | custom-call | flops 4294967296 | bytes 5242880 | tf_op jit(solution)/shard_map/teacher_attention/pallas_call | solution.py:151
  124.4 2.5 collective-permute-start.10
  127.0 10.1 %student_forward.1 = (bf16[1024,128]{1,0:T(8,128)(2,1)}, f32[1024,1024]{1,0:T(8,128)}) custom-call(s32[2]{0:T(128)S(1)} %pad_add_fusion.1.meta, s32[256]{0:T(256)S(1)} %reshape.54.sel, bf16[1024,128]{1,0:T(8,128)(2,1)S(1)} %copy-done.8, s32[16,1,1024]{2,1,0:T(1,128)S(1)} %broadcast_add_fusion.kpos_ref, bf16[2064,128]{1,0:T(8,128)(2,1)} %get-tuple-element.31.refs_0_, ...), custom_call_target="tpu_custom_call" | custom-call | flops 536870912 | bytes 9437184 | tf_op jit(solution)/shard_map/student_forward/pallas_call | solution.py:204
  137.1 0.7 collective-permute-done.10.b_ref
  137.8 0.7 copy-done.15
  138.5 8.0 %project_mismatch.2 = bf16[8,1024,256]{2,1,0:T(8,128)(2,1)} custom-call(s32[2]{0:T(128)S(1)} %pad_add_fusion.3.at, bf16[1024,128]{1,0:T(8,128)(2,1)} %get-tuple-element.35.s_ref, bf16[1024,128]{1,0:T(8,128)(2,1)} %get-tuple-element.39.a_ref, bf16[1024,128]{1,0:T(8,128)(2,1)} %copy-done.15, bf16[128,4096]{1,0:T(8,128)(2,1)S(1)} %copy-done.1, ...), custom_call_target="tpu_custom_call" | custom-call | flops 1610612736 | bytes 6291456 | tf_op jit(solution)/shard_map/project_mismatch/pallas_call | solution.py:353
  146.5 0.7 slice_bitcast_fusion.refs_1_
  147.2 1.4 copy-done.2
  148.6 5.0 %project_grad.2 = bf16[8,1024,128]{2,1,0:T(8,128)(2,1)S(1)} custom-call(s32[2]{0:T(128)S(1)} %pad_add_fusion.3.at, bf16[1024,128]{1,0:T(8,128)(2,1)} %get-tuple-element.35.s_ref, bf16[1024,128]{1,0:T(8,128)(2,1)} %get-tuple-element.39.a_ref, bf16[1024,128]{1,0:T(8,128)(2,1)} %copy-done.15, bf16[8,16,16,384]{3,2,1,0:T(8,128)(2,1)S(1)} %bitcast.9, ...), custom_call_target="tpu_custom_call" | custom-call | flops 805306368 | bytes 4194304 | tf_op jit(solution)/shard_map/project_grad/pallas_call | solution.py:353
  153.6 0.6 collective-permute-start.12
  154.3 3.7 %collective-permute-done.12.refs_1_ = bf16[8,1024,128]{2,1,0:T(8,128)(2,1)S(1)} collective-permute-done((bf16[8,1024,128]{2,1,0:T(8,128)(2,1)S(1)}, bf16[8,1024,128]{2,1,0:T(8,128)(2,1)S(1)}, u32[]{:S(2)}, u32[]{:S(2)}) %collective-permute-start.12) | collective-permute-done | bytes 2097184 | tf_op jit(solution)/shard_map/ppermute | solution.py:600
  158.0 6.5 %project_grad.3 = bf16[8,1024,128]{2,1,0:T(8,128)(2,1)} custom-call(s32[2]{0:T(128)S(1)} %pad_add_fusion.at, bf16[1024,128]{1,0:T(8,128)(2,1)} %get-tuple-element.35.s_ref, bf16[1024,128]{1,0:T(8,128)(2,1)} %get-tuple-element.39.a_ref, bf16[1024,128]{1,0:T(8,128)(2,1)} %copy-done.15, bf16[8,16,16,384]{3,2,1,0:T(8,128)(2,1)S(1)} %bitcast.10, ...), custom_call_target="tpu_custom_call" | custom-call | flops 805306368 | bytes 6291456 | tf_op jit(solution)/shard_map/project_grad/pallas_call | solution.py:353
  164.5 8.8 %all-to-all-start.1 = ((bf16[8,1024,128]{2,1,0:T(8,128)(2,1)}), bf16[8,1024,128]{2,1,0:T(8,128)(2,1)}, u32[]{:S(2)}, u32[]{:S(2)}) async-start(bf16[8,1024,128]{2,1,0:T(8,128)(2,1)} %project_grad.3), calls=%async_computation.1 | async-start | bytes 4194304 | tf_op jit(solution)/shard_map/all_to_all | solution.py:602
  173.3 9.5 %project_mismatch.3 = bf16[8,1024,256]{2,1,0:T(8,128)(2,1)} custom-call(s32[2]{0:T(128)S(1)} %pad_add_fusion.at, bf16[1024,128]{1,0:T(8,128)(2,1)} %get-tuple-element.35.s_ref, bf16[1024,128]{1,0:T(8,128)(2,1)} %get-tuple-element.39.a_ref, bf16[1024,128]{1,0:T(8,128)(2,1)} %copy-done.15, bf16[128,4096]{1,0:T(8,128)(2,1)S(1)} %copy-done.1, ...), custom_call_target="tpu_custom_call" | custom-call | flops 1610612736 | bytes 10485760 | tf_op jit(solution)/shard_map/project_mismatch/pallas_call | solution.py:353
  182.8 16.9 %all-to-all-done.1.g_ref = bf16[8,1024,128]{2,1,0:T(8,128)(2,1)} async-done(((bf16[8,1024,128]{2,1,0:T(8,128)(2,1)}), bf16[8,1024,128]{2,1,0:T(8,128)(2,1)}, u32[]{:S(2)}, u32[]{:S(2)}) %all-to-all-start.1) | async-done | bytes 2097184 | tf_op jit(solution)/shard_map/all_to_all | solution.py:602
  199.7 7.1 %all-to-all-start = ((bf16[8,1024,256]{2,1,0:T(8,128)(2,1)}), bf16[8,1024,256]{2,1,0:T(8,128)(2,1)}, u32[]{:S(2)}, u32[]{:S(2)}) async-start(bf16[8,1024,256]{2,1,0:T(8,128)(2,1)} %project_mismatch.3), calls=%async_computation | async-start | bytes 8388608 | tf_op jit(solution)/shard_map/all_to_all | solution.py:605
  206.8 14.1 %student_backward.1 = (f32[1024,128]{1,0:T(8,128)}, bf16[2048,128]{1,0:T(8,128)(2,1)S(1)}, bf16[2048,128]{1,0:T(8,128)(2,1)S(1)}, bf16[2048,128]{1,0:T(8,128)(2,...) custom-call(s32[2]{0:T(128)S(1)} %pad_add_fusion.1.meta, ...), custom_call_target="tpu_custom_call" | custom-call | flops 1073741824 | bytes 15728640 | tf_op jit(solution)/shard_map/student_backward/pallas_call | solution.py:289
  221.0 7.1 %collective-permute-start.13 = (bf16[2048,128]{1,0:T(8,128)(2,1)S(1)}, bf16[2048,128]{1,0:T(8,128)(2,1)S(1)}, u32[]{:S(2)}, u32[]{:S(2)}) collective-permute-start(bf16[2048,128]{1,0:T(8,128)(2,1)S(1)} %get-tuple-element.45), channel_id=1, source_target_pairs={{16,0},{32,16},{48,32},{64,112},{80,64},{96,80},{112,96},{17,1},{3... | collective-permute-start | bytes 1572872 | tf_op jit(solution)/shard_map/ppermute | solution.py:621
  228.1 1.9 collective-permute-start.14
  230.0 3.4 %collective-permute-start.15 = (bf16[2048,128]{1,0:T(8,128)(2,1)S(1)}, bf16[2048,128]{1,0:T(8,128)(2,1)S(1)}, u32[]{:S(2)}, u32[]{:S(2)}) collective-permute-start(bf16[2048,128]{1,0:T(8,128)(2,1)S(1)} %get-tuple-element.47), channel_id=1, source_target_pairs={{32,0},{48,16},{64,96},{80,112},{96,64},{112,80},{33,1},{49,17},{6... | collective-permute-start | bytes 1572872 | tf_op jit(solution)/shard_map/ppermute | solution.py:621
  233.4 16.2 %collective-permute-done.13.refs_1_ = bf16[2048,128]{1,0:T(8,128)(2,1)S(1)} collective-permute-done((bf16[2048,128]{1,0:T(8,128)(2,1)S(1)}, bf16[2048,128]{1,0:T(8,128)(2,1)S(1)}, u32[]{:S(2)}, u32[]{:S(2)}) %collective-permute-start.13) | collective-permute-done | bytes 524320 | tf_op jit(solution)/shard_map/ppermute | solution.py:621
  249.6 5.3 %collective-permute-done.14.refs_2_ = bf16[2048,128]{1,0:T(8,128)(2,1)S(1)} collective-permute-done((bf16[2048,128]{1,0:T(8,128)(2,1)S(1)}, bf16[2048,128]{1,0:T(8,128)(2,1)S(1)}, u32[]{:S(2)}, u32[]{:S(2)}) %collective-permute-start.14) | collective-permute-done | bytes 524320 | tf_op jit(solution)/shard_map/ppermute | solution.py:621
  254.9 0.3 add_convert_fusion
  255.2 0.6 slice.45.refs_4_
  255.8 0.2 copy-done.17
  256.0 1.3 collective-permute-start.17
  257.3 1.3 collective-permute-start.18
  258.6 1.4 collective-permute-start.19
  260.0 2.1 collective-permute-start.16
  262.1 4.2 %add_pieces.1 = f32[1024,256]{1,0:T(8,128)} custom-call(bf16[8,1024,256]{2,1,0:T(8,128)(2,1)} %all-to-all-done.in_ref), custom_call_target="tpu_custom_call" | custom-call | flops 8388608 | bytes 5242880 | tf_op jit(solution)/shard_map/add_pieces/pallas_call | solution.py:505
  266.3 0.7 slice.46.refs_9_
  267.0 1.5 collective-permute-done.17.refs_6_
  268.5 13.9 %collective-permute-done.18.refs_7_ = bf16[2048,128]{1,0:T(8,128)(2,1)} collective-permute-done((bf16[2048,128]{1,0:T(8,128)(2,1)}, bf16[2048,128]{1,0:T(8,128)(2,1)}, u32[]{:S(2)}, u32[]{:S(2)}) %collective-permute-start.18) | collective-permute-done | bytes 524320 | tf_op jit(solution)/shard_map/ppermute | solution.py:627
  282.4 2.7 finish.1
  (66 shorter events, 0.7 us)
Async XLA Ops:
  7.2 92.2 %all-gather.3.cloned.1.call-start = ((), (), s32[]{:S(2)}) async-start(), calls=%async_computation.2 | async-start | bytes 2228224 | tf_op jit(solution)/shard_map/all_gather | solution.py:573
  7.3 0.7 copy-start.10
  8.0 91.4 %copy-start.1 = (bf16[128,4096]{1,0:T(8,128)(2,1)S(1)}, bf16[128,4096]{1,0:T(8,128)(2,1)}, u32[]{:S(2)}) copy-start(bf16[128,4096]{1,0:T(8,128)(2,1)} %s_ref.1) | copy-start | bytes 3145732
  11.0 88.4 %copy-start = (bf16[256,4096]{1,0:T(8,128)(2,1)S(1)}, bf16[256,4096]{1,0:T(8,128)(2,1)}, u32[]{:S(2)}) copy-start(bf16[256,4096]{1,0:T(8,128)(2,1)} %t_ref.1) | copy-start | bytes 6291460
  11.1 136.1 %all-gather.5.cloned.1.call-start = ((), (), s32[]{:S(2)}) async-start(), calls=%async_computation.3 | async-start | bytes 1769472 | tf_op jit(solution)/shard_map/all_gather | solution.py:575
  11.1 41.0 %copy-start.22 = (bf16[1024,128]{1,0:T(8,128)(2,1)S(1)}, bf16[1024,128]{1,0:T(8,128)(2,1)}, u32[]{:S(2)}) copy-start(bf16[1024,128]{1,0:T(8,128)(2,1)} %get-tuple-element.36) | copy-start | bytes 786436
  11.1 18.5 %collective-permute-start.3 = (bf16[2064,128]{1,0:T(8,128)(2,1)}, bf16[2064,128]{1,0:T(8,128)(2,1)S(1)}, u32[]{:S(2)}, u32[]{:S(2)}) collective-permute-start(bf16[2064,128]{1,0:T(8,128)(2,1)} %get-tuple-element.31.refs_0_), channel_id=1, source_target_pairs={{0,64},{16,80},{32,96},{48,112},{1,65},{17,81},{33,97},{49,113},{2... | collective-permute-start | bytes 1585160 | tf_op jit(solution)/shard_map/ppermute | solution.py:567
  12.6 27.3 %collective-permute-start.4 = (bf16[2064,128]{1,0:T(8,128)(2,1)}, bf16[2064,128]{1,0:T(8,128)(2,1)S(1)}, u32[]{:S(2)}, u32[]{:S(2)}) collective-permute-start(bf16[2064,128]{1,0:T(8,128)(2,1)} %get-tuple-element.33), channel_id=1, source_target_pairs={{0,64},{16,80},{32,96},{48,112},{64,0},{80,16},{96,32},{112,48},{1... | collective-permute-start | bytes 1585160 | tf_op jit(solution)/shard_map/ppermute | solution.py:566
  15.3 24.5 %collective-permute-start.2 = (bf16[2064,128]{1,0:T(8,128)(2,1)}, bf16[2064,128]{1,0:T(8,128)(2,1)S(1)}, u32[]{:S(2)}, u32[]{:S(2)}) collective-permute-start(bf16[2064,128]{1,0:T(8,128)(2,1)} %get-tuple-element.31.refs_0_), channel_id=1, source_target_pairs={{0,32},{16,48},{32,0},{48,16},{64,96},{80,112},{1,33},{17,49},{33,... | collective-permute-start | bytes 1585160 | tf_op jit(solution)/shard_map/ppermute | solution.py:556
  20.5 22.4 %collective-permute-start.1 = (bf16[2064,128]{1,0:T(8,128)(2,1)}, bf16[2064,128]{1,0:T(8,128)(2,1)S(1)}, u32[]{:S(2)}, u32[]{:S(2)}) collective-permute-start(bf16[2064,128]{1,0:T(8,128)(2,1)} %get-tuple-element.31.refs_0_), channel_id=1, source_target_pairs={{0,48},{16,0},{32,16},{48,32},{64,112},{1,49},{17,1},{33,17},{49,3... | collective-permute-start | bytes 1585160 | tf_op jit(solution)/shard_map/ppermute | solution.py:556
  21.8 21.1 %collective-permute-start = (bf16[2064,128]{1,0:T(8,128)(2,1)}, bf16[2064,128]{1,0:T(8,128)(2,1)S(1)}, u32[]{:S(2)}, u32[]{:S(2)}) collective-permute-start(bf16[2064,128]{1,0:T(8,128)(2,1)} %get-tuple-element.31.refs_0_), channel_id=1, source_target_pairs={{0,16},{16,32},{32,48},{48,0},{64,80},{80,96},{96,112},{1,17},{17,... | collective-permute-start | bytes 1585160 | tf_op jit(solution)/shard_map/ppermute | solution.py:556
  29.7 14.6 %copy-start.16 = (bf16[2064,128]{1,0:T(8,128)(2,1)}, bf16[2064,128]{1,0:T(8,128)(2,1)S(1)}, u32[]{:S(2)}) copy-start(bf16[2064,128]{1,0:T(8,128)(2,1)S(1)} %collective-permute-done.3.refs_4_) | copy-start | bytes 1585156
  39.9 6.6 %copy-start.9 = (bf16[2064,128]{1,0:T(8,128)(2,1)}, bf16[2064,128]{1,0:T(8,128)(2,1)S(1)}, u32[]{:S(2)}) copy-start(bf16[2064,128]{1,0:T(8,128)(2,1)S(1)} %collective-permute-done.4.refs_0_.refs_1_) | copy-start | bytes 1585156
  42.9 1.5 copy-start.4
  42.9 2.3 copy-start.5
  44.3 0.8 copy-start.3
  45.1 51.8 %collective-permute-start.5 = (bf16[6192,128]{1,0:T(8,128)(2,1)S(1)}, bf16[6192,128]{1,0:T(8,128)(2,1)S(1)}, u32[]{:S(2)}, u32[]{:S(2)}) collective-permute-start(bf16[6192,128]{1,0:T(8,128)(2,1)S(1)} %get-tuple-element.34), channel_id=1, source_target_pairs={{0,64},{16,80},{32,96},{48,112},{1,65},{17,81},{33,97},{49,113},{2... | collective-permute-start | bytes 4755464 | tf_op jit(solution)/shard_map/ppermute | solution.py:570
  46.4 45.4 %collective-permute-start.9 = (bf16[4128,128]{1,0:T(8,128)(2,1)S(1)}, bf16[4128,128]{1,0:T(8,128)(2,1)S(1)}, u32[]{:S(2)}, u32[]{:S(2)}) collective-permute-start(bf16[4128,128]{1,0:T(8,128)(2,1)S(1)} %get-tuple-element.38), channel_id=1, source_target_pairs={{0,32},{16,48},{32,0},{48,16},{64,96},{80,112},{96,64},{112,80},{1... | collective-permute-start | bytes 3170312 | tf_op jit(solution)/shard_map/ppermute | solution.py:556
  50.1 46.8 %collective-permute-start.8 = (bf16[4128,128]{1,0:T(8,128)(2,1)S(1)}, bf16[4128,128]{1,0:T(8,128)(2,1)S(1)}, u32[]{:S(2)}, u32[]{:S(2)}) collective-permute-start(bf16[4128,128]{1,0:T(8,128)(2,1)S(1)} %get-tuple-element.38), channel_id=1, source_target_pairs={{0,48},{16,0},{32,16},{48,32},{64,112},{80,64},{96,80},{112,96},{1... | collective-permute-start | bytes 3170312 | tf_op jit(solution)/shard_map/ppermute | solution.py:556
  51.3 45.6 %collective-permute-start.7 = (bf16[4128,128]{1,0:T(8,128)(2,1)S(1)}, bf16[4128,128]{1,0:T(8,128)(2,1)S(1)}, u32[]{:S(2)}, u32[]{:S(2)}) collective-permute-start(bf16[4128,128]{1,0:T(8,128)(2,1)S(1)} %get-tuple-element.38), channel_id=1, source_target_pairs={{0,16},{16,32},{32,48},{48,0},{64,80},{80,96},{96,112},{112,64},{1... | collective-permute-start | bytes 3170312 | tf_op jit(solution)/shard_map/ppermute | solution.py:556
  52.1 39.7 %collective-permute-start.6 = (bf16[1024,128]{1,0:T(8,128)(2,1)S(1)}, bf16[1024,128]{1,0:T(8,128)(2,1)S(1)}, u32[]{:S(2)}, u32[]{:S(2)}) collective-permute-start(bf16[1024,128]{1,0:T(8,128)(2,1)S(1)} %copy-done.22), channel_id=1, source_target_pairs={{0,64},{16,80},{32,96},{48,112},{64,0},{80,16},{96,32},{112,48},{1... | collective-permute-start | bytes 786440 | tf_op jit(solution)/shard_map/ppermute | solution.py:571
  91.8 11.1 %copy-start.11 = (bf16[1024,128]{1,0:T(8,128)(2,1)}, bf16[1024,128]{1,0:T(8,128)(2,1)S(1)}, u32[]{:S(2)}) copy-start(bf16[1024,128]{1,0:T(8,128)(2,1)S(1)} %collective-permute-done.6.away_ref) | copy-start | bytes 786436
  91.8 5.1 %copy-start.19 = (bf16[4128,128]{1,0:T(8,128)(2,1)}, bf16[4128,128]{1,0:T(8,128)(2,1)S(1)}, u32[]{:S(2)}) copy-start(bf16[4128,128]{1,0:T(8,128)(2,1)S(1)} %collective-permute-done.9.refs_4_) | copy-start | bytes 3170308
  96.9 1.0 copy-start.20
  96.9 1.3 copy-start.21
  98.2 1.2 copy-start.14
  99.4 1.6 copy-start.6
  101.0 2.1 copy-start.18
  103.7 1.0 copy-start.12
  104.6 0.9 copy-start.13
  105.6 21.4 %copy-start.8 = (bf16[1024,128]{1,0:T(8,128)(2,1)S(1)}, bf16[1024,128]{1,0:T(8,128)(2,1)}, u32[]{:S(2)}) copy-start(bf16[1024,128]{1,0:T(8,128)(2,1)} %q_ref.3) | copy-start | bytes 786436
  124.4 13.4 %collective-permute-start.10 = (bf16[1024,128]{1,0:T(8,128)(2,1)}, bf16[1024,128]{1,0:T(8,128)(2,1)S(1)}, u32[]{:S(2)}, u32[]{:S(2)}) collective-permute-start(bf16[1024,128]{1,0:T(8,128)(2,1)} %get-tuple-element.40), channel_id=1, source_target_pairs={{0,64},{16,80},{32,96},{48,112},{64,0},{80,16},{96,32},{112,48},{1... | collective-permute-start | bytes 786440 | tf_op jit(solution)/shard_map/ppermute | solution.py:590
  137.8 0.7 copy-start.15
  146.5 26.8 %collective-permute-start.11 = (bf16[8,1024,256]{2,1,0:T(8,128)(2,1)}, bf16[8,1024,256]{2,1,0:T(8,128)(2,1)}, u32[]{:S(2)}, u32[]{:S(2)}) collective-permute-start(bf16[8,1024,256]{2,1,0:T(8,128)(2,1)} %project_mismatch.2), channel_id=1, source_target_pairs={{0,2},{2,0},{1,3},{3,1},{4,6},{6,4},{5,7},{7,5},{8,10},{10,8},{9,1... | collective-permute-start | bytes 12582920 | tf_op jit(solution)/shard_map/ppermute | solution.py:603
  147.2 1.4 copy-start.2
  153.6 4.4 %collective-permute-start.12 = (bf16[8,1024,128]{2,1,0:T(8,128)(2,1)S(1)}, bf16[8,1024,128]{2,1,0:T(8,128)(2,1)S(1)}, u32[]{:S(2)}, u32[]{:S(2)}) collective-permute-start(bf16[8,1024,128]{2,1,0:T(8,128)(2,1)S(1)} %project_grad.2), channel_id=1, source_target_pairs={{0,2},{2,0},{1,3},{3,1},{4,6},{6,4},{5,7},{7,5},{8,10},{10,8},{9,1... | collective-permute-start | bytes 6291464 | tf_op jit(solution)/shard_map/ppermute | solution.py:600
  164.5 35.1 %all-to-all-start.1 = ((bf16[8,1024,128]{2,1,0:T(8,128)(2,1)}), bf16[8,1024,128]{2,1,0:T(8,128)(2,1)}, u32[]{:S(2)}, u32[]{:S(2)}) async-start(bf16[8,1024,128]{2,1,0:T(8,128)(2,1)} %project_grad.3), calls=%async_computation.1 | async-start | bytes 4194304 | tf_op jit(solution)/shard_map/all_to_all | solution.py:602
  199.7 62.4 %all-to-all-start = ((bf16[8,1024,256]{2,1,0:T(8,128)(2,1)}), bf16[8,1024,256]{2,1,0:T(8,128)(2,1)}, u32[]{:S(2)}, u32[]{:S(2)}) async-start(bf16[8,1024,256]{2,1,0:T(8,128)(2,1)} %project_mismatch.3), calls=%async_computation | async-start | bytes 8388608 | tf_op jit(solution)/shard_map/all_to_all | solution.py:605
  221.0 28.6 %collective-permute-start.13 = (bf16[2048,128]{1,0:T(8,128)(2,1)S(1)}, bf16[2048,128]{1,0:T(8,128)(2,1)S(1)}, u32[]{:S(2)}, u32[]{:S(2)}) collective-permute-start(bf16[2048,128]{1,0:T(8,128)(2,1)S(1)} %get-tuple-element.45), channel_id=1, source_target_pairs={{16,0},{32,16},{48,32},{64,112},{80,64},{96,80},{112,96},{17,1},{3... | collective-permute-start | bytes 1572872 | tf_op jit(solution)/shard_map/ppermute | solution.py:621
  228.1 26.8 %collective-permute-start.14 = (bf16[2048,128]{1,0:T(8,128)(2,1)S(1)}, bf16[2048,128]{1,0:T(8,128)(2,1)S(1)}, u32[]{:S(2)}, u32[]{:S(2)}) collective-permute-start(bf16[2048,128]{1,0:T(8,128)(2,1)S(1)} %get-tuple-element.46), channel_id=1, source_target_pairs={{48,0},{64,80},{80,96},{96,112},{112,64},{49,1},{65,81},{81,97},{9... | collective-permute-start | bytes 1572872 | tf_op jit(solution)/shard_map/ppermute | solution.py:621
  230.0 24.9 %collective-permute-start.15 = (bf16[2048,128]{1,0:T(8,128)(2,1)S(1)}, bf16[2048,128]{1,0:T(8,128)(2,1)S(1)}, u32[]{:S(2)}, u32[]{:S(2)}) collective-permute-start(bf16[2048,128]{1,0:T(8,128)(2,1)S(1)} %get-tuple-element.47), channel_id=1, source_target_pairs={{32,0},{48,16},{64,96},{80,112},{96,64},{112,80},{33,1},{49,17},{6... | collective-permute-start | bytes 1572872 | tf_op jit(solution)/shard_map/ppermute | solution.py:621
  255.2 0.8 copy-start.17
  256.0 12.6 %collective-permute-start.17 = (bf16[2048,128]{1,0:T(8,128)(2,1)}, bf16[2048,128]{1,0:T(8,128)(2,1)S(1)}, u32[]{:S(2)}, u32[]{:S(2)}) collective-permute-start(bf16[2048,128]{1,0:T(8,128)(2,1)} %get-tuple-element.53), channel_id=1, source_target_pairs={{80,64},{96,80},{112,96},{81,65},{97,81},{113,97},{82,66},{98,82},... | collective-permute-start | bytes 1572872 | tf_op jit(solution)/shard_map/ppermute | solution.py:627
  257.3 25.1 %collective-permute-start.18 = (bf16[2048,128]{1,0:T(8,128)(2,1)}, bf16[2048,128]{1,0:T(8,128)(2,1)}, u32[]{:S(2)}, u32[]{:S(2)}) collective-permute-start(bf16[2048,128]{1,0:T(8,128)(2,1)} %get-tuple-element.54), channel_id=1, source_target_pairs={{112,64},{113,65},{114,66},{115,67},{116,68},{117,69},{118,70},{11... | collective-permute-start | bytes 1572872 | tf_op jit(solution)/shard_map/ppermute | solution.py:627
  258.6 23.8 %copy-start.7 = (bf16[2048,128]{1,0:T(8,128)(2,1)S(1)}, bf16[2048,128]{1,0:T(8,128)(2,1)}, u32[]{:S(2)}) copy-start(bf16[2048,128]{1,0:T(8,128)(2,1)} %get-tuple-element.52.refs_5_) | copy-start | bytes 1572868
  258.6 23.8 %collective-permute-start.19 = (bf16[2048,128]{1,0:T(8,128)(2,1)}, bf16[2048,128]{1,0:T(8,128)(2,1)}, u32[]{:S(2)}, u32[]{:S(2)}) collective-permute-start(bf16[2048,128]{1,0:T(8,128)(2,1)} %get-tuple-element.55), channel_id=1, source_target_pairs={{96,64},{112,80},{97,65},{113,81},{98,66},{114,82},{99,67},{115,83... | collective-permute-start | bytes 1572872 | tf_op jit(solution)/shard_map/ppermute | solution.py:627
  260.0 22.4 %collective-permute-start.16 = (bf16[2048,128]{1,0:T(8,128)(2,1)}, bf16[2048,128]{1,0:T(8,128)(2,1)}, u32[]{:S(2)}, u32[]{:S(2)}) collective-permute-start(bf16[2048,128]{1,0:T(8,128)(2,1)} %copy-done.17), channel_id=1, source_target_pairs={{64,0},{80,16},{96,32},{112,48},{65,1},{81,17},{97,33},{113,49},{6... | collective-permute-start | bytes 1572872 | tf_op jit(solution)/shard_map/ppermute | solution.py:625
Sparse Core Ops, SparseCore 0:
  11.2 49.8 all-gather.2
  103.1 43.2 all-gather.4

commit v4 on v3

--- a/solution.py
+++ b/solution.py
@@ -83,10 +83,13 @@
 WITH_COUNTS = KEYS + [pltpu.VMEM((8 * COUNTS, HD), bf16), pltpu.SemaphoreType.DMA((24,))]
 
 
-def teacher_kernel(meta, away_ref, here_ref, *refs):
-    blocks = blocks_of(refs[:-6])
-    away_out, here_out, key_all, value_all, counts, sems = refs[-6:]
+def teacher_kernel(meta, here_ref, *refs):
+    blocks = blocks_of(refs[:-8])
+    away_out, here_out, key_all, value_all, counts, sems, away_ref, away_sem = refs[-8:]
+    away_copy = pltpu.make_async_copy(refs[1].at[pl.ds(SPAN, BLOCK)], away_ref, away_sem)
+    away_copy.start()
     load(blocks, key_all, value_all, counts, sems)
+    away_copy.wait()
     border = border_of(counts)
     per_block = BLOCK // TILE_K
 
@@ -147,19 +150,19 @@
     one_block(here_ref, here_out, meta[0])
 
 
-def teacher_attention(meta, away, here, kv_blocks):
+def teacher_attention(meta, here, kv_blocks):
     return pl.pallas_call(
         teacher_kernel,
-        in_specs=[pl.BlockSpec(memory_space=SMEM), VMEM, VMEM] + [ANY] * len(kv_blocks),
+        in_specs=[pl.BlockSpec(memory_space=SMEM), VMEM] + [ANY] * len(kv_blocks),
         out_specs=[pl.BlockSpec((BLOCK, HD), lambda: (0, 0))] * 2,
         out_shape=[pltpu.HBM((BLOCK, HD), bf16)] * 2,
-        scratch_shapes=WITH_COUNTS,
+        scratch_shapes=WITH_COUNTS + [pltpu.VMEM((BLOCK, HD), bf16), pltpu.SemaphoreType.DMA],
         compiler_params=pltpu.CompilerParams(vmem_limit_bytes=24 << 20),
         cost_estimate=pl.CostEstimate(
             flops=8 * 4 * BLOCK * BLOCK * HD, bytes_accessed=5 << 20, transcendentals=8 * BLOCK * BLOCK
         ),
         name="teacher_attention",
-    )(meta, away, here, *kv_blocks)
+    )(meta, here, *kv_blocks)
 
 
 def chosen_rows(sel, row, table):
@@ -398,8 +401,8 @@
 
 
 def pack_kernel(at, seg_ref, tq_ref, tk_ref, tv_ref, sk_ref, sv_ref, so_ref, *refs):
-    outs, stages, sems = refs[:6], refs[6:12], refs[12]
-    s_own, t_sent, q_sent, rows, q_own, t_own = stages
+    outs, stages, sems = refs[:5], refs[5:10], refs[10]
+    s_own, t_sent, rows, q_own, t_own = stages
     near = pl.ds(pl.multiple_of(at[0] * HD, HD), HD)
     other = pl.ds(pl.multiple_of((1 - at[0]) * HD, HD), HD)
     started = 0
@@ -413,13 +416,20 @@
 
     keys, values, last = pl.ds(0, BLOCK), pl.ds(BLOCK, BLOCK), pl.ds(2 * BLOCK, COUNTS)
     part = pl.ds(pl.multiple_of(at[1] * COUNTS, COUNTS), COUNTS)
+    more = pl.ds(SPAN, BLOCK)
     coming = (
         (0, [move(sk_ref, s_own.at[keys]), move(sv_ref, s_own.at[values])]),
-        (1, [move(tk_ref.at[:, other], t_sent.at[keys]), move(tv_ref.at[:, other], t_sent.at[values])]),
-        (2, [move(tq_ref.at[:, other], q_sent)]),
-        (3, [move(so_ref.at[part], rows)]),
-        (5, [move(tk_ref.at[:, near], t_own.at[keys]), move(tv_ref.at[:, near], t_own.at[values])]),
-        (4, [move(tq_ref.at[:, near], q_own)]),
+        (
+            1,
+            [
+                move(tk_ref.at[:, other], t_sent.at[keys]),
+                move(tv_ref.at[:, other], t_sent.at[values]),
+                move(tq_ref.at[:, other], t_sent.at[more]),
+            ],
+        ),
+        (2, [move(so_ref.at[part], rows)]),
+        (4, [move(tk_ref.at[:, near], t_own.at[keys]), move(tv_ref.at[:, near], t_own.at[values])]),
+        (3, [move(tq_ref.at[:, near], q_own)]),
     )
     found = jnp.sum((seg_ref[...] == 0).astype(f32), axis=0, keepdims=True)
     first = lax.broadcasted_iota(jnp.int32, (COUNTS, HD), 0) == 0
@@ -437,13 +447,14 @@
 
 def pack(at, seg, *arrays):
     short = (BLOCK, HD)
-    shapes = [(SPAN, HD)] * 2 + [short, (COUNTS, arrays[-1].shape[1]), short, (SPAN, HD)]
+    span = (SPAN, HD)
+    shapes = [span, (SPAN + BLOCK, HD), (COUNTS, arrays[-1].shape[1]), short, span]
     return pl.pallas_call(
         pack_kernel,
         in_specs=[pl.BlockSpec(memory_space=SMEM), VMEM] + [FAR] * 6,
-        out_specs=[FAR] * 6,
+        out_specs=[FAR] * 5,
         out_shape=[pltpu.HBM(shape, bf16) for shape in shapes],
-        scratch_shapes=[pltpu.VMEM(shape, bf16) for shape in shapes] + [pltpu.SemaphoreType.DMA((15,))],
+        scratch_shapes=[pltpu.VMEM(shape, bf16) for shape in shapes] + [pltpu.SemaphoreType.DMA((14,))],
         compiler_params=pltpu.CompilerParams(vmem_limit_bytes=12 << 20),
         cost_estimate=pl.CostEstimate(flops=0, bytes_accessed=5 << 20, transcendentals=0),
         name="pack",
@@ -454,7 +465,7 @@
     target, sem = refs[-3], refs[-1]
     copy = pltpu.make_async_copy(kept_ref, target.at[pl.ds(0, SPAN)], sem)
     copy.start()
-    target[SPAN:, :] = refs[0][...]
+    target[SPAN:, :] = refs[0][:SPAN, :]
     for k, ref in enumerate(refs[1:4]):
         refs[-2][k * SPAN : (k + 1) * SPAN, :] = ref[...]
     copy.wait()
@@ -558,7 +569,7 @@
 
     to_partner = [(i, i ^ 4) for i in range(8)]
     at_x = jnp.stack([x, mine]).astype(jnp.int32)
-    s_own, t_sent, q_sent, rows, q_own, t_own = pack(
+    s_own, t_sent, rows, q_own, t_own = pack(
         at_x, segments.reshape(8, HD), t_query, t_key, t_value, s_key, s_value, s_out
     )
     up = [(i, i + 4) for i in range(4)]
@@ -568,11 +579,6 @@
     t_two, s_three = repack(t_own, t_got, s_near, (token(s_low),))
     t_near = along_y(t_two, (0, 1), ())
     s_lows = lax.ppermute(s_three, BLK, up)
-    q_got = lax.ppermute(q_sent, BLK, to_partner)
-
-    rows = lax.all_gather(rows, GROUP, axis=0, tiled=True)
-    through = compose(rows, s_out, t_out, (token(*t_near, s_lows, q_got),))
-    through = lax.all_gather(through, BLK, axis=0, tiled=True).reshape(8, 16, HD // 8, 3 * HD)
 
     def place_of(block):
         step = (block + 4 - y) % 4
@@ -585,11 +591,16 @@
     k_pos = (selection[:, :, None] * BS + jnp.arange(BS, dtype=jnp.int32)).reshape(-1, 1, NSEL * BS)
     s_meta = jnp.stack([mine, x]).astype(jnp.int32)
 
-    t_blocks = tuple(map(far, (t_own, t_got, *t_near)))
-    away, here = teacher_attention(t_meta, q_got, q_own, t_blocks)
-    back = lax.ppermute(away, BLK, to_partner)
     s_blocks = tuple(map(far, (s_own, *s_near, s_low, s_lows)))
     s_attn, weights = student_forward(s_meta, sel, s_query, k_pos, s_blocks)
+
+    rows = lax.all_gather(rows, GROUP, axis=0, tiled=True)
+    through = compose(rows, s_out, t_out, (token(*t_near, s_attn),))
+    through = lax.all_gather(through, BLK, axis=0, tiled=True).reshape(8, 16, HD // 8, 3 * HD)
+
+    t_blocks = tuple(map(far, (t_own, t_got, *t_near)))
+    away, here = teacher_attention(t_meta, q_own, t_blocks)
+    back = lax.ppermute(away, BLK, to_partner)
     attn = (s_attn, here, back)
 
     this = jnp.stack([core, x]).astype(jnp.int32)

time: 294 us -> 297 us (1.010); the launches traced: 292 us -> 299 us
  waiting for transfers between devices: 119 us -> 126 us
    ppermute x1 -> x0, waiting for transfers between devices: 37 us -> none  [on_device(): q_got = lax.ppermute(q_sent, BLK, to_partner)]
    ppermute x1, waiting for transfers between devices: 0.01 us -> 31.7 us  [on_device(): s_lows = lax.ppermute(s_three, BLK, up)]
    ppermute x1, waiting for transfers between devices: 5.9 us -> 21.7 us  [on_device(): s_low = lax.ppermute(s_own, BLK, up)]
    ppermute x1, waiting for transfers between devices: 0.7 us -> 12.1 us  [on_device(): back = lax.ppermute(away, BLK, to_partner)]
    ppermute x1, waiting for transfers between devices: 10.2 us -> 0.01 us  [on_device(): t_got = lax.ppermute(t_sent, BLK, to_partner)]
    ppermute x3, starting transfers between devices: 12.4 us -> 20.6 us  [on_device(): low[j] = lax.ppermute(low[j], BLK, earlier(shift, (1,), (0,)))]
    ppermute x6, waiting for transfers between devices: 8.07 us -> 1.49 us  [along_y(): lax.ppermute(block, BLK, y_pairs(shift, all_x, causal_x))]
    unnamed x46 -> x32, local copies, waits for them, and re-layouts: 9.77 us -> 6.96 us
  transfers between devices with their start and end apart: 24 -> 23, of which waited for: 12 -> 11; matrix products, arithmetic and copies ran while one was open for 1% -> 1% of each run, Pallas kernels for 27% -> 26%
where the time goes in v4:
time: 297 us; the launch traced here: 299 us
  waiting for transfers between devices  126 us (42%)
  Pallas kernels  85.2 us (29%)
  starting transfers between devices  62.1 us (21%)
  between operations  14.4 us (5%)
  local copies, waits for them, and re-layouts  9.41 us (3%)
    ppermute x1, waiting for transfers between devices, on_device(): s_lows = lax.ppermute(s_three, BLK, up)  31.7 us
    pallas_call x4, Pallas kernels, project(): pl.pallas_call(kernel, grid_spec=pltpu.PrefetchScalarGridSpec(num_scalar_...  28.9 us
    ppermute x1, waiting for transfers between devices, on_device(): s_low = lax.ppermute(s_own, BLK, up)  21.7 us
    ppermute x3, waiting for transfers between devices, on_device(): low[j] = lax.ppermute(low[j], BLK, earlier(shift, (1,), (0,)))  21.5 us
    ppermute x3, starting transfers between devices, on_device(): low[j] = lax.ppermute(low[j], BLK, earlier(shift, (1,), (0,)))  20.6 us
    pallas_call x1, Pallas kernels, teacher_attention(): pl.pallas_call(teacher_kernel, in_specs=[pl.BlockSpec(memory_space=SMEM),...  17.9 us
    all_to_all x1, waiting for transfers between devices, on_device(): grad = lax.all_to_all(grad, ZX, 0, 0, tiled=True)  16.7 us
    ppermute x3, waiting for transfers between devices, on_device(): high[j] = lax.ppermute(high[j], BLK, earlier(shift, (), (1,)))  15.3 us
  transfers between devices with their start and end apart: 23, of which 11 were waited for; matrix products, arithmetic and copies ran while one was open for 1% of the time, Pallas kernels for 26%

profile of v4, /device:TPU:6, one launch (start us, length us, event | category | flops | bytes accessed | tf_op | source)
XLA Modules:
  0.0 298.7 jit_solution(1995529550662686666)
XLA Ops:
  7.2 0.1 pad_add_fusion.2.at
  7.3 0.7 copy-done.11
  8.0 3.1 %pack.1 = (bf16[2064,128]{1,0:T(8,128)(2,1)}, bf16[3088,128]{1,0:T(8,128)(2,1)}, bf16[16,4096]{1,0:T(8,128)(2,1)}, bf16[1024,128]{1,0:T(8,128)(2,1)}, bf16[2064,128]{1,0:T(8,128)(2,1)}) custom-call(s32[2]{0:T(128)S(1)} %pad_add_fusion.2.at, s32[8,128]{1,0:T(8,128)S(1)} %bitcast.11, bf16[1024,256]{1,0:T(8,128)(2,1)} %tq_ref.1, bf16[1024,256]{1,0:T(8,128)(2,1)} %tk_ref.1, ...), custom_call_target="tpu_custom_call" | custom-call | bytes 5242880 | tf_op jit(solution)/shard_map/pack/pallas_call | solution.py:452
  11.2 0.9 collective-permute-start.4
  12.1 1.3 collective-permute-start.3
  13.4 5.1 %collective-permute-start.2 = (bf16[2064,128]{1,0:T(8,128)(2,1)}, bf16[2064,128]{1,0:T(8,128)(2,1)S(1)}, u32[]{:S(2)}, u32[]{:S(2)}) collective-permute-start(bf16[2064,128]{1,0:T(8,128)(2,1)} %get-tuple-element.30.refs_0_), channel_id=1, source_target_pairs={{0,32},{16,48},{32,0},{48,16},{64,96},{80,112},{1,33},{17,49},{33,... | collective-permute-start | bytes 1585160 | tf_op jit(solution)/shard_map/ppermute | solution.py:567
  18.5 1.3 collective-permute-start.1
  19.9 2.0 collective-permute-start
  21.9 21.7 %collective-permute-done.3.refs_4_ = bf16[2064,128]{1,0:T(8,128)(2,1)S(1)} collective-permute-done((bf16[2064,128]{1,0:T(8,128)(2,1)}, bf16[2064,128]{1,0:T(8,128)(2,1)S(1)}, u32[]{:S(2)}, u32[]{:S(2)}) %collective-permute-start.3) | collective-permute-done | bytes 528416 | tf_op jit(solution)/shard_map/ppermute | solution.py:578
  43.6 3.0 %repack.1 = (bf16[4128,128]{1,0:T(8,128)(2,1)}, bf16[6192,128]{1,0:T(8,128)(2,1)}) custom-call(bf16[2064,128]{1,0:T(8,128)(2,1)} %get-tuple-element.31.kept_ref.refs_0_, bf16[3088,128]{1,0:T(8,128)(2,1)S(1)} %collective-permute-done.4.refs_0_.refs_1_, bf16[2064,128]{1,0:T(8,128)(2,1)S(1)} %collective-permute-done.refs_1_, ...), custom_call_target="tpu_custom_call" | custom-call | bytes 5242880 | tf_op jit(solution)/shard_map/repack/pallas_call | solution.py:475
  46.7 0.8 copy-done.3
  47.5 1.3 collective-permute-start.5
  48.8 3.3 %collective-permute-start.8 = (bf16[4128,128]{1,0:T(8,128)(2,1)}, bf16[4128,128]{1,0:T(8,128)(2,1)}, u32[]{:S(2)}, u32[]{:S(2)}) collective-permute-start(bf16[4128,128]{1,0:T(8,128)(2,1)} %get-tuple-element.36), channel_id=1, source_target_pairs={{0,32},{16,48},{32,0},{48,16},{64,96},{80,112},{96,64},{112,80},{1... | collective-permute-start | bytes 3170312 | tf_op jit(solution)/shard_map/ppermute | solution.py:567
  52.1 1.1 collective-permute-start.7
  53.1 1.0 collective-permute-start.6
  54.1 0.1 add.101
  54.2 0.1 reshape.54.sel
  54.3 0.1 add.98
  54.4 0.1 add.99
  54.5 0.1 pad_add_fusion.1.meta
  54.7 31.7 %collective-permute-done.5.refs_5_ = bf16[6192,128]{1,0:T(8,128)(2,1)} collective-permute-done((bf16[6192,128]{1,0:T(8,128)(2,1)}, bf16[6192,128]{1,0:T(8,128)(2,1)}, u32[]{:S(2)}, u32[]{:S(2)}) %collective-permute-start.5) | collective-permute-done | bytes 1585184 | tf_op jit(solution)/shard_map/ppermute | solution.py:581
  86.4 10.0 %student_forward.1 = (bf16[1024,128]{1,0:T(8,128)(2,1)}, f32[1024,1024]{1,0:T(8,128)}) custom-call(s32[2]{0:T(128)S(1)} %pad_add_fusion.1.meta, s32[256]{0:T(256)S(1)} %reshape.54.sel, bf16[1024,128]{1,0:T(8,128)(2,1)S(1)} %copy-done.8, s32[16,1,1024]{2,1,0:T(1,128)S(1)} %broadcast_add_fusion.kpos_ref, bf16[2064,128]{1,0:T(8,128)(2,1)} %get-tuple-element.30.refs_0_, ...), custom_call_target="tpu_custom_call" | custom-call | flops 536870912 | bytes 9437184 | tf_op jit(solution)/shard_map/student_forward/pallas_call | solution.py:207
  96.4 1.5 collective-permute-done.7.refs_3_
  97.9 0.7 fusion.7.refs_0_
  98.6 1.6 copy-done.6
  100.2 1.2 compose.1
  101.5 0.7 copy-done.10
  102.2 0.1 concatenate.3.meta
  102.3 1.0 copy-done.12
  103.3 17.9 %teacher_attention.1 = (bf16[1024,128]{1,0:T(8,128)(2,1)}, bf16[1024,128]{1,0:T(8,128)(2,1)}) custom-call(s32[16]{0:T(128)S(1)} %concatenate.3.meta, bf16[1024,128]{1,0:T(8,128)(2,1)S(1)} %copy-done.12, bf16[2064,128]{1,0:T(8,128)(2,1)} %get-tuple-element.31.kept_ref.refs_0_, bf16[3088,128]{1,0:T(8,128)(2,1)} %copy-done.9, ...), custom_call_target="tpu_custom_call" | custom-call | flops 4294967296 | bytes 5242880 | tf_op jit(solution)/shard_map/teacher_attention/pallas_call | solution.py:154
  121.2 3.5 %collective-permute-start.9 = (bf16[1024,128]{1,0:T(8,128)(2,1)}, bf16[1024,128]{1,0:T(8,128)(2,1)}, u32[]{:S(2)}, u32[]{:S(2)}) collective-permute-start(bf16[1024,128]{1,0:T(8,128)(2,1)} %get-tuple-element.38), channel_id=1, source_target_pairs={{0,64},{16,80},{32,96},{48,112},{64,0},{80,16},{96,32},{112,48},{1... | collective-permute-start | bytes 786440 | tf_op jit(solution)/shard_map/ppermute | solution.py:603
  124.7 0.1 pad_add_fusion.3.at
  124.8 12.1 %collective-permute-done.9.b_ref = bf16[1024,128]{1,0:T(8,128)(2,1)} collective-permute-done((bf16[1024,128]{1,0:T(8,128)(2,1)}, bf16[1024,128]{1,0:T(8,128)(2,1)}, u32[]{:S(2)}, u32[]{:S(2)}) %collective-permute-start.9) | collective-permute-done | bytes 262176 | tf_op jit(solution)/shard_map/ppermute | solution.py:603
  136.9 8.0 %project_mismatch.2 = bf16[8,1024,256]{2,1,0:T(8,128)(2,1)} custom-call(s32[2]{0:T(128)S(1)} %pad_add_fusion.3.at, bf16[1024,128]{1,0:T(8,128)(2,1)} %get-tuple-element.34.s_ref, bf16[1024,128]{1,0:T(8,128)(2,1)} %get-tuple-element.37.a_ref, bf16[1024,128]{1,0:T(8,128)(2,1)} %collective-permute-done.9.b_ref, bf16[128,4096]{1,0:T(8,128)(2,1)S(1)} %copy-done.1, ...), custom_call_target="tpu_custom_call" | custom-call | flops 1610612736 | bytes 6291456 | tf_op jit(solution)/shard_map/project_mismatch/pallas_call | solution.py:356
  144.9 0.7 slice_bitcast_fusion.refs_1_
  145.6 1.6 all-gather.5.cloned.1.call-done
  147.2 1.4 copy-done.2
  148.6 5.0 %project_grad.2 = bf16[8,1024,128]{2,1,0:T(8,128)(2,1)S(1)} custom-call(s32[2]{0:T(128)S(1)} %pad_add_fusion.3.at, bf16[1024,128]{1,0:T(8,128)(2,1)} %get-tuple-element.34.s_ref, bf16[1024,128]{1,0:T(8,128)(2,1)} %get-tuple-element.37.a_ref, bf16[1024,128]{1,0:T(8,128)(2,1)} %collective-permute-done.9.b_ref, bf16[8,16,16,384]{3,2,1,0:T(8,128)(2,1)S(1)} %bitcast.9, ...), custom_call_target="tpu_custom_call" | custom-call | flops 805306368 | bytes 4194304 | tf_op jit(solution)/shard_map/project_grad/pallas_call | solution.py:356
  153.6 0.1 collective-permute-start.11
  153.7 0.1 pad_add_fusion.at
  153.7 4.1 %collective-permute-done.11.refs_1_ = bf16[8,1024,128]{2,1,0:T(8,128)(2,1)S(1)} collective-permute-done((bf16[8,1024,128]{2,1,0:T(8,128)(2,1)S(1)}, bf16[8,1024,128]{2,1,0:T(8,128)(2,1)S(1)}, u32[]{:S(2)}, u32[]{:S(2)}) %collective-permute-start.11) | collective-permute-done | bytes 2097184 | tf_op jit(solution)/shard_map/ppermute | solution.py:611
  157.8 6.5 %project_grad.3 = bf16[8,1024,128]{2,1,0:T(8,128)(2,1)} custom-call(s32[2]{0:T(128)S(1)} %pad_add_fusion.at, bf16[1024,128]{1,0:T(8,128)(2,1)} %get-tuple-element.34.s_ref, bf16[1024,128]{1,0:T(8,128)(2,1)} %get-tuple-element.37.a_ref, bf16[1024,128]{1,0:T(8,128)(2,1)} %collective-permute-done.9.b_ref, bf16[8,16,16,384]{3,2,1,0:T(8,128)(2,1)S(1)} %bitcast.10, ...), custom_call_target="tpu_custom_call" | custom-call | flops 805306368 | bytes 6291456 | tf_op jit(solution)/shard_map/project_grad/pallas_call | solution.py:356
  164.3 7.4 %all-to-all-start.1 = ((bf16[8,1024,128]{2,1,0:T(8,128)(2,1)}), bf16[8,1024,128]{2,1,0:T(8,128)(2,1)}, u32[]{:S(2)}, u32[]{:S(2)}) async-start(bf16[8,1024,128]{2,1,0:T(8,128)(2,1)} %project_grad.3), calls=%async_computation.1 | async-start | bytes 4194304 | tf_op jit(solution)/shard_map/all_to_all | solution.py:613
  171.6 9.5 %project_mismatch.3 = bf16[8,1024,256]{2,1,0:T(8,128)(2,1)} custom-call(s32[2]{0:T(128)S(1)} %pad_add_fusion.at, bf16[1024,128]{1,0:T(8,128)(2,1)} %get-tuple-element.34.s_ref, bf16[1024,128]{1,0:T(8,128)(2,1)} %get-tuple-element.37.a_ref, bf16[1024,128]{1,0:T(8,128)(2,1)} %collective-permute-done.9.b_ref, bf16[128,4096]{1,0:T(8,128)(2,1)S(1)} %copy-done.1, ...), custom_call_target="tpu_custom_call" | custom-call | flops 1610612736 | bytes 10485760 | tf_op jit(solution)/shard_map/project_mismatch/pallas_call | solution.py:356
  181.1 16.7 %all-to-all-done.1.g_ref = bf16[8,1024,128]{2,1,0:T(8,128)(2,1)} async-done(((bf16[8,1024,128]{2,1,0:T(8,128)(2,1)}), bf16[8,1024,128]{2,1,0:T(8,128)(2,1)}, u32[]{:S(2)}, u32[]{:S(2)}) %all-to-all-start.1) | async-done | bytes 2097184 | tf_op jit(solution)/shard_map/all_to_all | solution.py:613
  197.8 7.2 %all-to-all-start = ((bf16[8,1024,256]{2,1,0:T(8,128)(2,1)}), bf16[8,1024,256]{2,1,0:T(8,128)(2,1)}, u32[]{:S(2)}, u32[]{:S(2)}) async-start(bf16[8,1024,256]{2,1,0:T(8,128)(2,1)} %project_mismatch.3), calls=%async_computation | async-start | bytes 8388608 | tf_op jit(solution)/shard_map/all_to_all | solution.py:616
  205.0 14.1 %student_backward.1 = (f32[1024,128]{1,0:T(8,128)}, bf16[2048,128]{1,0:T(8,128)(2,1)S(1)}, bf16[2048,128]{1,0:T(8,128)(2,1)S(1)}, bf16[2048,128]{1,0:T(8,128)(2,...) custom-call(s32[2]{0:T(128)S(1)} %pad_add_fusion.1.meta, ...), custom_call_target="tpu_custom_call" | custom-call | flops 1073741824 | bytes 15728640 | tf_op jit(solution)/shard_map/student_backward/pallas_call | solution.py:292
  219.1 15.3 %collective-permute-start.12 = (bf16[2048,128]{1,0:T(8,128)(2,1)S(1)}, bf16[2048,128]{1,0:T(8,128)(2,1)S(1)}, u32[]{:S(2)}, u32[]{:S(2)}) collective-permute-start(bf16[2048,128]{1,0:T(8,128)(2,1)S(1)} %get-tuple-element.43), channel_id=1, source_target_pairs={{16,0},{32,16},{48,32},{64,112},{80,64},{96,80},{112,96},{17,1},{3... | collective-permute-start | bytes 1572872 | tf_op jit(solution)/shard_map/ppermute | solution.py:632
  234.4 1.9 collective-permute-start.13
  236.3 3.4 %collective-permute-start.14 = (bf16[2048,128]{1,0:T(8,128)(2,1)S(1)}, bf16[2048,128]{1,0:T(8,128)(2,1)S(1)}, u32[]{:S(2)}, u32[]{:S(2)}) collective-permute-start(bf16[2048,128]{1,0:T(8,128)(2,1)S(1)} %get-tuple-element.45), channel_id=1, source_target_pairs={{32,0},{48,16},{64,96},{80,112},{96,64},{112,80},{33,1},{49,17},{6... | collective-permute-start | bytes 1572872 | tf_op jit(solution)/shard_map/ppermute | solution.py:632
  239.7 16.2 %collective-permute-done.12.refs_1_ = bf16[2048,128]{1,0:T(8,128)(2,1)S(1)} collective-permute-done((bf16[2048,128]{1,0:T(8,128)(2,1)S(1)}, bf16[2048,128]{1,0:T(8,128)(2,1)S(1)}, u32[]{:S(2)}, u32[]{:S(2)}) %collective-permute-start.12) | collective-permute-done | bytes 524320 | tf_op jit(solution)/shard_map/ppermute | solution.py:632
  255.9 5.3 %collective-permute-done.13.refs_2_ = bf16[2048,128]{1,0:T(8,128)(2,1)S(1)} collective-permute-done((bf16[2048,128]{1,0:T(8,128)(2,1)S(1)}, bf16[2048,128]{1,0:T(8,128)(2,1)S(1)}, u32[]{:S(2)}, u32[]{:S(2)}) %collective-permute-start.13) | collective-permute-done | bytes 524320 | tf_op jit(solution)/shard_map/ppermute | solution.py:632
  261.2 0.3 add_convert_fusion
  261.5 0.8 copy-done.14
  262.3 0.6 slice.39.refs_4_
  262.9 1.3 collective-permute-start.16
  264.2 1.3 collective-permute-start.17
  265.5 1.4 collective-permute-start.18
  266.9 2.1 collective-permute-start.15
  269.0 4.2 %add_pieces.1 = f32[1024,256]{1,0:T(8,128)} custom-call(bf16[8,1024,256]{2,1,0:T(8,128)(2,1)} %all-to-all-done.in_ref), custom_call_target="tpu_custom_call" | custom-call | flops 8388608 | bytes 5242880 | tf_op jit(solution)/shard_map/add_pieces/pallas_call | solution.py:516
  273.2 0.7 slice.40.refs_9_
  273.9 1.4 collective-permute-done.16.refs_6_
  275.4 13.9 %collective-permute-done.17.refs_7_ = bf16[2048,128]{1,0:T(8,128)(2,1)} collective-permute-done((bf16[2048,128]{1,0:T(8,128)(2,1)}, bf16[2048,128]{1,0:T(8,128)(2,1)}, u32[]{:S(2)}, u32[]{:S(2)}) %collective-permute-start.17) | collective-permute-done | bytes 524320 | tf_op jit(solution)/shard_map/ppermute | solution.py:638
  289.2 2.6 finish.1
  (50 shorter events, 0.3 us)
Async XLA Ops:
  7.2 91.5 %all-gather.3.cloned.1.call-start = ((), (), s32[]{:S(2)}) async-start(), calls=%async_computation.2 | async-start | bytes 2228224 | tf_op jit(solution)/shard_map/all_gather | solution.py:597
  7.3 0.7 copy-start.11
  11.1 43.1 %copy-start.15 = (s32[16,16]{1,0:T(8,128)S(1)}, s32[16,16]{1,0:T(8,128)}, u32[]{:S(2)}) copy-start(s32[16,16]{1,0:T(8,128)} %param.19) | copy-start | bytes 3076
  11.1 75.3 %copy-start.8 = (bf16[1024,128]{1,0:T(8,128)(2,1)S(1)}, bf16[1024,128]{1,0:T(8,128)(2,1)}, u32[]{:S(2)}) copy-start(bf16[1024,128]{1,0:T(8,128)(2,1)} %q_ref.3) | copy-start | bytes 786436
  11.1 136.0 %all-gather.5.cloned.1.call-start = ((), (), s32[]{:S(2)}) async-start(), calls=%async_computation.3 | async-start | bytes 1769472 | tf_op jit(solution)/shard_map/all_gather | solution.py:599
  11.2 32.4 %collective-permute-start.4 = (bf16[3088,128]{1,0:T(8,128)(2,1)}, bf16[3088,128]{1,0:T(8,128)(2,1)S(1)}, u32[]{:S(2)}, u32[]{:S(2)}) collective-permute-start(bf16[3088,128]{1,0:T(8,128)(2,1)} %get-tuple-element.32), channel_id=1, source_target_pairs={{0,64},{16,80},{32,96},{48,112},{64,0},{80,16},{96,32},{112,48},{1... | collective-permute-start | bytes 2371592 | tf_op jit(solution)/shard_map/ppermute | solution.py:577
  12.1 31.5 %collective-permute-start.3 = (bf16[2064,128]{1,0:T(8,128)(2,1)}, bf16[2064,128]{1,0:T(8,128)(2,1)S(1)}, u32[]{:S(2)}, u32[]{:S(2)}) collective-permute-start(bf16[2064,128]{1,0:T(8,128)(2,1)} %get-tuple-element.30.refs_0_), channel_id=1, source_target_pairs={{0,64},{16,80},{32,96},{48,112},{1,65},{17,81},{33,97},{49,113},{2... | collective-permute-start | bytes 1585160 | tf_op jit(solution)/shard_map/ppermute | solution.py:578
  13.4 30.2 %collective-permute-start.2 = (bf16[2064,128]{1,0:T(8,128)(2,1)}, bf16[2064,128]{1,0:T(8,128)(2,1)S(1)}, u32[]{:S(2)}, u32[]{:S(2)}) collective-permute-start(bf16[2064,128]{1,0:T(8,128)(2,1)} %get-tuple-element.30.refs_0_), channel_id=1, source_target_pairs={{0,32},{16,48},{32,0},{48,16},{64,96},{80,112},{1,33},{17,49},{33,... | collective-permute-start | bytes 1585160 | tf_op jit(solution)/shard_map/ppermute | solution.py:567
  18.5 25.1 %collective-permute-start.1 = (bf16[2064,128]{1,0:T(8,128)(2,1)}, bf16[2064,128]{1,0:T(8,128)(2,1)S(1)}, u32[]{:S(2)}, u32[]{:S(2)}) collective-permute-start(bf16[2064,128]{1,0:T(8,128)(2,1)} %get-tuple-element.30.refs_0_), channel_id=1, source_target_pairs={{0,48},{16,0},{32,16},{48,32},{64,112},{1,49},{17,1},{33,17},{49,3... | collective-permute-start | bytes 1585160 | tf_op jit(solution)/shard_map/ppermute | solution.py:567
  19.9 23.7 %collective-permute-start = (bf16[2064,128]{1,0:T(8,128)(2,1)}, bf16[2064,128]{1,0:T(8,128)(2,1)S(1)}, u32[]{:S(2)}, u32[]{:S(2)}) collective-permute-start(bf16[2064,128]{1,0:T(8,128)(2,1)} %get-tuple-element.30.refs_0_), channel_id=1, source_target_pairs={{0,16},{16,32},{32,48},{48,0},{64,80},{80,96},{96,112},{1,17},{17,... | collective-permute-start | bytes 1585160 | tf_op jit(solution)/shard_map/ppermute | solution.py:567
  43.6 5.2 %copy-start.13 = (bf16[2064,128]{1,0:T(8,128)(2,1)}, bf16[2064,128]{1,0:T(8,128)(2,1)S(1)}, u32[]{:S(2)}) copy-start(bf16[2064,128]{1,0:T(8,128)(2,1)S(1)} %collective-permute-done.3.refs_4_) | copy-start | bytes 1585156
  43.6 3.1 %copy-start.4 = (bf16[2064,128]{1,0:T(8,128)(2,1)}, bf16[2064,128]{1,0:T(8,128)(2,1)S(1)}, u32[]{:S(2)}) copy-start(bf16[2064,128]{1,0:T(8,128)(2,1)S(1)} %collective-permute-done.1.refs_2_) | copy-start | bytes 1585156
  43.6 3.9 %copy-start.5 = (bf16[2064,128]{1,0:T(8,128)(2,1)}, bf16[2064,128]{1,0:T(8,128)(2,1)S(1)}, u32[]{:S(2)}) copy-start(bf16[2064,128]{1,0:T(8,128)(2,1)S(1)} %collective-permute-done.refs_1_) | copy-start | bytes 1585156
  43.6 5.1 %copy-start.9 = (bf16[3088,128]{1,0:T(8,128)(2,1)}, bf16[3088,128]{1,0:T(8,128)(2,1)S(1)}, u32[]{:S(2)}) copy-start(bf16[3088,128]{1,0:T(8,128)(2,1)S(1)} %collective-permute-done.4.refs_0_.refs_1_) | copy-start | bytes 2371588
  46.7 0.8 copy-start.3
  47.5 38.9 %collective-permute-start.5 = (bf16[6192,128]{1,0:T(8,128)(2,1)}, bf16[6192,128]{1,0:T(8,128)(2,1)}, u32[]{:S(2)}, u32[]{:S(2)}) collective-permute-start(bf16[6192,128]{1,0:T(8,128)(2,1)} %get-tuple-element.33), channel_id=1, source_target_pairs={{0,64},{16,80},{32,96},{48,112},{1,65},{17,81},{33,97},{49,113},{2... | collective-permute-start | bytes 4755464 | tf_op jit(solution)/shard_map/ppermute | solution.py:581
  48.8 47.6 %collective-permute-start.8 = (bf16[4128,128]{1,0:T(8,128)(2,1)}, bf16[4128,128]{1,0:T(8,128)(2,1)}, u32[]{:S(2)}, u32[]{:S(2)}) collective-permute-start(bf16[4128,128]{1,0:T(8,128)(2,1)} %get-tuple-element.36), channel_id=1, source_target_pairs={{0,32},{16,48},{32,0},{48,16},{64,96},{80,112},{96,64},{112,80},{1... | collective-permute-start | bytes 3170312 | tf_op jit(solution)/shard_map/ppermute | solution.py:567
  52.1 45.9 %collective-permute-start.7 = (bf16[4128,128]{1,0:T(8,128)(2,1)}, bf16[4128,128]{1,0:T(8,128)(2,1)}, u32[]{:S(2)}, u32[]{:S(2)}) collective-permute-start(bf16[4128,128]{1,0:T(8,128)(2,1)} %get-tuple-element.36), channel_id=1, source_target_pairs={{0,48},{16,0},{32,16},{48,32},{64,112},{80,64},{96,80},{112,96},{1... | collective-permute-start | bytes 3170312 | tf_op jit(solution)/shard_map/ppermute | solution.py:567
  53.1 44.8 %collective-permute-start.6 = (bf16[4128,128]{1,0:T(8,128)(2,1)}, bf16[4128,128]{1,0:T(8,128)(2,1)}, u32[]{:S(2)}, u32[]{:S(2)}) collective-permute-start(bf16[4128,128]{1,0:T(8,128)(2,1)} %get-tuple-element.36), channel_id=1, source_target_pairs={{0,16},{16,32},{32,48},{48,0},{64,80},{80,96},{96,112},{112,64},{1... | collective-permute-start | bytes 3170312 | tf_op jit(solution)/shard_map/ppermute | solution.py:567
  54.6 44.0 %copy-start = (bf16[256,4096]{1,0:T(8,128)(2,1)S(1)}, bf16[256,4096]{1,0:T(8,128)(2,1)}, u32[]{:S(2)}) copy-start(bf16[256,4096]{1,0:T(8,128)(2,1)} %t_ref.1) | copy-start | bytes 6291460
  54.7 44.0 %copy-start.1 = (bf16[128,4096]{1,0:T(8,128)(2,1)S(1)}, bf16[128,4096]{1,0:T(8,128)(2,1)}, u32[]{:S(2)}) copy-start(bf16[128,4096]{1,0:T(8,128)(2,1)} %s_ref.1) | copy-start | bytes 3145732
  98.6 1.6 copy-start.6
  101.5 0.7 copy-start.10
  102.3 1.0 copy-start.12
  121.2 15.7 %collective-permute-start.9 = (bf16[1024,128]{1,0:T(8,128)(2,1)}, bf16[1024,128]{1,0:T(8,128)(2,1)}, u32[]{:S(2)}, u32[]{:S(2)}) collective-permute-start(bf16[1024,128]{1,0:T(8,128)(2,1)} %get-tuple-element.38), channel_id=1, source_target_pairs={{0,64},{16,80},{32,96},{48,112},{64,0},{80,16},{96,32},{112,48},{1... | collective-permute-start | bytes 786440 | tf_op jit(solution)/shard_map/ppermute | solution.py:603
  144.9 26.7 %collective-permute-start.10 = (bf16[8,1024,256]{2,1,0:T(8,128)(2,1)}, bf16[8,1024,256]{2,1,0:T(8,128)(2,1)}, u32[]{:S(2)}, u32[]{:S(2)}) collective-permute-start(bf16[8,1024,256]{2,1,0:T(8,128)(2,1)} %project_mismatch.2), channel_id=1, source_target_pairs={{0,2},{2,0},{1,3},{3,1},{4,6},{6,4},{5,7},{7,5},{8,10},{10,8},{9,1... | collective-permute-start | bytes 12582920 | tf_op jit(solution)/shard_map/ppermute | solution.py:614
  147.2 1.4 copy-start.2
  153.6 4.2 %collective-permute-start.11 = (bf16[8,1024,128]{2,1,0:T(8,128)(2,1)S(1)}, bf16[8,1024,128]{2,1,0:T(8,128)(2,1)S(1)}, u32[]{:S(2)}, u32[]{:S(2)}) collective-permute-start(bf16[8,1024,128]{2,1,0:T(8,128)(2,1)S(1)} %project_grad.2), channel_id=1, source_target_pairs={{0,2},{2,0},{1,3},{3,1},{4,6},{6,4},{5,7},{7,5},{8,10},{10,8},{9,1... | collective-permute-start | bytes 6291464 | tf_op jit(solution)/shard_map/ppermute | solution.py:611
  164.3 33.5 %all-to-all-start.1 = ((bf16[8,1024,128]{2,1,0:T(8,128)(2,1)}), bf16[8,1024,128]{2,1,0:T(8,128)(2,1)}, u32[]{:S(2)}, u32[]{:S(2)}) async-start(bf16[8,1024,128]{2,1,0:T(8,128)(2,1)} %project_grad.3), calls=%async_computation.1 | async-start | bytes 4194304 | tf_op jit(solution)/shard_map/all_to_all | solution.py:613
  197.8 71.2 %all-to-all-start = ((bf16[8,1024,256]{2,1,0:T(8,128)(2,1)}), bf16[8,1024,256]{2,1,0:T(8,128)(2,1)}, u32[]{:S(2)}, u32[]{:S(2)}) async-start(bf16[8,1024,256]{2,1,0:T(8,128)(2,1)} %project_mismatch.3), calls=%async_computation | async-start | bytes 8388608 | tf_op jit(solution)/shard_map/all_to_all | solution.py:616
  219.1 36.8 %collective-permute-start.12 = (bf16[2048,128]{1,0:T(8,128)(2,1)S(1)}, bf16[2048,128]{1,0:T(8,128)(2,1)S(1)}, u32[]{:S(2)}, u32[]{:S(2)}) collective-permute-start(bf16[2048,128]{1,0:T(8,128)(2,1)S(1)} %get-tuple-element.43), channel_id=1, source_target_pairs={{16,0},{32,16},{48,32},{64,112},{80,64},{96,80},{112,96},{17,1},{3... | collective-permute-start | bytes 1572872 | tf_op jit(solution)/shard_map/ppermute | solution.py:632
  234.4 26.8 %collective-permute-start.13 = (bf16[2048,128]{1,0:T(8,128)(2,1)S(1)}, bf16[2048,128]{1,0:T(8,128)(2,1)S(1)}, u32[]{:S(2)}, u32[]{:S(2)}) collective-permute-start(bf16[2048,128]{1,0:T(8,128)(2,1)S(1)} %get-tuple-element.44), channel_id=1, source_target_pairs={{48,0},{64,80},{80,96},{96,112},{112,64},{49,1},{65,81},{81,97},{9... | collective-permute-start | bytes 1572872 | tf_op jit(solution)/shard_map/ppermute | solution.py:632
  236.3 24.9 %collective-permute-start.14 = (bf16[2048,128]{1,0:T(8,128)(2,1)S(1)}, bf16[2048,128]{1,0:T(8,128)(2,1)S(1)}, u32[]{:S(2)}, u32[]{:S(2)}) collective-permute-start(bf16[2048,128]{1,0:T(8,128)(2,1)S(1)} %get-tuple-element.45), channel_id=1, source_target_pairs={{32,0},{48,16},{64,96},{80,112},{96,64},{112,80},{33,1},{49,17},{6... | collective-permute-start | bytes 1572872 | tf_op jit(solution)/shard_map/ppermute | solution.py:632
  261.5 0.8 copy-start.14
  262.9 12.5 %collective-permute-start.16 = (bf16[2048,128]{1,0:T(8,128)(2,1)}, bf16[2048,128]{1,0:T(8,128)(2,1)S(1)}, u32[]{:S(2)}, u32[]{:S(2)}) collective-permute-start(bf16[2048,128]{1,0:T(8,128)(2,1)} %get-tuple-element.51), channel_id=1, source_target_pairs={{80,64},{96,80},{112,96},{81,65},{97,81},{113,97},{82,66},{98,82},... | collective-permute-start | bytes 1572872 | tf_op jit(solution)/shard_map/ppermute | solution.py:638
  264.2 25.0 %collective-permute-start.17 = (bf16[2048,128]{1,0:T(8,128)(2,1)}, bf16[2048,128]{1,0:T(8,128)(2,1)}, u32[]{:S(2)}, u32[]{:S(2)}) collective-permute-start(bf16[2048,128]{1,0:T(8,128)(2,1)} %get-tuple-element.52), channel_id=1, source_target_pairs={{112,64},{113,65},{114,66},{115,67},{116,68},{117,69},{118,70},{11... | collective-permute-start | bytes 1572872 | tf_op jit(solution)/shard_map/ppermute | solution.py:638
  265.5 23.7 %copy-start.7 = (bf16[2048,128]{1,0:T(8,128)(2,1)S(1)}, bf16[2048,128]{1,0:T(8,128)(2,1)}, u32[]{:S(2)}) copy-start(bf16[2048,128]{1,0:T(8,128)(2,1)} %get-tuple-element.50.refs_5_) | copy-start | bytes 1572868
  265.5 23.7 %collective-permute-start.18 = (bf16[2048,128]{1,0:T(8,128)(2,1)}, bf16[2048,128]{1,0:T(8,128)(2,1)}, u32[]{:S(2)}, u32[]{:S(2)}) collective-permute-start(bf16[2048,128]{1,0:T(8,128)(2,1)} %get-tuple-element.53), channel_id=1, source_target_pairs={{96,64},{112,80},{97,65},{113,81},{98,66},{114,82},{99,67},{115,83... | collective-permute-start | bytes 1572872 | tf_op jit(solution)/shard_map/ppermute | solution.py:638
  266.9 22.3 %collective-permute-start.15 = (bf16[2048,128]{1,0:T(8,128)(2,1)}, bf16[2048,128]{1,0:T(8,128)(2,1)}, u32[]{:S(2)}, u32[]{:S(2)}) collective-permute-start(bf16[2048,128]{1,0:T(8,128)(2,1)} %copy-done.14), channel_id=1, source_target_pairs={{64,0},{80,16},{96,32},{112,48},{65,1},{81,17},{97,33},{113,49},{6... | collective-permute-start | bytes 1572872 | tf_op jit(solution)/shard_map/ppermute | solution.py:636
Sparse Core Ops, SparseCore 0:
  11.3 49.9 all-gather.2
  102.3 44.8 all-gather.4

commit v5 on v4

--- a/solution.py
+++ b/solution.py
@@ -153,7 +153,8 @@
 def teacher_attention(meta, here, kv_blocks):
     return pl.pallas_call(
         teacher_kernel,
-        in_specs=[pl.BlockSpec(memory_space=SMEM), VMEM] + [ANY] * len(kv_blocks),
+        in_specs=[pl.BlockSpec(memory_space=SMEM), pl.BlockSpec((BLOCK, HD), lambda: (0, 0))]
+        + [ANY] * len(kv_blocks),
         out_specs=[pl.BlockSpec((BLOCK, HD), lambda: (0, 0))] * 2,
         out_shape=[pltpu.HBM((BLOCK, HD), bf16)] * 2,
         scratch_shapes=WITH_COUNTS + [pltpu.VMEM((BLOCK, HD), bf16), pltpu.SemaphoreType.DMA],
@@ -162,7 +163,7 @@
             flops=8 * 4 * BLOCK * BLOCK * HD, bytes_accessed=5 << 20, transcendentals=8 * BLOCK * BLOCK
         ),
         name="teacher_attention",
-    )(meta, here, *kv_blocks)
+    )(meta, far(here), *kv_blocks)
 
 
 def chosen_rows(sel, row, table):
@@ -316,48 +317,57 @@
 def project(where, attn, weights, width, extra=None, after=()):
     composed = len(weights) == 1
 
-    def piece(p, at):
-        return (p // 2) * 4 + at[0] * 2 + p % 2
+    def pair(step, at):
+        return step * 2 + at[0]
 
     if composed:
-        w_specs = [pl.BlockSpec((8, 1, COUNTS, 3 * HD), lambda p, c: (0, piece(p, c), 0, 0))]
+        w_specs = [pl.BlockSpec((8, 2, COUNTS, 3 * HD), lambda p, c: (0, pair(p, c), 0, 0))]
     else:
         w_specs = [
-            pl.BlockSpec((HD, width), lambda p, c: (0, piece(p, c))),
-            pl.BlockSpec((2 * HD, width), lambda p, c: (0, piece(p, c))),
+            pl.BlockSpec((HD, 2 * width), lambda p, c: (0, pair(p, c))),
+            pl.BlockSpec((2 * HD, 2 * width), lambda p, c: (0, pair(p, c))),
         ]
-    out_spec = pl.BlockSpec((1, BLOCK, width), lambda p, c: (p, 0, 0))
+    out_spec = pl.BlockSpec((2, BLOCK, width), lambda p, c: (p, 0, 0))
     more = [] if extra is None else [extra]
     args = [far(a) for a in attn] + list(weights) + more + list(after)
 
     def kernel(at, s_ref, a_ref, b_ref, *refs):
-        near = pl.multiple_of(at[1] * HD, HD)
-        far = pl.multiple_of((1 - at[1]) * HD, HD)
+        first = pl.multiple_of(at[1] * HD, HD)
+        second = pl.multiple_of((1 - at[1]) * HD, HD)
+
+        def store(k, acc):
+            if extra is not None:
+                acc = acc + refs[len(weights)][k].astype(f32)
+            refs[-1][k] = acc.astype(bf16)
+
         if composed:
-            wide = refs[0][...].reshape(HD, 3 * HD)
             here, back = a_ref[...], b_ref[...]
-            first = jnp.where(at[1] == 0, here, back)
-            second = jnp.where(at[1] == 0, back, here)
-
-            def times(value, j):
-                return lax.dot_general(
-                    value, wide[:, j * HD : (j + 1) * HD], ROWS_NT, preferred_element_type=f32
-                )
-
-            acc = times(s_ref[...], 0) - times(first, 1) - times(second, 2)
+            low = jnp.where(at[1] == 0, here, back)
+            high = jnp.where(at[1] == 0, back, here)
+            for k in range(2):
+                wide = refs[0][:, k].reshape(HD, 3 * HD)
+
+                def times(value, j):
+                    return lax.dot_general(
+                        value, wide[:, j * HD : (j + 1) * HD], ROWS_NT, preferred_element_type=f32
+                    )
+
+                store(k, times(s_ref[...], 0) - times(low, 1) - times(high, 2))
         else:
-            acc = jnp.dot(s_ref[...], refs[0][...], preferred_element_type=f32)
-            acc -= jnp.dot(a_ref[...], refs[1][pl.ds(near, HD), :], preferred_element_type=f32)
-            acc -= jnp.dot(b_ref[...], refs[1][pl.ds(far, HD), :], preferred_element_type=f32)
-        if extra is not None:
-            acc = acc + refs[len(weights)][0].astype(f32)
-        refs[-1][0] = acc.astype(bf16)
+            for k in range(2):
+                span = pl.ds(k * width, width)
+                acc = jnp.dot(s_ref[...], refs[0][:, span], preferred_element_type=f32)
+                for ref, start in ((a_ref, first), (b_ref, second)):
+                    acc -= jnp.dot(
+                        ref[...], refs[1][pl.ds(start, HD), span], preferred_element_type=f32
+                    )
+                store(k, acc)
 
     return pl.pallas_call(
         kernel,
         grid_spec=pltpu.PrefetchScalarGridSpec(
             num_scalar_prefetch=1,
-            grid=(8,),
+            grid=(4,),
             in_specs=[pl.BlockSpec((BLOCK, HD), lambda p, c: (0, 0))] * 3
             + w_specs
             + [out_spec] * len(more)
@@ -365,7 +375,7 @@
             out_specs=out_spec,
         ),
         out_shape=(pltpu.HBM if more else jax.ShapeDtypeStruct)((8, BLOCK, width), bf16),
-        compiler_params=pltpu.CompilerParams(vmem_limit_bytes=16 << 20),
+        compiler_params=pltpu.CompilerParams(vmem_limit_bytes=20 << 20),
         cost_estimate=pl.CostEstimate(
             flops=2 * 8 * BLOCK * width * 3 * HD,
             bytes_accessed=2 * 8 * BLOCK * width * (1 + len(more)) + (2 << 20),
@@ -485,25 +495,39 @@
 
 
 def compose_kernel(rows_ref, s_ref, t_ref, *refs):
+    out_ref, acc = refs[-2:]
+    step = pl.program_id(0)
+
+    @pl.when(step == 0)
+    def _():
+        acc[...] = jnp.zeros_like(acc)
+
     rows = rows_ref[...]
     for ref, low, high in ((s_ref, 0, HD), (t_ref, HD, 3 * HD)):
-        refs[-1][:, low:high] = lax.dot_general(
-            rows, ref[...], ROWS_NT, preferred_element_type=f32
-        ).astype(bf16)
+        acc[:, low:high] += lax.dot_general(rows, ref[...], ROWS_NT, preferred_element_type=f32)
+
+    @pl.when(step == pl.num_programs(0) - 1)
+    def _():
+        out_ref[...] = acc[...].astype(bf16)
 
 
 def compose(rows, s_out, t_out, after):
+    count, depth = rows.shape
+    size = depth // 4
     return pl.pallas_call(
         compose_kernel,
-        in_specs=[VMEM] * 3 + [ANY] * len(after),
-        out_specs=VMEM,
-        out_shape=jax.ShapeDtypeStruct((rows.shape[0], 3 * HD), bf16),
-        compiler_params=pltpu.CompilerParams(vmem_limit_bytes=24 << 20),
+        grid=(4,),
+        in_specs=[pl.BlockSpec((n, size), lambda i: (0, i)) for n in (count, HD, 2 * HD)]
+        + [ANY] * len(after),
+        out_specs=pl.BlockSpec((count, 3 * HD), lambda i: (0, 0)),
+        out_shape=pltpu.HBM((count, 3 * HD), bf16),
+        scratch_shapes=[pltpu.VMEM((count, 3 * HD), f32)],
+        compiler_params=pltpu.CompilerParams(vmem_limit_bytes=12 << 20),
         cost_estimate=pl.CostEstimate(
-            flops=2 * rows.shape[0] * 3 * HD * rows.shape[1], bytes_accessed=5 << 20, transcendentals=0
+            flops=2 * count * 3 * HD * depth, bytes_accessed=5 << 20, transcendentals=0
         ),
         name="compose",
-    )(rows, s_out, t_out, *after)
+    )(far(rows), s_out, t_out, *after)
 
 
 def add_pieces_kernel(in_ref, out_ref):

time: 297 us -> 294 us (0.990); the launches traced: 299 us -> 292 us
  waiting for transfers between devices: 126 us -> 136 us
  Pallas kernels: 85.2 us -> 76.8 us
  starting transfers between devices: 62.1 us -> 57 us
  local copies, waits for them, and re-layouts: 9.41 us -> 6.19 us
    all_gather x1, waiting for transfers between devices: 1.57 us -> 11.8 us  [on_device(): lax.all_gather(through, BLK, axis=0, tiled=True)]
    pallas_call x1, Pallas kernels: 17.9 us -> 11.5 us  [teacher_attention(): pl.pallas_call(teacher_kernel, in_specs=[pl.BlockSpec(memory_space=SMEM),...]
    ppermute x3, starting transfers between devices: 20.6 us -> 15.2 us  [on_device(): low[j] = lax.ppermute(low[j], BLK, earlier(shift, (1,), (0,)))]
    pallas_call x4, Pallas kernels: 28.9 us -> 24 us  [project(): pl.pallas_call(kernel, grid_spec=pltpu.PrefetchScalarGridSpec(num_scalar_...]
    unnamed x32 -> x26, local copies, waits for them, and re-layouts: 6.96 us -> 3.74 us
    pallas_call x1, Pallas kernels: 1.25 us -> 4.25 us  [compose(): pl.pallas_call(compose_kernel, grid=(4,), in_specs=[pl.BlockSpec((n, size...]
  transfers between devices with their start and end apart: 23 -> 23, of which waited for: 11 -> 11; matrix products, arithmetic and copies ran while one was open for 1% -> 1% of each run, Pallas kernels for 26% -> 23%
where the time goes in v5:
time: 294 us; the launch traced here: 292 us
  waiting for transfers between devices  136 us (46%)
  Pallas kernels  76.8 us (26%)
  starting transfers between devices  57 us (19%)
  between operations  14.4 us (5%)
  local copies, waits for them, and re-layouts  6.19 us (2%)
    ppermute x1, waiting for transfers between devices, on_device(): s_lows = lax.ppermute(s_three, BLK, up)  31.7 us
    pallas_call x4, Pallas kernels, project(): pl.pallas_call(kernel, grid_spec=pltpu.PrefetchScalarGridSpec(num_scalar_...  24 us
    ppermute x1, waiting for transfers between devices, on_device(): s_low = lax.ppermute(s_own, BLK, up)  21.7 us
    ppermute x3, waiting for transfers between devices, on_device(): low[j] = lax.ppermute(low[j], BLK, earlier(shift, (1,), (0,)))  21.5 us
    all_to_all x1, waiting for transfers between devices, on_device(): grad = lax.all_to_all(grad, ZX, 0, 0, tiled=True)  18.3 us
    ppermute x3, waiting for transfers between devices, on_device(): high[j] = lax.ppermute(high[j], BLK, earlier(shift, (), (1,)))  15.4 us
    ppermute x3, starting transfers between devices, on_device(): low[j] = lax.ppermute(low[j], BLK, earlier(shift, (1,), (0,)))  15.2 us
    pallas_call x1, Pallas kernels, student_backward(): pl.pallas_call(student_backward_kernel, grid=(BLOCK // size,), in_specs=[...  14.1 us
  transfers between devices with their start and end apart: 23, of which 11 were waited for; matrix products, arithmetic and copies ran while one was open for 1% of the time, Pallas kernels for 23%

profile of v5, /device:TPU:6, one launch (start us, length us, event | category | flops | bytes accessed | tf_op | source)
XLA Modules:
  0.0 292.0 jit_solution(16441369680064262478)
XLA Ops:
  7.2 0.0 all-gather.3.cloned.1.call-start
  7.2 0.1 pad_add_fusion.2.at
  7.3 0.7 copy-done.9
  8.0 3.1 %pack.1 = (bf16[2064,128]{1,0:T(8,128)(2,1)}, bf16[3088,128]{1,0:T(8,128)(2,1)}, bf16[16,4096]{1,0:T(8,128)(2,1)}, bf16[1024,128]{1,0:T(8,128)(2,1)}, bf16[2064,128]{1,0:T(8,128)(2,1)}) custom-call(s32[2]{0:T(128)S(1)} %pad_add_fusion.2.at, s32[8,128]{1,0:T(8,128)S(1)} %bitcast.11, bf16[1024,256]{1,0:T(8,128)(2,1)} %tq_ref.1, bf16[1024,256]{1,0:T(8,128)(2,1)} %tk_ref.1, ...), custom_call_target="tpu_custom_call" | custom-call | bytes 5242880 | tf_op jit(solution)/shard_map/pack/pallas_call | solution.py:462
  11.1 0.0 all-gather.3.cloned.1.call-update
  11.1 0.0 all-gather.5.cloned.1.call-start
  11.2 0.9 collective-permute-start.4
  12.1 1.3 collective-permute-start.3
  13.4 5.1 %collective-permute-start.2 = (bf16[2064,128]{1,0:T(8,128)(2,1)}, bf16[2064,128]{1,0:T(8,128)(2,1)S(1)}, u32[]{:S(2)}, u32[]{:S(2)}) collective-permute-start(bf16[2064,128]{1,0:T(8,128)(2,1)} %get-tuple-element.30.refs_0_), channel_id=1, source_target_pairs={{0,32},{16,48},{32,0},{48,16},{64,96},{80,112},{1,33},{17,49},{33,... | collective-permute-start | bytes 1585160 | tf_op jit(solution)/shard_map/ppermute | solution.py:591
  18.5 1.3 collective-permute-start.1
  19.9 2.0 collective-permute-start
  21.9 21.7 %collective-permute-done.3.refs_4_ = bf16[2064,128]{1,0:T(8,128)(2,1)S(1)} collective-permute-done((bf16[2064,128]{1,0:T(8,128)(2,1)}, bf16[2064,128]{1,0:T(8,128)(2,1)S(1)}, u32[]{:S(2)}, u32[]{:S(2)}) %collective-permute-start.3) | collective-permute-done | bytes 528416 | tf_op jit(solution)/shard_map/ppermute | solution.py:602
  43.6 3.0 %repack.1 = (bf16[4128,128]{1,0:T(8,128)(2,1)}, bf16[6192,128]{1,0:T(8,128)(2,1)}) custom-call(bf16[2064,128]{1,0:T(8,128)(2,1)} %get-tuple-element.31.kept_ref.refs_0_, bf16[3088,128]{1,0:T(8,128)(2,1)S(1)} %collective-permute-done.4.refs_0_.refs_1_, bf16[2064,128]{1,0:T(8,128)(2,1)S(1)} %collective-permute-done.refs_1_, ...), custom_call_target="tpu_custom_call" | custom-call | bytes 5242880 | tf_op jit(solution)/shard_map/repack/pallas_call | solution.py:485
  46.7 0.8 copy-done.3
  47.5 1.3 collective-permute-start.5
  48.8 3.3 %collective-permute-start.8 = (bf16[4128,128]{1,0:T(8,128)(2,1)}, bf16[4128,128]{1,0:T(8,128)(2,1)}, u32[]{:S(2)}, u32[]{:S(2)}) collective-permute-start(bf16[4128,128]{1,0:T(8,128)(2,1)} %get-tuple-element.36), channel_id=1, source_target_pairs={{0,32},{16,48},{32,0},{48,16},{64,96},{80,112},{96,64},{112,80},{1... | collective-permute-start | bytes 3170312 | tf_op jit(solution)/shard_map/ppermute | solution.py:591
  52.1 1.1 collective-permute-start.7
  53.1 1.0 collective-permute-start.6
  54.1 0.1 add.101
  54.2 0.1 reshape.54.sel
  54.3 0.1 add.98
  54.4 0.1 add.99
  54.5 0.1 pad_add_fusion.1.meta
  54.7 31.7 %collective-permute-done.5.refs_5_ = bf16[6192,128]{1,0:T(8,128)(2,1)} collective-permute-done((bf16[6192,128]{1,0:T(8,128)(2,1)}, bf16[6192,128]{1,0:T(8,128)(2,1)}, u32[]{:S(2)}, u32[]{:S(2)}) %collective-permute-start.5) | collective-permute-done | bytes 1585184 | tf_op jit(solution)/shard_map/ppermute | solution.py:605
  86.4 10.0 %student_forward.1 = (bf16[1024,128]{1,0:T(8,128)(2,1)}, f32[1024,1024]{1,0:T(8,128)}) custom-call(s32[2]{0:T(128)S(1)} %pad_add_fusion.1.meta, s32[256]{0:T(256)S(1)} %reshape.54.sel, bf16[1024,128]{1,0:T(8,128)(2,1)S(1)} %copy-done.7, s32[16,1,1024]{2,1,0:T(1,128)S(1)} %broadcast_add_fusion.kpos_ref, bf16[2064,128]{1,0:T(8,128)(2,1)} %get-tuple-element.30.refs_0_, ...), custom_call_target="tpu_custom_call" | custom-call | flops 536870912 | bytes 9437184 | tf_op jit(solution)/shard_map/student_forward/pallas_call | solution.py:208
  96.4 1.5 collective-permute-done.7.refs_3_
  97.9 0.7 fusion.7.refs_0_
  98.7 4.3 %compose.1 = bf16[256,384]{1,0:T(8,128)(2,1)} custom-call(bf16[256,4096]{1,0:T(8,128)(2,1)} %all-gather.3.cloned.1.call-done.rows_ref, bf16[128,4096]{1,0:T(8,128)(2,1)S(1)} %copy-done.1, bf16[256,4096]{1,0:T(8,128)(2,1)S(1)} %copy-done, bf16[16,128]{1,0:T(8,128)(2,1)S(1)} %fusion.7.refs_0_), custom_call_target="tpu_custom_call" | custom-call | flops 805306368 | bytes 5242880 | tf_op jit(solution)/shard_map/compose/pallas_call | solution.py:517
  103.0 0.1 concatenate.3.meta
  103.1 11.5 %teacher_attention.1 = (bf16[1024,128]{1,0:T(8,128)(2,1)}, bf16[1024,128]{1,0:T(8,128)(2,1)}) custom-call(s32[16]{0:T(128)S(1)} %concatenate.3.meta, bf16[1024,128]{1,0:T(8,128)(2,1)} %get-tuple-element.35.here_ref, bf16[2064,128]{1,0:T(8,128)(2,1)} %get-tuple-element.31.kept_ref.refs_0_, bf16[3088,128]{1,0:T(8,128)(2,1)} %copy-done.8, ...), custom_call_target="tpu_custom_call" | custom-call | flops 4294967296 | bytes 5242880 | tf_op jit(solution)/shard_map/teacher_attention/pallas_call | solution.py:154
  114.6 3.5 %collective-permute-start.9 = (bf16[1024,128]{1,0:T(8,128)(2,1)}, bf16[1024,128]{1,0:T(8,128)(2,1)}, u32[]{:S(2)}, u32[]{:S(2)}) collective-permute-start(bf16[1024,128]{1,0:T(8,128)(2,1)} %get-tuple-element.38), channel_id=1, source_target_pairs={{0,64},{16,80},{32,96},{48,112},{64,0},{80,16},{96,32},{112,48},{1... | collective-permute-start | bytes 786440 | tf_op jit(solution)/shard_map/ppermute | solution.py:627
  118.1 0.1 pad_add_fusion.3.at
  118.2 10.2 %collective-permute-done.9.b_ref = bf16[1024,128]{1,0:T(8,128)(2,1)} collective-permute-done((bf16[1024,128]{1,0:T(8,128)(2,1)}, bf16[1024,128]{1,0:T(8,128)(2,1)}, u32[]{:S(2)}, u32[]{:S(2)}) %collective-permute-start.9) | collective-permute-done | bytes 262176 | tf_op jit(solution)/shard_map/ppermute | solution.py:627
  128.3 6.8 %project_mismatch.2 = bf16[8,1024,256]{2,1,0:T(8,128)(2,1)} custom-call(s32[2]{0:T(128)S(1)} %pad_add_fusion.3.at, bf16[1024,128]{1,0:T(8,128)(2,1)} %get-tuple-element.34.s_ref, bf16[1024,128]{1,0:T(8,128)(2,1)} %get-tuple-element.37.a_ref, bf16[1024,128]{1,0:T(8,128)(2,1)} %collective-permute-done.9.b_ref, bf16[128,4096]{1,0:T(8,128)(2,1)S(1)} %copy-done.1, ...), custom_call_target="tpu_custom_call" | custom-call | flops 1610612736 | bytes 6291456 | tf_op jit(solution)/shard_map/project_mismatch/pallas_call | solution.py:366
  135.2 0.7 slice_bitcast_fusion.refs_1_
  135.9 11.8 %all-gather.5.cloned.1.call-done = bf16[2048,384]{1,0:T(8,128)(2,1)} async-done(((bf16[256,384]{1,0:T(8,128)(2,1)}), bf16[2048,384]{1,0:T(8,128)(2,1)}) %all-gather.5.cloned.1.call-update) | async-done | bytes 1572880 | tf_op jit(solution)/shard_map/all_gather | solution.py:623
  147.7 1.4 copy-done.2
  149.1 4.1 %project_grad.2 = bf16[8,1024,128]{2,1,0:T(8,128)(2,1)S(1)} custom-call(s32[2]{0:T(128)S(1)} %pad_add_fusion.3.at, bf16[1024,128]{1,0:T(8,128)(2,1)} %get-tuple-element.34.s_ref, bf16[1024,128]{1,0:T(8,128)(2,1)} %get-tuple-element.37.a_ref, bf16[1024,128]{1,0:T(8,128)(2,1)} %collective-permute-done.9.b_ref, bf16[8,16,16,384]{3,2,1,0:T(8,128)(2,1)S(1)} %bitcast.9, ...), custom_call_target="tpu_custom_call" | custom-call | flops 805306368 | bytes 4194304 | tf_op jit(solution)/shard_map/project_grad/pallas_call | solution.py:366
  153.2 0.1 collective-permute-start.11
  153.3 0.1 pad_add_fusion.at
  153.4 4.1 %collective-permute-done.11.refs_1_ = bf16[8,1024,128]{2,1,0:T(8,128)(2,1)S(1)} collective-permute-done((bf16[8,1024,128]{2,1,0:T(8,128)(2,1)S(1)}, bf16[8,1024,128]{2,1,0:T(8,128)(2,1)S(1)}, u32[]{:S(2)}, u32[]{:S(2)}) %collective-permute-start.11) | collective-permute-done | bytes 2097184 | tf_op jit(solution)/shard_map/ppermute | solution.py:635
  157.5 5.2 %project_grad.3 = bf16[8,1024,128]{2,1,0:T(8,128)(2,1)} custom-call(s32[2]{0:T(128)S(1)} %pad_add_fusion.at, bf16[1024,128]{1,0:T(8,128)(2,1)} %get-tuple-element.34.s_ref, bf16[1024,128]{1,0:T(8,128)(2,1)} %get-tuple-element.37.a_ref, bf16[1024,128]{1,0:T(8,128)(2,1)} %collective-permute-done.9.b_ref, bf16[8,16,16,384]{3,2,1,0:T(8,128)(2,1)S(1)} %bitcast.10, ...), custom_call_target="tpu_custom_call" | custom-call | flops 805306368 | bytes 6291456 | tf_op jit(solution)/shard_map/project_grad/pallas_call | solution.py:366
  162.7 7.6 %all-to-all-start.1 = ((bf16[8,1024,128]{2,1,0:T(8,128)(2,1)}), bf16[8,1024,128]{2,1,0:T(8,128)(2,1)}, u32[]{:S(2)}, u32[]{:S(2)}) async-start(bf16[8,1024,128]{2,1,0:T(8,128)(2,1)} %project_grad.3), calls=%async_computation.1 | async-start | bytes 4194304 | tf_op jit(solution)/shard_map/all_to_all | solution.py:637
  170.3 7.8 %project_mismatch.3 = bf16[8,1024,256]{2,1,0:T(8,128)(2,1)} custom-call(s32[2]{0:T(128)S(1)} %pad_add_fusion.at, bf16[1024,128]{1,0:T(8,128)(2,1)} %get-tuple-element.34.s_ref, bf16[1024,128]{1,0:T(8,128)(2,1)} %get-tuple-element.37.a_ref, bf16[1024,128]{1,0:T(8,128)(2,1)} %collective-permute-done.9.b_ref, bf16[128,4096]{1,0:T(8,128)(2,1)S(1)} %copy-done.1, ...), custom_call_target="tpu_custom_call" | custom-call | flops 1610612736 | bytes 10485760 | tf_op jit(solution)/shard_map/project_mismatch/pallas_call | solution.py:366
  178.1 18.3 %all-to-all-done.1.g_ref = bf16[8,1024,128]{2,1,0:T(8,128)(2,1)} async-done(((bf16[8,1024,128]{2,1,0:T(8,128)(2,1)}), bf16[8,1024,128]{2,1,0:T(8,128)(2,1)}, u32[]{:S(2)}, u32[]{:S(2)}) %all-to-all-start.1) | async-done | bytes 2097184 | tf_op jit(solution)/shard_map/all_to_all | solution.py:637
  196.4 7.2 %all-to-all-start = ((bf16[8,1024,256]{2,1,0:T(8,128)(2,1)}), bf16[8,1024,256]{2,1,0:T(8,128)(2,1)}, u32[]{:S(2)}, u32[]{:S(2)}) async-start(bf16[8,1024,256]{2,1,0:T(8,128)(2,1)} %project_mismatch.3), calls=%async_computation | async-start | bytes 8388608 | tf_op jit(solution)/shard_map/all_to_all | solution.py:640
  203.6 14.1 %student_backward.1 = (f32[1024,128]{1,0:T(8,128)}, bf16[2048,128]{1,0:T(8,128)(2,1)S(1)}, bf16[2048,128]{1,0:T(8,128)(2,1)S(1)}, bf16[2048,128]{1,0:T(8,128)(2,...) custom-call(s32[2]{0:T(128)S(1)} %pad_add_fusion.1.meta, ...), custom_call_target="tpu_custom_call" | custom-call | flops 1073741824 | bytes 15728640 | tf_op jit(solution)/shard_map/student_backward/pallas_call | solution.py:293
  217.7 9.9 %collective-permute-start.12 = (bf16[2048,128]{1,0:T(8,128)(2,1)S(1)}, bf16[2048,128]{1,0:T(8,128)(2,1)S(1)}, u32[]{:S(2)}, u32[]{:S(2)}) collective-permute-start(bf16[2048,128]{1,0:T(8,128)(2,1)S(1)} %get-tuple-element.43), channel_id=1, source_target_pairs={{16,0},{32,16},{48,32},{64,112},{80,64},{96,80},{112,96},{17,1},{3... | collective-permute-start | bytes 1572872 | tf_op jit(solution)/shard_map/ppermute | solution.py:656
  227.6 1.9 collective-permute-start.13
  229.6 3.4 %collective-permute-start.14 = (bf16[2048,128]{1,0:T(8,128)(2,1)S(1)}, bf16[2048,128]{1,0:T(8,128)(2,1)S(1)}, u32[]{:S(2)}, u32[]{:S(2)}) collective-permute-start(bf16[2048,128]{1,0:T(8,128)(2,1)S(1)} %get-tuple-element.45), channel_id=1, source_target_pairs={{32,0},{48,16},{64,96},{80,112},{96,64},{112,80},{33,1},{49,17},{6... | collective-permute-start | bytes 1572872 | tf_op jit(solution)/shard_map/ppermute | solution.py:656
  233.0 16.2 %collective-permute-done.12.refs_1_ = bf16[2048,128]{1,0:T(8,128)(2,1)S(1)} collective-permute-done((bf16[2048,128]{1,0:T(8,128)(2,1)S(1)}, bf16[2048,128]{1,0:T(8,128)(2,1)S(1)}, u32[]{:S(2)}, u32[]{:S(2)}) %collective-permute-start.12) | collective-permute-done | bytes 524320 | tf_op jit(solution)/shard_map/ppermute | solution.py:656
  249.1 5.3 %collective-permute-done.13.refs_2_ = bf16[2048,128]{1,0:T(8,128)(2,1)S(1)} collective-permute-done((bf16[2048,128]{1,0:T(8,128)(2,1)S(1)}, bf16[2048,128]{1,0:T(8,128)(2,1)S(1)}, u32[]{:S(2)}, u32[]{:S(2)}) %collective-permute-start.13) | collective-permute-done | bytes 524320 | tf_op jit(solution)/shard_map/ppermute | solution.py:656
  254.5 0.3 add_convert_fusion
  254.7 0.8 copy-done.11
  255.5 0.6 slice.39.refs_4_
  256.1 1.3 collective-permute-start.16
  257.4 1.3 collective-permute-start.17
  258.7 1.4 collective-permute-start.18
  260.2 2.1 collective-permute-start.15
  262.3 4.2 %add_pieces.1 = f32[1024,256]{1,0:T(8,128)} custom-call(bf16[8,1024,256]{2,1,0:T(8,128)(2,1)} %all-to-all-done.in_ref), custom_call_target="tpu_custom_call" | custom-call | flops 8388608 | bytes 5242880 | tf_op jit(solution)/shard_map/add_pieces/pallas_call | solution.py:540
  266.5 0.7 slice.40.refs_9_
  267.2 1.5 collective-permute-done.16.refs_6_
  268.7 13.9 %collective-permute-done.17.refs_7_ = bf16[2048,128]{1,0:T(8,128)(2,1)} collective-permute-done((bf16[2048,128]{1,0:T(8,128)(2,1)}, bf16[2048,128]{1,0:T(8,128)(2,1)}, u32[]{:S(2)}, u32[]{:S(2)}) %collective-permute-start.17) | collective-permute-done | bytes 524320 | tf_op jit(solution)/shard_map/ppermute | solution.py:662
  282.6 2.6 finish.1
  (44 shorter events, 0.2 us)
Async XLA Ops:
  7.2 91.5 %all-gather.3.cloned.1.call-start = ((), (), s32[]{:S(2)}) async-start(), calls=%async_computation.2 | async-start | bytes 2228224 | tf_op jit(solution)/shard_map/all_gather | solution.py:621
  7.3 0.7 copy-start.9
  11.1 43.1 %copy-start.12 = (s32[16,16]{1,0:T(8,128)S(1)}, s32[16,16]{1,0:T(8,128)}, u32[]{:S(2)}) copy-start(s32[16,16]{1,0:T(8,128)} %param.19) | copy-start | bytes 3076
  11.1 75.3 %copy-start.7 = (bf16[1024,128]{1,0:T(8,128)(2,1)S(1)}, bf16[1024,128]{1,0:T(8,128)(2,1)}, u32[]{:S(2)}) copy-start(bf16[1024,128]{1,0:T(8,128)(2,1)} %q_ref.3) | copy-start | bytes 786436
  11.1 136.5 %all-gather.5.cloned.1.call-start = ((), (), s32[]{:S(2)}) async-start(), calls=%async_computation.3 | async-start | bytes 1769472 | tf_op jit(solution)/shard_map/all_gather | solution.py:623
  11.2 32.4 %collective-permute-start.4 = (bf16[3088,128]{1,0:T(8,128)(2,1)}, bf16[3088,128]{1,0:T(8,128)(2,1)S(1)}, u32[]{:S(2)}, u32[]{:S(2)}) collective-permute-start(bf16[3088,128]{1,0:T(8,128)(2,1)} %get-tuple-element.32), channel_id=1, source_target_pairs={{0,64},{16,80},{32,96},{48,112},{64,0},{80,16},{96,32},{112,48},{1... | collective-permute-start | bytes 2371592 | tf_op jit(solution)/shard_map/ppermute | solution.py:601
  12.1 31.5 %collective-permute-start.3 = (bf16[2064,128]{1,0:T(8,128)(2,1)}, bf16[2064,128]{1,0:T(8,128)(2,1)S(1)}, u32[]{:S(2)}, u32[]{:S(2)}) collective-permute-start(bf16[2064,128]{1,0:T(8,128)(2,1)} %get-tuple-element.30.refs_0_), channel_id=1, source_target_pairs={{0,64},{16,80},{32,96},{48,112},{1,65},{17,81},{33,97},{49,113},{2... | collective-permute-start | bytes 1585160 | tf_op jit(solution)/shard_map/ppermute | solution.py:602
  13.4 30.2 %collective-permute-start.2 = (bf16[2064,128]{1,0:T(8,128)(2,1)}, bf16[2064,128]{1,0:T(8,128)(2,1)S(1)}, u32[]{:S(2)}, u32[]{:S(2)}) collective-permute-start(bf16[2064,128]{1,0:T(8,128)(2,1)} %get-tuple-element.30.refs_0_), channel_id=1, source_target_pairs={{0,32},{16,48},{32,0},{48,16},{64,96},{80,112},{1,33},{17,49},{33,... | collective-permute-start | bytes 1585160 | tf_op jit(solution)/shard_map/ppermute | solution.py:591
  18.5 25.1 %collective-permute-start.1 = (bf16[2064,128]{1,0:T(8,128)(2,1)}, bf16[2064,128]{1,0:T(8,128)(2,1)S(1)}, u32[]{:S(2)}, u32[]{:S(2)}) collective-permute-start(bf16[2064,128]{1,0:T(8,128)(2,1)} %get-tuple-element.30.refs_0_), channel_id=1, source_target_pairs={{0,48},{16,0},{32,16},{48,32},{64,112},{1,49},{17,1},{33,17},{49,3... | collective-permute-start | bytes 1585160 | tf_op jit(solution)/shard_map/ppermute | solution.py:591
  19.9 23.7 %collective-permute-start = (bf16[2064,128]{1,0:T(8,128)(2,1)}, bf16[2064,128]{1,0:T(8,128)(2,1)S(1)}, u32[]{:S(2)}, u32[]{:S(2)}) collective-permute-start(bf16[2064,128]{1,0:T(8,128)(2,1)} %get-tuple-element.30.refs_0_), channel_id=1, source_target_pairs={{0,16},{16,32},{32,48},{48,0},{64,80},{80,96},{96,112},{1,17},{17,... | collective-permute-start | bytes 1585160 | tf_op jit(solution)/shard_map/ppermute | solution.py:591
  43.6 5.2 %copy-start.10 = (bf16[2064,128]{1,0:T(8,128)(2,1)}, bf16[2064,128]{1,0:T(8,128)(2,1)S(1)}, u32[]{:S(2)}) copy-start(bf16[2064,128]{1,0:T(8,128)(2,1)S(1)} %collective-permute-done.3.refs_4_) | copy-start | bytes 1585156
  43.6 3.1 %copy-start.4 = (bf16[2064,128]{1,0:T(8,128)(2,1)}, bf16[2064,128]{1,0:T(8,128)(2,1)S(1)}, u32[]{:S(2)}) copy-start(bf16[2064,128]{1,0:T(8,128)(2,1)S(1)} %collective-permute-done.1.refs_2_) | copy-start | bytes 1585156
  43.6 3.9 %copy-start.5 = (bf16[2064,128]{1,0:T(8,128)(2,1)}, bf16[2064,128]{1,0:T(8,128)(2,1)S(1)}, u32[]{:S(2)}) copy-start(bf16[2064,128]{1,0:T(8,128)(2,1)S(1)} %collective-permute-done.refs_1_) | copy-start | bytes 1585156
  43.6 5.2 %copy-start.8 = (bf16[3088,128]{1,0:T(8,128)(2,1)}, bf16[3088,128]{1,0:T(8,128)(2,1)S(1)}, u32[]{:S(2)}) copy-start(bf16[3088,128]{1,0:T(8,128)(2,1)S(1)} %collective-permute-done.4.refs_0_.refs_1_) | copy-start | bytes 2371588
  46.7 0.8 copy-start.3
  47.5 38.9 %collective-permute-start.5 = (bf16[6192,128]{1,0:T(8,128)(2,1)}, bf16[6192,128]{1,0:T(8,128)(2,1)}, u32[]{:S(2)}, u32[]{:S(2)}) collective-permute-start(bf16[6192,128]{1,0:T(8,128)(2,1)} %get-tuple-element.33), channel_id=1, source_target_pairs={{0,64},{16,80},{32,96},{48,112},{1,65},{17,81},{33,97},{49,113},{2... | collective-permute-start | bytes 4755464 | tf_op jit(solution)/shard_map/ppermute | solution.py:605
  48.8 47.6 %collective-permute-start.8 = (bf16[4128,128]{1,0:T(8,128)(2,1)}, bf16[4128,128]{1,0:T(8,128)(2,1)}, u32[]{:S(2)}, u32[]{:S(2)}) collective-permute-start(bf16[4128,128]{1,0:T(8,128)(2,1)} %get-tuple-element.36), channel_id=1, source_target_pairs={{0,32},{16,48},{32,0},{48,16},{64,96},{80,112},{96,64},{112,80},{1... | collective-permute-start | bytes 3170312 | tf_op jit(solution)/shard_map/ppermute | solution.py:591
  52.1 45.9 %collective-permute-start.7 = (bf16[4128,128]{1,0:T(8,128)(2,1)}, bf16[4128,128]{1,0:T(8,128)(2,1)}, u32[]{:S(2)}, u32[]{:S(2)}) collective-permute-start(bf16[4128,128]{1,0:T(8,128)(2,1)} %get-tuple-element.36), channel_id=1, source_target_pairs={{0,48},{16,0},{32,16},{48,32},{64,112},{80,64},{96,80},{112,96},{1... | collective-permute-start | bytes 3170312 | tf_op jit(solution)/shard_map/ppermute | solution.py:591
  53.1 44.8 %collective-permute-start.6 = (bf16[4128,128]{1,0:T(8,128)(2,1)}, bf16[4128,128]{1,0:T(8,128)(2,1)}, u32[]{:S(2)}, u32[]{:S(2)}) collective-permute-start(bf16[4128,128]{1,0:T(8,128)(2,1)} %get-tuple-element.36), channel_id=1, source_target_pairs={{0,16},{16,32},{32,48},{48,0},{64,80},{80,96},{96,112},{112,64},{1... | collective-permute-start | bytes 3170312 | tf_op jit(solution)/shard_map/ppermute | solution.py:591
  54.7 44.0 %copy-start = (bf16[256,4096]{1,0:T(8,128)(2,1)S(1)}, bf16[256,4096]{1,0:T(8,128)(2,1)}, u32[]{:S(2)}) copy-start(bf16[256,4096]{1,0:T(8,128)(2,1)} %t_ref.1) | copy-start | bytes 6291460
  54.7 44.0 %copy-start.1 = (bf16[128,4096]{1,0:T(8,128)(2,1)S(1)}, bf16[128,4096]{1,0:T(8,128)(2,1)}, u32[]{:S(2)}) copy-start(bf16[128,4096]{1,0:T(8,128)(2,1)} %s_ref.1) | copy-start | bytes 3145732
  114.6 13.8 %collective-permute-start.9 = (bf16[1024,128]{1,0:T(8,128)(2,1)}, bf16[1024,128]{1,0:T(8,128)(2,1)}, u32[]{:S(2)}, u32[]{:S(2)}) collective-permute-start(bf16[1024,128]{1,0:T(8,128)(2,1)} %get-tuple-element.38), channel_id=1, source_target_pairs={{0,64},{16,80},{32,96},{48,112},{64,0},{80,16},{96,32},{112,48},{1... | collective-permute-start | bytes 786440 | tf_op jit(solution)/shard_map/ppermute | solution.py:627
  135.2 35.1 %collective-permute-start.10 = (bf16[8,1024,256]{2,1,0:T(8,128)(2,1)}, bf16[8,1024,256]{2,1,0:T(8,128)(2,1)}, u32[]{:S(2)}, u32[]{:S(2)}) collective-permute-start(bf16[8,1024,256]{2,1,0:T(8,128)(2,1)} %project_mismatch.2), channel_id=1, source_target_pairs={{0,2},{2,0},{1,3},{3,1},{4,6},{6,4},{5,7},{7,5},{8,10},{10,8},{9,1... | collective-permute-start | bytes 12582920 | tf_op jit(solution)/shard_map/ppermute | solution.py:638
  147.7 1.4 copy-start.2
  153.2 4.2 %collective-permute-start.11 = (bf16[8,1024,128]{2,1,0:T(8,128)(2,1)S(1)}, bf16[8,1024,128]{2,1,0:T(8,128)(2,1)S(1)}, u32[]{:S(2)}, u32[]{:S(2)}) collective-permute-start(bf16[8,1024,128]{2,1,0:T(8,128)(2,1)S(1)} %project_grad.2), channel_id=1, source_target_pairs={{0,2},{2,0},{1,3},{3,1},{4,6},{6,4},{5,7},{7,5},{8,10},{10,8},{9,1... | collective-permute-start | bytes 6291464 | tf_op jit(solution)/shard_map/ppermute | solution.py:635
  162.7 33.8 %all-to-all-start.1 = ((bf16[8,1024,128]{2,1,0:T(8,128)(2,1)}), bf16[8,1024,128]{2,1,0:T(8,128)(2,1)}, u32[]{:S(2)}, u32[]{:S(2)}) async-start(bf16[8,1024,128]{2,1,0:T(8,128)(2,1)} %project_grad.3), calls=%async_computation.1 | async-start | bytes 4194304 | tf_op jit(solution)/shard_map/all_to_all | solution.py:637
  196.4 65.8 %all-to-all-start = ((bf16[8,1024,256]{2,1,0:T(8,128)(2,1)}), bf16[8,1024,256]{2,1,0:T(8,128)(2,1)}, u32[]{:S(2)}, u32[]{:S(2)}) async-start(bf16[8,1024,256]{2,1,0:T(8,128)(2,1)} %project_mismatch.3), calls=%async_computation | async-start | bytes 8388608 | tf_op jit(solution)/shard_map/all_to_all | solution.py:640
  217.7 31.4 %collective-permute-start.12 = (bf16[2048,128]{1,0:T(8,128)(2,1)S(1)}, bf16[2048,128]{1,0:T(8,128)(2,1)S(1)}, u32[]{:S(2)}, u32[]{:S(2)}) collective-permute-start(bf16[2048,128]{1,0:T(8,128)(2,1)S(1)} %get-tuple-element.43), channel_id=1, source_target_pairs={{16,0},{32,16},{48,32},{64,112},{80,64},{96,80},{112,96},{17,1},{3... | collective-permute-start | bytes 1572872 | tf_op jit(solution)/shard_map/ppermute | solution.py:656
  227.6 26.8 %collective-permute-start.13 = (bf16[2048,128]{1,0:T(8,128)(2,1)S(1)}, bf16[2048,128]{1,0:T(8,128)(2,1)S(1)}, u32[]{:S(2)}, u32[]{:S(2)}) collective-permute-start(bf16[2048,128]{1,0:T(8,128)(2,1)S(1)} %get-tuple-element.44), channel_id=1, source_target_pairs={{48,0},{64,80},{80,96},{96,112},{112,64},{49,1},{65,81},{81,97},{9... | collective-permute-start | bytes 1572872 | tf_op jit(solution)/shard_map/ppermute | solution.py:656
  229.6 24.9 %collective-permute-start.14 = (bf16[2048,128]{1,0:T(8,128)(2,1)S(1)}, bf16[2048,128]{1,0:T(8,128)(2,1)S(1)}, u32[]{:S(2)}, u32[]{:S(2)}) collective-permute-start(bf16[2048,128]{1,0:T(8,128)(2,1)S(1)} %get-tuple-element.45), channel_id=1, source_target_pairs={{32,0},{48,16},{64,96},{80,112},{96,64},{112,80},{33,1},{49,17},{6... | collective-permute-start | bytes 1572872 | tf_op jit(solution)/shard_map/ppermute | solution.py:656
  254.7 0.8 copy-start.11
  256.1 12.6 %collective-permute-start.16 = (bf16[2048,128]{1,0:T(8,128)(2,1)}, bf16[2048,128]{1,0:T(8,128)(2,1)S(1)}, u32[]{:S(2)}, u32[]{:S(2)}) collective-permute-start(bf16[2048,128]{1,0:T(8,128)(2,1)} %get-tuple-element.51), channel_id=1, source_target_pairs={{80,64},{96,80},{112,96},{81,65},{97,81},{113,97},{82,66},{98,82},... | collective-permute-start | bytes 1572872 | tf_op jit(solution)/shard_map/ppermute | solution.py:662
  257.4 25.1 %collective-permute-start.17 = (bf16[2048,128]{1,0:T(8,128)(2,1)}, bf16[2048,128]{1,0:T(8,128)(2,1)}, u32[]{:S(2)}, u32[]{:S(2)}) collective-permute-start(bf16[2048,128]{1,0:T(8,128)(2,1)} %get-tuple-element.52), channel_id=1, source_target_pairs={{112,64},{113,65},{114,66},{115,67},{116,68},{117,69},{118,70},{11... | collective-permute-start | bytes 1572872 | tf_op jit(solution)/shard_map/ppermute | solution.py:662
  258.7 23.9 %copy-start.6 = (bf16[2048,128]{1,0:T(8,128)(2,1)S(1)}, bf16[2048,128]{1,0:T(8,128)(2,1)}, u32[]{:S(2)}) copy-start(bf16[2048,128]{1,0:T(8,128)(2,1)} %get-tuple-element.50.refs_5_) | copy-start | bytes 1572868
  258.7 23.8 %collective-permute-start.18 = (bf16[2048,128]{1,0:T(8,128)(2,1)}, bf16[2048,128]{1,0:T(8,128)(2,1)}, u32[]{:S(2)}, u32[]{:S(2)}) collective-permute-start(bf16[2048,128]{1,0:T(8,128)(2,1)} %get-tuple-element.53), channel_id=1, source_target_pairs={{96,64},{112,80},{97,65},{113,81},{98,66},{114,82},{99,67},{115,83... | collective-permute-start | bytes 1572872 | tf_op jit(solution)/shard_map/ppermute | solution.py:662
  260.2 22.4 %collective-permute-start.15 = (bf16[2048,128]{1,0:T(8,128)(2,1)}, bf16[2048,128]{1,0:T(8,128)(2,1)}, u32[]{:S(2)}, u32[]{:S(2)}) collective-permute-start(bf16[2048,128]{1,0:T(8,128)(2,1)} %copy-done.11), channel_id=1, source_target_pairs={{64,0},{80,16},{96,32},{112,48},{65,1},{81,17},{97,33},{113,49},{6... | collective-permute-start | bytes 1572872 | tf_op jit(solution)/shard_map/ppermute | solution.py:660
Sparse Core Ops, SparseCore 0:
  11.3 49.9 all-gather.2
  103.1 44.5 all-gather.4

commit v6 on v5

--- a/solution.py
+++ b/solution.py
@@ -14,7 +14,7 @@
 FORWARD_ROWS = 4
 BACKWARD_ROWS = 4
 TILE_Q = 512
-TILE_K = 512
+TILE_K = 1024
 SCALE = HD ** (-0.5)
 EXP_SCALE = SCALE * 1.4426950408889634
 LOWEST = -1e30

time: 294 us -> 295 us (level)
  Pallas kernels: 76.8 us -> 82.5 us
  waiting for transfers between devices: 136 us -> 132 us
    all_gather x1, waiting for transfers between devices: 11.8 us -> 5.11 us  [on_device(): lax.all_gather(through, BLK, axis=0, tiled=True)]
    pallas_call x1, Pallas kernels: 11.5 us -> 17.1 us  [teacher_attention(): pl.pallas_call(teacher_kernel, in_specs=[pl.BlockSpec(memory_space=SMEM),...]
  transfers between devices with their start and end apart: 23 -> 23, of which waited for: 11 -> 11; matrix products, arithmetic and copies ran while one was open for 1% -> 1% of each run, Pallas kernels for 23% -> 25%
where the time goes in v6:
time: 295 us; the launch traced here: 294 us
  waiting for transfers between devices  132 us (45%)
  Pallas kernels  82.5 us (28%)
  starting transfers between devices  57.9 us (20%)
  between operations  14.4 us (5%)
  local copies, waits for them, and re-layouts  6.19 us (2%)
    ppermute x1, waiting for transfers between devices, on_device(): s_lows = lax.ppermute(s_three, BLK, up)  31.7 us
    pallas_call x4, Pallas kernels, project(): pl.pallas_call(kernel, grid_spec=pltpu.PrefetchScalarGridSpec(num_scalar_...  24 us
    ppermute x1, waiting for transfers between devices, on_device(): s_low = lax.ppermute(s_own, BLK, up)  21.7 us
    ppermute x3, waiting for transfers between devices, on_device(): low[j] = lax.ppermute(low[j], BLK, earlier(shift, (1,), (0,)))  21.5 us
    all_to_all x1, waiting for transfers between devices, on_device(): grad = lax.all_to_all(grad, ZX, 0, 0, tiled=True)  18.3 us
    pallas_call x1, Pallas kernels, teacher_attention(): pl.pallas_call(teacher_kernel, in_specs=[pl.BlockSpec(memory_space=SMEM),...  17.1 us
    ppermute x3, starting transfers between devices, on_device(): low[j] = lax.ppermute(low[j], BLK, earlier(shift, (1,), (0,)))  17 us
    ppermute x3, waiting for transfers between devices, on_device(): high[j] = lax.ppermute(high[j], BLK, earlier(shift, (), (1,)))  15.3 us
  transfers between devices with their start and end apart: 23, of which 11 were waited for; matrix products, arithmetic and copies ran while one was open for 1% of the time, Pallas kernels for 25%

profile of v6, /device:TPU:6, one launch (start us, length us, event | category | flops | bytes accessed | tf_op | source)
XLA Modules:
  0.0 293.9 jit_solution(2038409596631719692)
XLA Ops:
  7.2 0.0 all-gather.3.cloned.1.call-start
  7.2 0.1 pad_add_fusion.2.at
  7.3 0.7 copy-done.9
  8.0 3.1 %pack.1 = (bf16[2064,128]{1,0:T(8,128)(2,1)}, bf16[3088,128]{1,0:T(8,128)(2,1)}, bf16[16,4096]{1,0:T(8,128)(2,1)}, bf16[1024,128]{1,0:T(8,128)(2,1)}, bf16[2064,128]{1,0:T(8,128)(2,1)}) custom-call(s32[2]{0:T(128)S(1)} %pad_add_fusion.2.at, s32[8,128]{1,0:T(8,128)S(1)} %bitcast.11, bf16[1024,256]{1,0:T(8,128)(2,1)} %tq_ref.1, bf16[1024,256]{1,0:T(8,128)(2,1)} %tk_ref.1, ...), custom_call_target="tpu_custom_call" | custom-call | bytes 5242880 | tf_op jit(solution)/shard_map/pack/pallas_call | solution.py:462
  11.1 0.0 all-gather.3.cloned.1.call-update
  11.1 0.0 all-gather.5.cloned.1.call-start
  11.2 0.9 collective-permute-start.4
  12.1 1.3 collective-permute-start.3
  13.4 5.1 %collective-permute-start.2 = (bf16[2064,128]{1,0:T(8,128)(2,1)}, bf16[2064,128]{1,0:T(8,128)(2,1)S(1)}, u32[]{:S(2)}, u32[]{:S(2)}) collective-permute-start(bf16[2064,128]{1,0:T(8,128)(2,1)} %get-tuple-element.30.refs_0_), channel_id=1, source_target_pairs={{0,32},{16,48},{32,0},{48,16},{64,96},{80,112},{1,33},{17,49},{33,... | collective-permute-start | bytes 1585160 | tf_op jit(solution)/shard_map/ppermute | solution.py:591
  18.5 1.3 collective-permute-start.1
  19.9 2.0 collective-permute-start
  21.9 21.7 %collective-permute-done.3.refs_4_ = bf16[2064,128]{1,0:T(8,128)(2,1)S(1)} collective-permute-done((bf16[2064,128]{1,0:T(8,128)(2,1)}, bf16[2064,128]{1,0:T(8,128)(2,1)S(1)}, u32[]{:S(2)}, u32[]{:S(2)}) %collective-permute-start.3) | collective-permute-done | bytes 528416 | tf_op jit(solution)/shard_map/ppermute | solution.py:602
  43.6 3.0 %repack.1 = (bf16[4128,128]{1,0:T(8,128)(2,1)}, bf16[6192,128]{1,0:T(8,128)(2,1)}) custom-call(bf16[2064,128]{1,0:T(8,128)(2,1)} %get-tuple-element.31.kept_ref.refs_0_, bf16[3088,128]{1,0:T(8,128)(2,1)S(1)} %collective-permute-done.4.refs_0_.refs_1_, bf16[2064,128]{1,0:T(8,128)(2,1)S(1)} %collective-permute-done.refs_1_, ...), custom_call_target="tpu_custom_call" | custom-call | bytes 5242880 | tf_op jit(solution)/shard_map/repack/pallas_call | solution.py:485
  46.7 0.8 copy-done.3
  47.5 1.3 collective-permute-start.5
  48.8 3.3 %collective-permute-start.8 = (bf16[4128,128]{1,0:T(8,128)(2,1)}, bf16[4128,128]{1,0:T(8,128)(2,1)}, u32[]{:S(2)}, u32[]{:S(2)}) collective-permute-start(bf16[4128,128]{1,0:T(8,128)(2,1)} %get-tuple-element.36), channel_id=1, source_target_pairs={{0,32},{16,48},{32,0},{48,16},{64,96},{80,112},{96,64},{112,80},{1... | collective-permute-start | bytes 3170312 | tf_op jit(solution)/shard_map/ppermute | solution.py:591
  52.1 1.1 collective-permute-start.7
  53.1 1.0 collective-permute-start.6
  54.1 0.1 add.101
  54.2 0.1 reshape.54.sel
  54.3 0.1 add.98
  54.4 0.1 add.99
  54.5 0.1 pad_add_fusion.1.meta
  54.7 31.7 %collective-permute-done.5.refs_5_ = bf16[6192,128]{1,0:T(8,128)(2,1)} collective-permute-done((bf16[6192,128]{1,0:T(8,128)(2,1)}, bf16[6192,128]{1,0:T(8,128)(2,1)}, u32[]{:S(2)}, u32[]{:S(2)}) %collective-permute-start.5) | collective-permute-done | bytes 1585184 | tf_op jit(solution)/shard_map/ppermute | solution.py:605
  86.4 10.0 %student_forward.1 = (bf16[1024,128]{1,0:T(8,128)(2,1)}, f32[1024,1024]{1,0:T(8,128)}) custom-call(s32[2]{0:T(128)S(1)} %pad_add_fusion.1.meta, s32[256]{0:T(256)S(1)} %reshape.54.sel, bf16[1024,128]{1,0:T(8,128)(2,1)S(1)} %copy-done.7, s32[16,1,1024]{2,1,0:T(1,128)S(1)} %broadcast_add_fusion.kpos_ref, bf16[2064,128]{1,0:T(8,128)(2,1)} %get-tuple-element.30.refs_0_, ...), custom_call_target="tpu_custom_call" | custom-call | flops 536870912 | bytes 9437184 | tf_op jit(solution)/shard_map/student_forward/pallas_call | solution.py:208
  96.4 1.5 collective-permute-done.7.refs_3_
  97.9 0.7 fusion.7.refs_0_
  98.7 4.3 %compose.1 = bf16[256,384]{1,0:T(8,128)(2,1)} custom-call(bf16[256,4096]{1,0:T(8,128)(2,1)} %all-gather.3.cloned.1.call-done.rows_ref, bf16[128,4096]{1,0:T(8,128)(2,1)S(1)} %copy-done.1, bf16[256,4096]{1,0:T(8,128)(2,1)S(1)} %copy-done, bf16[16,128]{1,0:T(8,128)(2,1)S(1)} %fusion.7.refs_0_), custom_call_target="tpu_custom_call" | custom-call | flops 805306368 | bytes 5242880 | tf_op jit(solution)/shard_map/compose/pallas_call | solution.py:517
  103.0 0.1 concatenate.3.meta
  103.1 17.1 %teacher_attention.1 = (bf16[1024,128]{1,0:T(8,128)(2,1)}, bf16[1024,128]{1,0:T(8,128)(2,1)}) custom-call(s32[16]{0:T(128)S(1)} %concatenate.3.meta, bf16[1024,128]{1,0:T(8,128)(2,1)} %get-tuple-element.35.here_ref, bf16[2064,128]{1,0:T(8,128)(2,1)} %get-tuple-element.31.kept_ref.refs_0_, bf16[3088,128]{1,0:T(8,128)(2,1)} %copy-done.8, ...), custom_call_target="tpu_custom_call" | custom-call | flops 4294967296 | bytes 5242880 | tf_op jit(solution)/shard_map/teacher_attention/pallas_call | solution.py:154
  120.2 3.5 %collective-permute-start.9 = (bf16[1024,128]{1,0:T(8,128)(2,1)}, bf16[1024,128]{1,0:T(8,128)(2,1)}, u32[]{:S(2)}, u32[]{:S(2)}) collective-permute-start(bf16[1024,128]{1,0:T(8,128)(2,1)} %get-tuple-element.38), channel_id=1, source_target_pairs={{0,64},{16,80},{32,96},{48,112},{64,0},{80,16},{96,32},{112,48},{1... | collective-permute-start | bytes 786440 | tf_op jit(solution)/shard_map/ppermute | solution.py:627
  123.7 0.1 pad_add_fusion.3.at
  123.8 12.3 %collective-permute-done.9.b_ref = bf16[1024,128]{1,0:T(8,128)(2,1)} collective-permute-done((bf16[1024,128]{1,0:T(8,128)(2,1)}, bf16[1024,128]{1,0:T(8,128)(2,1)}, u32[]{:S(2)}, u32[]{:S(2)}) %collective-permute-start.9) | collective-permute-done | bytes 262176 | tf_op jit(solution)/shard_map/ppermute | solution.py:627
  136.0 6.8 %project_mismatch.2 = bf16[8,1024,256]{2,1,0:T(8,128)(2,1)} custom-call(s32[2]{0:T(128)S(1)} %pad_add_fusion.3.at, bf16[1024,128]{1,0:T(8,128)(2,1)} %get-tuple-element.34.s_ref, bf16[1024,128]{1,0:T(8,128)(2,1)} %get-tuple-element.37.a_ref, bf16[1024,128]{1,0:T(8,128)(2,1)} %collective-permute-done.9.b_ref, bf16[128,4096]{1,0:T(8,128)(2,1)S(1)} %copy-done.1, ...), custom_call_target="tpu_custom_call" | custom-call | flops 1610612736 | bytes 6291456 | tf_op jit(solution)/shard_map/project_mismatch/pallas_call | solution.py:366
  142.9 0.7 slice_bitcast_fusion.refs_1_
  143.6 5.1 %all-gather.5.cloned.1.call-done = bf16[2048,384]{1,0:T(8,128)(2,1)} async-done(((bf16[256,384]{1,0:T(8,128)(2,1)}), bf16[2048,384]{1,0:T(8,128)(2,1)}) %all-gather.5.cloned.1.call-update) | async-done | bytes 1572880 | tf_op jit(solution)/shard_map/all_gather | solution.py:623
  148.7 1.4 copy-done.2
  150.1 4.1 %project_grad.2 = bf16[8,1024,128]{2,1,0:T(8,128)(2,1)S(1)} custom-call(s32[2]{0:T(128)S(1)} %pad_add_fusion.3.at, bf16[1024,128]{1,0:T(8,128)(2,1)} %get-tuple-element.34.s_ref, bf16[1024,128]{1,0:T(8,128)(2,1)} %get-tuple-element.37.a_ref, bf16[1024,128]{1,0:T(8,128)(2,1)} %collective-permute-done.9.b_ref, bf16[8,16,16,384]{3,2,1,0:T(8,128)(2,1)S(1)} %bitcast.9, ...), custom_call_target="tpu_custom_call" | custom-call | flops 805306368 | bytes 4194304 | tf_op jit(solution)/shard_map/project_grad/pallas_call | solution.py:366
  154.2 0.1 collective-permute-start.11
  154.3 0.1 pad_add_fusion.at
  154.4 4.1 %collective-permute-done.11.refs_1_ = bf16[8,1024,128]{2,1,0:T(8,128)(2,1)S(1)} collective-permute-done((bf16[8,1024,128]{2,1,0:T(8,128)(2,1)S(1)}, bf16[8,1024,128]{2,1,0:T(8,128)(2,1)S(1)}, u32[]{:S(2)}, u32[]{:S(2)}) %collective-permute-start.11) | collective-permute-done | bytes 2097184 | tf_op jit(solution)/shard_map/ppermute | solution.py:635
  158.5 5.2 %project_grad.3 = bf16[8,1024,128]{2,1,0:T(8,128)(2,1)} custom-call(s32[2]{0:T(128)S(1)} %pad_add_fusion.at, bf16[1024,128]{1,0:T(8,128)(2,1)} %get-tuple-element.34.s_ref, bf16[1024,128]{1,0:T(8,128)(2,1)} %get-tuple-element.37.a_ref, bf16[1024,128]{1,0:T(8,128)(2,1)} %collective-permute-done.9.b_ref, bf16[8,16,16,384]{3,2,1,0:T(8,128)(2,1)S(1)} %bitcast.10, ...), custom_call_target="tpu_custom_call" | custom-call | flops 805306368 | bytes 6291456 | tf_op jit(solution)/shard_map/project_grad/pallas_call | solution.py:366
  163.7 6.8 %all-to-all-start.1 = ((bf16[8,1024,128]{2,1,0:T(8,128)(2,1)}), bf16[8,1024,128]{2,1,0:T(8,128)(2,1)}, u32[]{:S(2)}, u32[]{:S(2)}) async-start(bf16[8,1024,128]{2,1,0:T(8,128)(2,1)} %project_grad.3), calls=%async_computation.1 | async-start | bytes 4194304 | tf_op jit(solution)/shard_map/all_to_all | solution.py:637
  170.4 7.8 %project_mismatch.3 = bf16[8,1024,256]{2,1,0:T(8,128)(2,1)} custom-call(s32[2]{0:T(128)S(1)} %pad_add_fusion.at, bf16[1024,128]{1,0:T(8,128)(2,1)} %get-tuple-element.34.s_ref, bf16[1024,128]{1,0:T(8,128)(2,1)} %get-tuple-element.37.a_ref, bf16[1024,128]{1,0:T(8,128)(2,1)} %collective-permute-done.9.b_ref, bf16[128,4096]{1,0:T(8,128)(2,1)S(1)} %copy-done.1, ...), custom_call_target="tpu_custom_call" | custom-call | flops 1610612736 | bytes 10485760 | tf_op jit(solution)/shard_map/project_mismatch/pallas_call | solution.py:366
  178.3 18.3 %all-to-all-done.1.g_ref = bf16[8,1024,128]{2,1,0:T(8,128)(2,1)} async-done(((bf16[8,1024,128]{2,1,0:T(8,128)(2,1)}), bf16[8,1024,128]{2,1,0:T(8,128)(2,1)}, u32[]{:S(2)}, u32[]{:S(2)}) %all-to-all-start.1) | async-done | bytes 2097184 | tf_op jit(solution)/shard_map/all_to_all | solution.py:637
  196.6 7.2 %all-to-all-start = ((bf16[8,1024,256]{2,1,0:T(8,128)(2,1)}), bf16[8,1024,256]{2,1,0:T(8,128)(2,1)}, u32[]{:S(2)}, u32[]{:S(2)}) async-start(bf16[8,1024,256]{2,1,0:T(8,128)(2,1)} %project_mismatch.3), calls=%async_computation | async-start | bytes 8388608 | tf_op jit(solution)/shard_map/all_to_all | solution.py:640
  203.8 14.1 %student_backward.1 = (f32[1024,128]{1,0:T(8,128)}, bf16[2048,128]{1,0:T(8,128)(2,1)S(1)}, bf16[2048,128]{1,0:T(8,128)(2,1)S(1)}, bf16[2048,128]{1,0:T(8,128)(2,...) custom-call(s32[2]{0:T(128)S(1)} %pad_add_fusion.1.meta, ...), custom_call_target="tpu_custom_call" | custom-call | flops 1073741824 | bytes 15728640 | tf_op jit(solution)/shard_map/student_backward/pallas_call | solution.py:293
  217.9 11.7 %collective-permute-start.12 = (bf16[2048,128]{1,0:T(8,128)(2,1)S(1)}, bf16[2048,128]{1,0:T(8,128)(2,1)S(1)}, u32[]{:S(2)}, u32[]{:S(2)}) collective-permute-start(bf16[2048,128]{1,0:T(8,128)(2,1)S(1)} %get-tuple-element.43), channel_id=1, source_target_pairs={{16,0},{32,16},{48,32},{64,112},{80,64},{96,80},{112,96},{17,1},{3... | collective-permute-start | bytes 1572872 | tf_op jit(solution)/shard_map/ppermute | solution.py:656
  229.7 1.9 collective-permute-start.13
  231.6 3.4 %collective-permute-start.14 = (bf16[2048,128]{1,0:T(8,128)(2,1)S(1)}, bf16[2048,128]{1,0:T(8,128)(2,1)S(1)}, u32[]{:S(2)}, u32[]{:S(2)}) collective-permute-start(bf16[2048,128]{1,0:T(8,128)(2,1)S(1)} %get-tuple-element.45), channel_id=1, source_target_pairs={{32,0},{48,16},{64,96},{80,112},{96,64},{112,80},{33,1},{49,17},{6... | collective-permute-start | bytes 1572872 | tf_op jit(solution)/shard_map/ppermute | solution.py:656
  235.0 16.2 %collective-permute-done.12.refs_1_ = bf16[2048,128]{1,0:T(8,128)(2,1)S(1)} collective-permute-done((bf16[2048,128]{1,0:T(8,128)(2,1)S(1)}, bf16[2048,128]{1,0:T(8,128)(2,1)S(1)}, u32[]{:S(2)}, u32[]{:S(2)}) %collective-permute-start.12) | collective-permute-done | bytes 524320 | tf_op jit(solution)/shard_map/ppermute | solution.py:656
  251.2 5.3 %collective-permute-done.13.refs_2_ = bf16[2048,128]{1,0:T(8,128)(2,1)S(1)} collective-permute-done((bf16[2048,128]{1,0:T(8,128)(2,1)S(1)}, bf16[2048,128]{1,0:T(8,128)(2,1)S(1)}, u32[]{:S(2)}, u32[]{:S(2)}) %collective-permute-start.13) | collective-permute-done | bytes 524320 | tf_op jit(solution)/shard_map/ppermute | solution.py:656
  256.5 0.3 add_convert_fusion
  256.8 0.8 copy-done.11
  257.6 0.6 slice.39.refs_4_
  258.2 1.3 collective-permute-start.16
  259.5 1.3 collective-permute-start.17
  260.8 1.4 collective-permute-start.18
  262.2 2.1 collective-permute-start.15
  264.3 4.2 %add_pieces.1 = f32[1024,256]{1,0:T(8,128)} custom-call(bf16[8,1024,256]{2,1,0:T(8,128)(2,1)} %all-to-all-done.in_ref), custom_call_target="tpu_custom_call" | custom-call | flops 8388608 | bytes 5242880 | tf_op jit(solution)/shard_map/add_pieces/pallas_call | solution.py:540
  268.5 0.7 slice.40.refs_9_
  269.2 1.4 collective-permute-done.16.refs_6_
  270.7 13.9 %collective-permute-done.17.refs_7_ = bf16[2048,128]{1,0:T(8,128)(2,1)} collective-permute-done((bf16[2048,128]{1,0:T(8,128)(2,1)}, bf16[2048,128]{1,0:T(8,128)(2,1)}, u32[]{:S(2)}, u32[]{:S(2)}) %collective-permute-start.17) | collective-permute-done | bytes 524320 | tf_op jit(solution)/shard_map/ppermute | solution.py:662
  284.5 2.6 finish.1
  (44 shorter events, 0.2 us)
Async XLA Ops:
  7.2 91.5 %all-gather.3.cloned.1.call-start = ((), (), s32[]{:S(2)}) async-start(), calls=%async_computation.2 | async-start | bytes 2228224 | tf_op jit(solution)/shard_map/all_gather | solution.py:621
  7.3 0.7 copy-start.9
  11.1 43.1 %copy-start.12 = (s32[16,16]{1,0:T(8,128)S(1)}, s32[16,16]{1,0:T(8,128)}, u32[]{:S(2)}) copy-start(s32[16,16]{1,0:T(8,128)} %param.19) | copy-start | bytes 3076
  11.1 75.3 %copy-start.7 = (bf16[1024,128]{1,0:T(8,128)(2,1)S(1)}, bf16[1024,128]{1,0:T(8,128)(2,1)}, u32[]{:S(2)}) copy-start(bf16[1024,128]{1,0:T(8,128)(2,1)} %q_ref.3) | copy-start | bytes 786436
  11.1 137.5 %all-gather.5.cloned.1.call-start = ((), (), s32[]{:S(2)}) async-start(), calls=%async_computation.3 | async-start | bytes 1769472 | tf_op jit(solution)/shard_map/all_gather | solution.py:623
  11.2 32.4 %collective-permute-start.4 = (bf16[3088,128]{1,0:T(8,128)(2,1)}, bf16[3088,128]{1,0:T(8,128)(2,1)S(1)}, u32[]{:S(2)}, u32[]{:S(2)}) collective-permute-start(bf16[3088,128]{1,0:T(8,128)(2,1)} %get-tuple-element.32), channel_id=1, source_target_pairs={{0,64},{16,80},{32,96},{48,112},{64,0},{80,16},{96,32},{112,48},{1... | collective-permute-start | bytes 2371592 | tf_op jit(solution)/shard_map/ppermute | solution.py:601
  12.1 31.5 %collective-permute-start.3 = (bf16[2064,128]{1,0:T(8,128)(2,1)}, bf16[2064,128]{1,0:T(8,128)(2,1)S(1)}, u32[]{:S(2)}, u32[]{:S(2)}) collective-permute-start(bf16[2064,128]{1,0:T(8,128)(2,1)} %get-tuple-element.30.refs_0_), channel_id=1, source_target_pairs={{0,64},{16,80},{32,96},{48,112},{1,65},{17,81},{33,97},{49,113},{2... | collective-permute-start | bytes 1585160 | tf_op jit(solution)/shard_map/ppermute | solution.py:602
  13.4 30.2 %collective-permute-start.2 = (bf16[2064,128]{1,0:T(8,128)(2,1)}, bf16[2064,128]{1,0:T(8,128)(2,1)S(1)}, u32[]{:S(2)}, u32[]{:S(2)}) collective-permute-start(bf16[2064,128]{1,0:T(8,128)(2,1)} %get-tuple-element.30.refs_0_), channel_id=1, source_target_pairs={{0,32},{16,48},{32,0},{48,16},{64,96},{80,112},{1,33},{17,49},{33,... | collective-permute-start | bytes 1585160 | tf_op jit(solution)/shard_map/ppermute | solution.py:591
  18.5 25.1 %collective-permute-start.1 = (bf16[2064,128]{1,0:T(8,128)(2,1)}, bf16[2064,128]{1,0:T(8,128)(2,1)S(1)}, u32[]{:S(2)}, u32[]{:S(2)}) collective-permute-start(bf16[2064,128]{1,0:T(8,128)(2,1)} %get-tuple-element.30.refs_0_), channel_id=1, source_target_pairs={{0,48},{16,0},{32,16},{48,32},{64,112},{1,49},{17,1},{33,17},{49,3... | collective-permute-start | bytes 1585160 | tf_op jit(solution)/shard_map/ppermute | solution.py:591
  19.9 23.7 %collective-permute-start = (bf16[2064,128]{1,0:T(8,128)(2,1)}, bf16[2064,128]{1,0:T(8,128)(2,1)S(1)}, u32[]{:S(2)}, u32[]{:S(2)}) collective-permute-start(bf16[2064,128]{1,0:T(8,128)(2,1)} %get-tuple-element.30.refs_0_), channel_id=1, source_target_pairs={{0,16},{16,32},{32,48},{48,0},{64,80},{80,96},{96,112},{1,17},{17,... | collective-permute-start | bytes 1585160 | tf_op jit(solution)/shard_map/ppermute | solution.py:591
  43.6 5.2 %copy-start.10 = (bf16[2064,128]{1,0:T(8,128)(2,1)}, bf16[2064,128]{1,0:T(8,128)(2,1)S(1)}, u32[]{:S(2)}) copy-start(bf16[2064,128]{1,0:T(8,128)(2,1)S(1)} %collective-permute-done.3.refs_4_) | copy-start | bytes 1585156
  43.6 3.1 %copy-start.4 = (bf16[2064,128]{1,0:T(8,128)(2,1)}, bf16[2064,128]{1,0:T(8,128)(2,1)S(1)}, u32[]{:S(2)}) copy-start(bf16[2064,128]{1,0:T(8,128)(2,1)S(1)} %collective-permute-done.1.refs_2_) | copy-start | bytes 1585156
  43.6 3.9 %copy-start.5 = (bf16[2064,128]{1,0:T(8,128)(2,1)}, bf16[2064,128]{1,0:T(8,128)(2,1)S(1)}, u32[]{:S(2)}) copy-start(bf16[2064,128]{1,0:T(8,128)(2,1)S(1)} %collective-permute-done.refs_1_) | copy-start | bytes 1585156
  43.6 5.2 %copy-start.8 = (bf16[3088,128]{1,0:T(8,128)(2,1)}, bf16[3088,128]{1,0:T(8,128)(2,1)S(1)}, u32[]{:S(2)}) copy-start(bf16[3088,128]{1,0:T(8,128)(2,1)S(1)} %collective-permute-done.4.refs_0_.refs_1_) | copy-start | bytes 2371588
  46.7 0.8 copy-start.3
  47.5 38.9 %collective-permute-start.5 = (bf16[6192,128]{1,0:T(8,128)(2,1)}, bf16[6192,128]{1,0:T(8,128)(2,1)}, u32[]{:S(2)}, u32[]{:S(2)}) collective-permute-start(bf16[6192,128]{1,0:T(8,128)(2,1)} %get-tuple-element.33), channel_id=1, source_target_pairs={{0,64},{16,80},{32,96},{48,112},{1,65},{17,81},{33,97},{49,113},{2... | collective-permute-start | bytes 4755464 | tf_op jit(solution)/shard_map/ppermute | solution.py:605
  48.8 47.6 %collective-permute-start.8 = (bf16[4128,128]{1,0:T(8,128)(2,1)}, bf16[4128,128]{1,0:T(8,128)(2,1)}, u32[]{:S(2)}, u32[]{:S(2)}) collective-permute-start(bf16[4128,128]{1,0:T(8,128)(2,1)} %get-tuple-element.36), channel_id=1, source_target_pairs={{0,32},{16,48},{32,0},{48,16},{64,96},{80,112},{96,64},{112,80},{1... | collective-permute-start | bytes 3170312 | tf_op jit(solution)/shard_map/ppermute | solution.py:591
  52.1 45.9 %collective-permute-start.7 = (bf16[4128,128]{1,0:T(8,128)(2,1)}, bf16[4128,128]{1,0:T(8,128)(2,1)}, u32[]{:S(2)}, u32[]{:S(2)}) collective-permute-start(bf16[4128,128]{1,0:T(8,128)(2,1)} %get-tuple-element.36), channel_id=1, source_target_pairs={{0,48},{16,0},{32,16},{48,32},{64,112},{80,64},{96,80},{112,96},{1... | collective-permute-start | bytes 3170312 | tf_op jit(solution)/shard_map/ppermute | solution.py:591
  53.1 44.8 %collective-permute-start.6 = (bf16[4128,128]{1,0:T(8,128)(2,1)}, bf16[4128,128]{1,0:T(8,128)(2,1)}, u32[]{:S(2)}, u32[]{:S(2)}) collective-permute-start(bf16[4128,128]{1,0:T(8,128)(2,1)} %get-tuple-element.36), channel_id=1, source_target_pairs={{0,16},{16,32},{32,48},{48,0},{64,80},{80,96},{96,112},{112,64},{1... | collective-permute-start | bytes 3170312 | tf_op jit(solution)/shard_map/ppermute | solution.py:591
  54.7 44.0 %copy-start = (bf16[256,4096]{1,0:T(8,128)(2,1)S(1)}, bf16[256,4096]{1,0:T(8,128)(2,1)}, u32[]{:S(2)}) copy-start(bf16[256,4096]{1,0:T(8,128)(2,1)} %t_ref.1) | copy-start | bytes 6291460
  54.7 44.0 %copy-start.1 = (bf16[128,4096]{1,0:T(8,128)(2,1)S(1)}, bf16[128,4096]{1,0:T(8,128)(2,1)}, u32[]{:S(2)}) copy-start(bf16[128,4096]{1,0:T(8,128)(2,1)} %s_ref.1) | copy-start | bytes 3145732
  120.2 15.8 %collective-permute-start.9 = (bf16[1024,128]{1,0:T(8,128)(2,1)}, bf16[1024,128]{1,0:T(8,128)(2,1)}, u32[]{:S(2)}, u32[]{:S(2)}) collective-permute-start(bf16[1024,128]{1,0:T(8,128)(2,1)} %get-tuple-element.38), channel_id=1, source_target_pairs={{0,64},{16,80},{32,96},{48,112},{64,0},{80,16},{96,32},{112,48},{1... | collective-permute-start | bytes 786440 | tf_op jit(solution)/shard_map/ppermute | solution.py:627
  142.9 27.6 %collective-permute-start.10 = (bf16[8,1024,256]{2,1,0:T(8,128)(2,1)}, bf16[8,1024,256]{2,1,0:T(8,128)(2,1)}, u32[]{:S(2)}, u32[]{:S(2)}) collective-permute-start(bf16[8,1024,256]{2,1,0:T(8,128)(2,1)} %project_mismatch.2), channel_id=1, source_target_pairs={{0,2},{2,0},{1,3},{3,1},{4,6},{6,4},{5,7},{7,5},{8,10},{10,8},{9,1... | collective-permute-start | bytes 12582920 | tf_op jit(solution)/shard_map/ppermute | solution.py:638
  148.7 1.4 copy-start.2
  154.2 4.2 %collective-permute-start.11 = (bf16[8,1024,128]{2,1,0:T(8,128)(2,1)S(1)}, bf16[8,1024,128]{2,1,0:T(8,128)(2,1)S(1)}, u32[]{:S(2)}, u32[]{:S(2)}) collective-permute-start(bf16[8,1024,128]{2,1,0:T(8,128)(2,1)S(1)} %project_grad.2), channel_id=1, source_target_pairs={{0,2},{2,0},{1,3},{3,1},{4,6},{6,4},{5,7},{7,5},{8,10},{10,8},{9,1... | collective-permute-start | bytes 6291464 | tf_op jit(solution)/shard_map/ppermute | solution.py:635
  163.7 32.9 %all-to-all-start.1 = ((bf16[8,1024,128]{2,1,0:T(8,128)(2,1)}), bf16[8,1024,128]{2,1,0:T(8,128)(2,1)}, u32[]{:S(2)}, u32[]{:S(2)}) async-start(bf16[8,1024,128]{2,1,0:T(8,128)(2,1)} %project_grad.3), calls=%async_computation.1 | async-start | bytes 4194304 | tf_op jit(solution)/shard_map/all_to_all | solution.py:637
  196.6 67.7 %all-to-all-start = ((bf16[8,1024,256]{2,1,0:T(8,128)(2,1)}), bf16[8,1024,256]{2,1,0:T(8,128)(2,1)}, u32[]{:S(2)}, u32[]{:S(2)}) async-start(bf16[8,1024,256]{2,1,0:T(8,128)(2,1)} %project_mismatch.3), calls=%async_computation | async-start | bytes 8388608 | tf_op jit(solution)/shard_map/all_to_all | solution.py:640
  217.9 33.2 %collective-permute-start.12 = (bf16[2048,128]{1,0:T(8,128)(2,1)S(1)}, bf16[2048,128]{1,0:T(8,128)(2,1)S(1)}, u32[]{:S(2)}, u32[]{:S(2)}) collective-permute-start(bf16[2048,128]{1,0:T(8,128)(2,1)S(1)} %get-tuple-element.43), channel_id=1, source_target_pairs={{16,0},{32,16},{48,32},{64,112},{80,64},{96,80},{112,96},{17,1},{3... | collective-permute-start | bytes 1572872 | tf_op jit(solution)/shard_map/ppermute | solution.py:656
  229.7 26.8 %collective-permute-start.13 = (bf16[2048,128]{1,0:T(8,128)(2,1)S(1)}, bf16[2048,128]{1,0:T(8,128)(2,1)S(1)}, u32[]{:S(2)}, u32[]{:S(2)}) collective-permute-start(bf16[2048,128]{1,0:T(8,128)(2,1)S(1)} %get-tuple-element.44), channel_id=1, source_target_pairs={{48,0},{64,80},{80,96},{96,112},{112,64},{49,1},{65,81},{81,97},{9... | collective-permute-start | bytes 1572872 | tf_op jit(solution)/shard_map/ppermute | solution.py:656
  231.6 24.9 %collective-permute-start.14 = (bf16[2048,128]{1,0:T(8,128)(2,1)S(1)}, bf16[2048,128]{1,0:T(8,128)(2,1)S(1)}, u32[]{:S(2)}, u32[]{:S(2)}) collective-permute-start(bf16[2048,128]{1,0:T(8,128)(2,1)S(1)} %get-tuple-element.45), channel_id=1, source_target_pairs={{32,0},{48,16},{64,96},{80,112},{96,64},{112,80},{33,1},{49,17},{6... | collective-permute-start | bytes 1572872 | tf_op jit(solution)/shard_map/ppermute | solution.py:656
  256.8 0.8 copy-start.11
  258.2 12.5 %collective-permute-start.16 = (bf16[2048,128]{1,0:T(8,128)(2,1)}, bf16[2048,128]{1,0:T(8,128)(2,1)S(1)}, u32[]{:S(2)}, u32[]{:S(2)}) collective-permute-start(bf16[2048,128]{1,0:T(8,128)(2,1)} %get-tuple-element.51), channel_id=1, source_target_pairs={{80,64},{96,80},{112,96},{81,65},{97,81},{113,97},{82,66},{98,82},... | collective-permute-start | bytes 1572872 | tf_op jit(solution)/shard_map/ppermute | solution.py:662
  259.5 25.1 %collective-permute-start.17 = (bf16[2048,128]{1,0:T(8,128)(2,1)}, bf16[2048,128]{1,0:T(8,128)(2,1)}, u32[]{:S(2)}, u32[]{:S(2)}) collective-permute-start(bf16[2048,128]{1,0:T(8,128)(2,1)} %get-tuple-element.52), channel_id=1, source_target_pairs={{112,64},{113,65},{114,66},{115,67},{116,68},{117,69},{118,70},{11... | collective-permute-start | bytes 1572872 | tf_op jit(solution)/shard_map/ppermute | solution.py:662
  260.8 23.8 %copy-start.6 = (bf16[2048,128]{1,0:T(8,128)(2,1)S(1)}, bf16[2048,128]{1,0:T(8,128)(2,1)}, u32[]{:S(2)}) copy-start(bf16[2048,128]{1,0:T(8,128)(2,1)} %get-tuple-element.50.refs_5_) | copy-start | bytes 1572868
  260.8 23.7 %collective-permute-start.18 = (bf16[2048,128]{1,0:T(8,128)(2,1)}, bf16[2048,128]{1,0:T(8,128)(2,1)}, u32[]{:S(2)}, u32[]{:S(2)}) collective-permute-start(bf16[2048,128]{1,0:T(8,128)(2,1)} %get-tuple-element.53), channel_id=1, source_target_pairs={{96,64},{112,80},{97,65},{113,81},{98,66},{114,82},{99,67},{115,83... | collective-permute-start | bytes 1572872 | tf_op jit(solution)/shard_map/ppermute | solution.py:662
  262.2 22.3 %collective-permute-start.15 = (bf16[2048,128]{1,0:T(8,128)(2,1)}, bf16[2048,128]{1,0:T(8,128)(2,1)}, u32[]{:S(2)}, u32[]{:S(2)}) collective-permute-start(bf16[2048,128]{1,0:T(8,128)(2,1)} %copy-done.11), channel_id=1, source_target_pairs={{64,0},{80,16},{96,32},{112,48},{65,1},{81,17},{97,33},{113,49},{6... | collective-permute-start | bytes 1572872 | tf_op jit(solution)/shard_map/ppermute | solution.py:660
Sparse Core Ops, SparseCore 0:
  11.3 49.9 all-gather.2
  103.1 45.5 all-gather.4
